TPU v7x, 256 devices: a whole 4x4x8 slice. The times are simulated.
256 devices in a mesh: step: 16 (over y, x), frame: 16 (over z, core).
Axes of the slice: x: 4, y: 4, z: 8, core: 2. Of those that a mesh axis runs over, the one named last changes fastest.
Arguments:
- start_state: bfloat16 [16, 32, 32, 320], P('frame'), may hold values from -6 to 6
- step_noise: bfloat16 [16, 16, 32, 32, 320], P('step', 'frame'), may hold values from -6 to 6
- timesteps: int32 [16], P('step'), may hold values from 0 to 999
- gn_gain: float32 [320], replicated, may hold values from 0.1 to 1.9
- gn_bias: float32 [320], replicated, may hold values from -3 to 3
- spatial_weight: bfloat16 [3, 3, 320, 320], replicated, may hold values from -0.109375 to 0.109375
- temporal_weight: bfloat16 [3, 320, 320], replicated, may hold values from -0.1875 to 0.1875
- temb_weight: bfloat16 [320, 320], replicated, may hold values from -0.3125 to 0.3125
Outputs:
- next_states: bfloat16 [16, 16, 32, 32, 320], P('step', 'frame')
All inputs are finite; a program needn't handle non-finite values.
Results may differ from a plain program's by a relative error of at most 0.005.
Values may be sent and summed in bfloat16 or wider, within the bound.
No kernel may reach another device: no remote copies, remote signals or barrier semaphores. Data moves between devices by JAX's collectives and lax.ppermute only.
A program may use at most 128 MiB of HBM per device.

v0:
```python
import math

import jax
import jax.numpy as jnp
from jax import lax
from jax.experimental import pallas as pl
from jax.experimental.pallas import tpu as pltpu
from jax.sharding import Mesh, PartitionSpec as P


F32, BF16 = jnp.float32, jnp.bfloat16
AXES = ("y", "x", "z", "core")
HIGHEST = lax.Precision.HIGHEST

POS, ROWS, LANES = 256, 640, 128


def silu(a):
    half = 0.5 * a
    return half + half * jnp.tanh(half)


def low_lanes(rows):
    return lax.broadcasted_iota(jnp.int32, (rows, LANES), 1) < 64


def swapped(tile):
    return pltpu.roll(tile, 64, 1)


def pack_tail(tail):
    return jnp.concatenate([tail[:128], tail[128:]], axis=1)


def twice(tail):
    return jnp.concatenate([tail, tail], axis=1)


def spread_tail(tile):
    low, other = low_lanes(128), swapped(tile)
    return jnp.concatenate([jnp.where(low, tile, other), jnp.where(low, other, tile)], axis=0)


def same_group(size):
    rows = lax.broadcasted_iota(jnp.int32, (size, size), 0)
    columns = lax.broadcasted_iota(jnp.int32, (size, size), 1)
    return (((rows * 6554) >> 16) == ((columns * 6554) >> 16)).astype(F32)


def group_sum(sums, members):
    return jnp.dot(sums, members, precision=HIGHEST, preferred_element_type=F32)


def store_taps(taps, tiles):
    column = lax.broadcasted_iota(jnp.int32, (320, LANES), 0) & 31
    low = low_lanes(320)
    shifted = []
    for place, step in enumerate((-1, 0, 1)):
        moved = []
        for tile in tiles:
            if step:
                tile = pltpu.roll(tile, -step % 320, 0)
                tile = jnp.where(column == (0 if step < 0 else 31), 0.0, tile)
            moved.append(tile)
        taps[:, place * 256 : place * 256 + 128] = moved[0].astype(BF16)
        taps[:, place * 256 + 128 : place * 256 + 256] = moved[1].astype(BF16)
        shifted.append(moved[2])
    taps[:, 768:896] = jnp.where(low, shifted[0], shifted[1]).astype(BF16)
    taps[:, 896:1024] = jnp.where(low, shifted[2], 0.0).astype(BF16)


def conv_rows(taps, wp):
    total = None
    for row in range(3):
        term = jnp.dot(taps[row * 32 : row * 32 + POS, :], wp[row], preferred_element_type=F32)
        total = term if total is None else total + term
    return total


def hop_of(slot):
    return jnp.where(lax.axis_index("core") == 0, slot, (4 - slot) % 4)


def prologue_kernel(
    noise_hbm, start_hbm, sw, tw, tew_hbm, gain_hbm, bias_hbm, emb,
    o0, o1, o2, o3, start, wp, tp, tew, gain, bias, noise, sems,
):
    x = lax.axis_index("x")
    frame = lax.axis_index("z") * 2 + lax.axis_index("core")
    moves = [(noise_hbm, noise), (start_hbm, start), (gain_hbm, gain), (bias_hbm, bias)]
    for row in range(4):
        out = tp if row == 3 else wp.at[row]
        for place in range(3):
            one = tw.at[place] if row == 3 else sw.at[row, place]
            moves.append((one.at[0:256], out.at[place * 256 : place * 256 + 256]))
            moves.append((one.at[256:320], out.at[768 + 64 * place : 832 + 64 * place]))
    moves.append((tew_hbm, tew))
    copies = [pltpu.make_async_copy(source, target, sems.at[i]) for i, (source, target) in enumerate(moves)]
    for copy in copies:
        copy.start()
    for row in range(3):
        wp[row, 960:1024] = jnp.zeros((64, 320), BF16)
    tp[960:1024] = jnp.zeros((64, 320), BF16)
    copies[0].wait()
    for slot, out in enumerate((o0, o1, o2, o3)):
        at = pl.multiple_of(lax.rem(x + hop_of(slot), 4) * POS, POS)
        out[0:256] = noise[pl.ds(at, POS), 0:128]
        out[256:512] = noise[pl.ds(at, POS), 128:256]
        out[512:640] = pack_tail(noise[pl.ds(at, POS), 256:320].astype(F32)).astype(BF16)
        for tile in range(3):
            out[640 + 16 * tile : 656 + 16 * tile] = emb[:, tile * 128 : tile * 128 + 128]
    for copy in copies[1:]:
        copy.wait()
    for place, missing in ((0, frame == 0), (2, frame == 15)):

        @pl.when(missing)
        def _():
            tp[place * 256 : place * 256 + 256] = jnp.zeros((256, 320), BF16)
            tp[768 + 64 * place : 832 + 64 * place] = jnp.zeros((64, 320), BF16)


def norm_start_kernel(start, gain_ref, bias_ref, nq, sp):
    x = lax.axis_index("x")
    members = same_group(320)
    values = start[...].astype(F32)
    mean = group_sum(jnp.broadcast_to(jnp.sum(values, axis=0, keepdims=True), (8, 320)), members)[0:1] * (1.0 / 10240)
    centered = start[...].astype(F32) - mean
    spread = jnp.sum(centered * centered, axis=0, keepdims=True)
    var = group_sum(jnp.broadcast_to(spread, (8, 320)), members)[0:1] * (1.0 / 10240)
    scale = lax.rsqrt(var + 1e-05)
    gain, bias = gain_ref[...].reshape(1, 320), bias_ref[...].reshape(1, 320)
    first = pl.multiple_of(x * POS, POS)
    above = pl.multiple_of(jnp.maximum(x * POS - 32, 0), 32)
    below = pl.multiple_of(jnp.minimum(x * POS + POS, 992), 32)
    for at, size, rows, kept in (
        (above, 32, 0, x > 0),
        (first, POS, 32, None),
        (below, 32, 288, x < 3),
    ):
        block = start[pl.ds(at, size), :].astype(F32)
        normed = silu((block - mean) * scale * gain + bias)
        if kept is not None:
            normed = jnp.where(kept, normed, 0.0)
        nq[0, rows : rows + size] = normed[:, 0:128].astype(BF16)
        nq[1, rows : rows + size] = normed[:, 128:256].astype(BF16)
        nq[2, rows : rows + size] = twice(normed[:, 256:320]).astype(BF16)
    sp[0:256] = start[pl.ds(first, POS), 0:128]
    sp[256:512] = start[pl.ds(first, POS), 128:256]
    sp[512:640] = pack_tail(start[pl.ds(first, POS), 256:320].astype(F32)).astype(BF16)


def drift_of(a3, tp, noise, step):
    update = jnp.dot(a3[...], tp[...], preferred_element_type=F32)
    packed = (update[:, 0:128], update[:, 128:256], pack_tail(update[:, 256:320]))
    spans = ((0, 256), (256, 512), (512, 640))
    return [(a, b, 0.25 * (u + noise[step, a:b].astype(F32))) for u, (a, b) in zip(packed, spans)]


def first_sweep_kernel(own, before, after, wp, tp, tew, n0, n1, n2, n3, rt, prefix, noise, tb, taps, pre, a3, run):
    x = lax.axis_index("x")
    for slot, one in enumerate((n0, n1, n2, n3)):
        step = lax.rem(x + 4 - hop_of(slot), 4)
        noise[step] = one[0:640]
        bias = (
            jnp.dot(one[640:656], tew[0:128], preferred_element_type=F32)
            + jnp.dot(one[656:672], tew[128:256], preferred_element_type=F32)
            + jnp.dot(one[672:688, 0:64], tew[256:320], preferred_element_type=F32)
        )
        tb[step] = bias / (1.0 + jnp.exp(-bias))
    for place, normed in enumerate((before, own, after)):
        store_taps(taps, [normed[i].astype(F32) for i in range(3)])
        pre[place] = conv_rows(taps, wp)
    run[...] = jnp.zeros_like(run)

    def one_step(step, carry):
        bias = tb[step][0:1]
        tails = []
        for place in range(3):
            activated = silu(pre[place] + bias)
            a3[:, place * 256 : place * 256 + 256] = activated[:, 0:256].astype(BF16)
            tails.append(activated[:, 256:320])
        a3[:, 768:896] = jnp.concatenate(tails[:2], axis=1).astype(BF16)
        a3[:, 896:1024] = jnp.concatenate([tails[2], jnp.zeros_like(tails[2])], axis=1).astype(BF16)
        for a, b, drift in drift_of(a3, tp, noise, step):
            earlier = run[a:b]
            prefix[step, a:b] = earlier
            run[a:b] = earlier + drift
        return carry

    lax.fori_loop(0, 4, one_step, 0)
    rt[...] = run[...].astype(BF16)


def dup_third(parts):
    third = parts[:, 256:384]
    third = jnp.where(low_lanes(third.shape[0]), third, swapped(third))
    return jnp.concatenate([parts[:, 0:256], third], axis=1)


def offset_of(totals):
    y = lax.axis_index("y")
    kept = [jnp.where(y >= hop_of(slot), one[...].astype(F32), 0.0) for slot, one in enumerate(totals, 1)]
    return kept[0] + kept[1] + kept[2]


def position_sum(tiles):
    sums = [jnp.sum(tile, axis=0, keepdims=True) for tile in tiles]
    third = jnp.broadcast_to(sums[2], (8, LANES))
    return jnp.concatenate(sums[:2] + [(third + swapped(third))[0:1]], axis=1)


def states_kernel(sp, prefix, r1, r2, r3, states, up, down, far):
    members = same_group(384)
    base = sp[...].astype(F32) + offset_of((r1, r2, r3))
    spans = ((0, 256), (256, 512), (512, 640))
    sums = []
    for step in range(4):
        states[step] = (base + prefix[step]).astype(BF16)
        sums.append(position_sum([states[step, a:b].astype(F32) for a, b in spans]))
        for i, (first, last) in enumerate(((0, 224), (256, 480), (512, 608))):
            at = step * 96 + i * 32
            up[at : at + 32] = states[step, last : last + 32]
            down[at : at + 32] = states[step, first : first + 32]
    means = dup_third(group_sum(jnp.concatenate(sums + sums, axis=0), members) * (1.0 / 2560))
    spreads = []
    for step in range(4):
        mean = means[step : step + 1]
        centered = [states[step, a:b].astype(F32) - mean[:, 128 * i : 128 * i + 128] for i, (a, b) in enumerate(spans)]
        spreads.append(position_sum([c * c for c in centered]))
    spread = dup_third(group_sum(jnp.concatenate(spreads + spreads, axis=0), members))
    rest = jnp.concatenate([means[0:4], spread[0:4]], axis=0)
    for part in range(3):
        piece = rest.astype(BF16)
        rest = rest - piece.astype(F32)
        for tile in range(3):
            at = (part * 3 + tile) * 8
            value = piece[:, tile * 128 : tile * 128 + 128]
            far[at : at + 8] = value
            up[384 + at : 392 + at] = value
            down[384 + at : 392 + at] = value


def stats_of(ref, base):
    total = None
    for part in range(3):
        piece = jnp.concatenate(
            [ref[base + (part * 3 + t) * 8 : base + (part * 3 + t) * 8 + 8].astype(F32) for t in range(3)], axis=1
        )
        total = piece if total is None else total + piece
    return total[0:4], total[4:8]


def wide(vector):
    vector = vector[...].reshape(1, 320)
    return jnp.concatenate([vector, vector[:, 256:320]], axis=1)


def second_sweep_kernel(states, above, below, far, mine, gain_ref, bias_ref, wp, tb, out, taps, scales):
    gain, bias = wide(gain_ref), wide(bias_ref)
    x = lax.axis_index("x")
    parts = [stats_of(mine, 0), stats_of(above, 384), stats_of(below, 384), stats_of(far, 0)]
    mean = (parts[0][0] + parts[1][0] + parts[2][0] + parts[3][0]) * 0.25
    spread = parts[0][1] + parts[1][1] + parts[2][1] + parts[3][1]
    for one in parts:
        spread = spread + 2560.0 * (one[0] - mean) * (one[0] - mean)
    rstd = lax.rsqrt(spread * (1.0 / 10240) + 1e-05)
    for step in range(4):
        scales[step, 0:1] = mean[step : step + 1]
        scales[step, 1:2] = rstd[step : step + 1]

    def one_step(step, carry):
        here = scales[step]

        def normed(value, tile):
            lanes = slice(tile * 128, tile * 128 + 128)
            value = (value.astype(F32) - here[0:1, lanes]) * here[1:2, lanes]
            return silu(value * gain[:, lanes] + bias[:, lanes])

        edge = pl.multiple_of(step * 96, 32)
        tiles = []
        low = low_lanes(32)
        for tile in range(3):
            top = normed(above[pl.ds(edge + 32 * tile, 32)], tile)
            bottom = normed(below[pl.ds(edge + 32 * tile, 32)], tile)
            if tile < 2:
                middle = normed(states[step, 256 * tile : 256 * tile + 256], tile)
            else:
                middle = spread_tail(normed(states[step, 512:640], 2))
                top = jnp.where(low, swapped(top), top)
                bottom = jnp.where(low, bottom, swapped(bottom))
            top = jnp.where(x > 0, top, 0.0)
            bottom = jnp.where(x < 3, bottom, 0.0)
            tiles.append(jnp.concatenate([top, middle, bottom], axis=0))
        store_taps(taps, tiles)
        activated = silu(conv_rows(taps, wp) + tb[step][0:1])
        out[step, 0:256] = activated[:, 0:128].astype(BF16)
        out[step, 256:512] = activated[:, 128:256].astype(BF16)
        out[step, 512:640] = pack_tail(activated[:, 256:320]).astype(BF16)
        return carry

    lax.fori_loop(0, 4, one_step, 0)


def second_drift_kernel(own, before, after, tp, noise, rt, prefix, a3, run):
    run[...] = jnp.zeros_like(run)
    low = low_lanes(POS)

    def one_step(step, carry):
        tails = []
        for place, one in enumerate((before, own, after)):
            a3[:, place * 256 : place * 256 + 128] = one[step, 0:256]
            a3[:, place * 256 + 128 : place * 256 + 256] = one[step, 256:512]
            tails.append(spread_tail(one[step, 512:640].astype(F32)))
        a3[:, 768:896] = jnp.where(low, tails[0], tails[1]).astype(BF16)
        a3[:, 896:1024] = jnp.where(low, tails[2], 0.0).astype(BF16)
        for a, b, drift in drift_of(a3, tp, noise, step):
            now = run[a:b] + drift
            prefix[step, a:b] = now
            run[a:b] = now
        return carry

    lax.fori_loop(0, 4, one_step, 0)
    rt[...] = run[...].astype(BF16)


def result_kernel(sp, prefix, r1, r2, r3, *outs):
    x = lax.axis_index("x")
    base = sp[...].astype(F32) + offset_of((r1, r2, r3))
    for slot, out in enumerate(outs):
        out[...] = (base + prefix[lax.rem(x + hop_of(slot), 4)]).astype(BF16)


def unpack_kernel(r0, r1, r2, r3, out):
    x = lax.axis_index("x")
    for slot, one in enumerate((r0, r1, r2, r3)):
        start = pl.multiple_of(lax.rem(x + 4 - hop_of(slot), 4) * POS, POS)
        out[pl.ds(start, POS), 0:128] = one[0:256]
        out[pl.ds(start, POS), 128:256] = one[256:512]
        tail = spread_tail(one[512:640].astype(F32))
        out[pl.ds(start, POS), 256:320] = tail[:, 0:64].astype(BF16)


def call(body, outs, *args, scratch=(), flops=0, limit=24, hbm=0, sems=0):
    shapes = [jax.ShapeDtypeStruct(shape, kind) for shape, kind in outs]
    vmem = pl.BlockSpec(memory_space=pltpu.VMEM)
    nbytes = sum(a.size * a.dtype.itemsize for a in args) + sum(s.size * s.dtype.itemsize for s in shapes)
    scratch_shapes = [pltpu.VMEM(shape, kind) for shape, kind in scratch]
    if sems:
        scratch_shapes.append(pltpu.SemaphoreType.DMA((sems,)))
    return pl.pallas_call(
        body,
        out_shape=shapes,
        in_specs=[pl.BlockSpec(memory_space=pltpu.HBM)] * hbm + [vmem] * (len(args) - hbm),
        out_specs=[vmem] * len(shapes),
        scratch_shapes=scratch_shapes,
        compiler_params=pltpu.CompilerParams(vmem_limit_bytes=limit << 20),
        cost_estimate=pl.CostEstimate(flops=flops, bytes_accessed=nbytes, transcendentals=0),
    )(*(pltpu.with_memory_space_constraint(a, pltpu.HBM) if i < hbm else a for i, a in enumerate(args)))


def moved(value, place):
    pairs = []
    for y in range(4):
        for x in range(4):
            for z in range(8):
                for core in range(2):
                    ty, tx, frame = place(y, x, z * 2 + core)
                    pairs.append(((y * 4 + x) * 16 + z * 2 + core, (ty * 4 + tx) * 16 + frame))
    return lax.ppermute(value, AXES, pairs)


def hop_on(slot, core):
    return slot if core == 0 else 4 - slot


def swap_x(values):
    out = [values[0]]
    for slot in (1, 2, 3):
        out.append(moved(values[slot], lambda y, x, frame: (y, (x + hop_on(slot, frame % 2)) % 4, frame)))
    return out


def gather_y(value):
    out = []
    for slot in (1, 2, 3):
        out.append(moved(value, lambda y, x, frame: ((y + hop_on(slot, frame % 2)) % 4, x, frame)))
    return out


def along_x(value, hop):
    return moved(value, lambda y, x, frame: (y, (x + hop) % 4, frame))


def along_frame(value, hop):
    return moved(value, lambda y, x, frame: (y, x, (frame + hop) % 16))


def embedding_of(step_index, half_dim):
    frequencies = jnp.exp(-math.log(10000.0) * jnp.arange(half_dim, dtype=F32) / half_dim)
    angles = step_index.astype(F32) * frequencies
    return jnp.concatenate([jnp.cos(angles), jnp.sin(angles)]).astype(BF16)


def local(start_state, step_noise, timesteps, gn_gain, gn_bias, spatial_weight, temporal_weight, temb_weight):
    start = start_state.reshape(1024, 320)
    noise = step_noise.reshape(1024, 320)
    emb = embedding_of(timesteps[0], temb_weight.shape[0] // 2)
    emb = jnp.broadcast_to(jnp.pad(emb, (0, 64))[None], (16, 384))
    packed = (ROWS, LANES)
    four = (4, ROWS, LANES)

    *outgoing, start, wp, tp, tew, gain, bias = call(
        prologue_kernel,
        [((688, 128), BF16)] * 4
        + [((1024, 320), BF16), ((3, 1024, 320), BF16), ((1024, 320), BF16), ((320, 320), BF16), ((320,), F32), ((320,), F32)],
        noise, start, spatial_weight, temporal_weight, temb_weight, gn_gain, gn_bias, emb,
        scratch=(((1024, 320), BF16),),
        hbm=7,
        sems=29,
    )
    arrived = swap_x(outgoing)
    nq, sp = call(norm_start_kernel, [((3, 320, 128), BF16), (packed, BF16)], start, gain, bias)
    before, after = along_frame(nq, 1), along_frame(nq, -1)
    a3 = ((256, 1024), BF16)
    taps = ((320, 1024), BF16)
    run = (packed, F32)
    rt, prefix, noises, tb = call(
        first_sweep_kernel,
        [(packed, BF16), (four, F32), (four, BF16), ((4, 16, 320), F32)],
        nq, before, after, wp, tp, tew, *arrived,
        scratch=(taps, ((3, 256, 320), F32), a3, run),
        flops=2 * 1024 * 320 * 3200,
    )
    totals = gather_y(rt)
    states, up, down, far = call(
        states_kernel,
        [(four, BF16), ((464, 128), BF16), ((464, 128), BF16), ((72, 128), BF16)],
        sp, prefix, *totals,
    )
    activated = call(
        second_sweep_kernel,
        [(four, BF16)],
        states, along_x(up, 1), along_x(down, -1), along_x(far, 2), far, gain, bias, wp, tb,
        scratch=(taps, ((4, 8, 384), F32)),
        flops=2 * 1024 * 320 * 2880,
    )[0]
    rt, prefix = call(
        second_drift_kernel,
        [(packed, BF16), (four, F32)],
        activated, along_frame(activated, 1), along_frame(activated, -1), tp, noises,
        scratch=(a3, run),
        flops=2 * 1024 * 320 * 960,
    )
    totals = gather_y(rt)
    results = call(result_kernel, [(packed, BF16)] * 4, sp, prefix, *totals)
    out = call(unpack_kernel, [((1024, 320), BF16)], *swap_x(results))[0]
    return out.reshape(1, 1, 32, 32, 320)


def solution(mesh):
    split = Mesh(mesh.devices.reshape(4, 4, 8, 2), AXES)
    steps, frames = ("y", "x"), ("z", "core")
    placed = (
        P(frames, None, None, None),
        P(steps, frames, None, None, None),
        P(steps),
        P(),
        P(),
        P(),
        P(),
        P(),
    )
    return jax.shard_map(
        local,
        mesh=split,
        in_specs=placed,
        out_specs=P(steps, frames, None, None, None),
        check_vma=False,
    )
```

profile of v0, /device:TPU:6, one launch (start us, length us, event | category | flops | bytes accessed | tf_op | source)
XLA Modules:
  0.0 88.7 jit_solution(13635197649897366398)
XLA Ops:
  0.7 0.1 sine_convert_fusion
  0.7 0.1 fusion.2
  0.8 2.6 %shard_map.82 = (bf16[688,128]{1,0:T(8,128)(2,1)S(1)}, bf16[688,128]{1,0:T(8,128)(2,1)S(1)}, bf16[688,128]{1,0:T(8,128)(2,1)S(1)}, bf16[688,128]{1,0:T(8,128)(2,...) custom-call(bf16[1024,320]{1,0:T(8,128)(2,1)} %bitcast.4, ...), custom_call_target="tpu_custom_call" | custom-call | bytes 8176640 | tf_op jit(solution)/shard_map/pallas_call | solution.py:350
  3.4 1.2 %shard_map.83 = (bf16[3,320,128]{2,1,0:T(8,128)(2,1)S(1)}, bf16[640,128]{1,0:T(8,128)(2,1)S(1)}) custom-call(bf16[1024,320]{1,0:T(8,128)(2,1)S(1)} %get-tuple-element.31.start, f32[320]{0:T(512)S(1)} %get-tuple-element.32.gain_ref, f32[320]{0:T(512)S(1)} %get-tuple-element.33.bias_ref), custom_call_target="tpu_custom_call" | custom-call | bytes 1067520 | tf_op jit(solution)/shard_map/pallas_call | solution.py:350
  4.6 5.3 %collective-permute-start.1 = (bf16[3,320,128]{2,1,0:T(8,128)(2,1)S(1)}, bf16[3,320,128]{2,1,0:T(8,128)(2,1)S(1)}, u32[]{:S(2)}, u32[]{:S(2)}) collective-permute-start(bf16[3,320,128]{2,1,0:T(8,128)(2,1)S(1)} %get-tuple-element.35.own), channel_id=1, source_target_pairs={{0,15},{1,0},{2,1},{3,2},{4,3},{5,4},{6,5},{7,6},{8,7},{9,8},{10,9... | collective-permute-start | bytes 737288 | tf_op jit(solution)/shard_map/ppermute | solution.py:369
  9.9 0.0 collective-permute-start
  10.0 0.5 collective-permute-start.2
  10.4 2.4 %collective-permute-start.3 = (bf16[688,128]{1,0:T(8,128)(2,1)S(1)}, bf16[688,128]{1,0:T(8,128)(2,1)S(1)}, u32[]{:S(2)}, u32[]{:S(2)}) collective-permute-start(bf16[688,128]{1,0:T(8,128)(2,1)S(1)} %get-tuple-element.41), channel_id=1, source_target_pairs={{0,32},{1,33},{2,34},{3,35},{4,36},{5,37},{6,38},{7,39},{8,40},{9,... | collective-permute-start | bytes 528392 | tf_op jit(solution)/shard_map/ppermute | solution.py:369
  12.9 0.0 collective-permute-start.4
  12.9 3.9 %collective-permute-done.2.n1 = bf16[688,128]{1,0:T(8,128)(2,1)S(1)} collective-permute-done((bf16[688,128]{1,0:T(8,128)(2,1)S(1)}, bf16[688,128]{1,0:T(8,128)(2,1)S(1)}, u32[]{:S(2)}, u32[]{:S(2)}) %collective-permute-start.2) | collective-permute-done | bytes 176160 | tf_op jit(solution)/shard_map/ppermute | solution.py:369
  16.8 0.6 collective-permute-done.3.n2
  17.4 2.1 %collective-permute-done.4.n3 = bf16[688,128]{1,0:T(8,128)(2,1)S(1)} collective-permute-done((bf16[688,128]{1,0:T(8,128)(2,1)S(1)}, bf16[688,128]{1,0:T(8,128)(2,1)S(1)}, u32[]{:S(2)}, u32[]{:S(2)}) %collective-permute-start.4) | collective-permute-done | bytes 176160 | tf_op jit(solution)/shard_map/ppermute | solution.py:369
  19.5 0.0 collective-permute-done.1.after
  19.5 0.0 collective-permute-done.before
  19.5 5.1 %shard_map.84 = (bf16[640,128]{1,0:T(8,128)(2,1)S(1)}, f32[4,640,128]{2,1,0:T(8,128)S(1)}, bf16[4,640,128]{2,1,0:T(8,128)(2,1)S(1)}, f32[4,16,320]{2,1,0:T(8,128)S(1)}) custom-call(bf16[3,320,128]{2,1,0:T(8,128)(2,1)S(1)} %get-tuple-element.35.own, bf16[3,320,128]{2,1,0:T(8,128)(2,1)S(1)} %collective-permute-done.before, ...), custom_call_target="tpu_custom_call" | custom-call | flops 2097152000 | bytes 6479872 | tf_op jit(solution)/shard_map/pallas_call | solution.py:350
  24.6 3.1 %collective-permute-start.7 = (bf16[640,128]{1,0:T(8,128)(2,1)S(1)}, bf16[640,128]{1,0:T(8,128)(2,1)S(1)}, u32[]{:S(2)}, u32[]{:S(2)}) collective-permute-start(bf16[640,128]{1,0:T(8,128)(2,1)S(1)} %get-tuple-element.44), channel_id=1, source_target_pairs={{0,192},{1,65},{2,194},{3,67},{4,196},{5,69},{6,198},{7,71},{8,200... | collective-permute-start | bytes 491528 | tf_op jit(solution)/shard_map/ppermute | solution.py:369
  27.7 0.6 collective-permute-start.6
  28.3 1.0 %collective-permute-start.5 = (bf16[640,128]{1,0:T(8,128)(2,1)S(1)}, bf16[640,128]{1,0:T(8,128)(2,1)S(1)}, u32[]{:S(2)}, u32[]{:S(2)}) collective-permute-start(bf16[640,128]{1,0:T(8,128)(2,1)S(1)} %get-tuple-element.44), channel_id=1, source_target_pairs={{0,64},{1,193},{2,66},{3,195},{4,68},{5,197},{6,70},{7,199},{8,72}... | collective-permute-start | bytes 491528 | tf_op jit(solution)/shard_map/ppermute | solution.py:369
  29.3 2.2 %collective-permute-done.7.r3 = bf16[640,128]{1,0:T(8,128)(2,1)S(1)} collective-permute-done((bf16[640,128]{1,0:T(8,128)(2,1)S(1)}, bf16[640,128]{1,0:T(8,128)(2,1)S(1)}, u32[]{:S(2)}, u32[]{:S(2)}) %collective-permute-start.7) | collective-permute-done | bytes 163872 | tf_op jit(solution)/shard_map/ppermute | solution.py:369
  31.5 3.1 %collective-permute-done.6.r2 = bf16[640,128]{1,0:T(8,128)(2,1)S(1)} collective-permute-done((bf16[640,128]{1,0:T(8,128)(2,1)S(1)}, bf16[640,128]{1,0:T(8,128)(2,1)S(1)}, u32[]{:S(2)}, u32[]{:S(2)}) %collective-permute-start.6) | collective-permute-done | bytes 163872 | tf_op jit(solution)/shard_map/ppermute | solution.py:369
  34.6 1.7 %collective-permute-done.5.r1 = bf16[640,128]{1,0:T(8,128)(2,1)S(1)} collective-permute-done((bf16[640,128]{1,0:T(8,128)(2,1)S(1)}, bf16[640,128]{1,0:T(8,128)(2,1)S(1)}, u32[]{:S(2)}, u32[]{:S(2)}) %collective-permute-start.5) | collective-permute-done | bytes 163872 | tf_op jit(solution)/shard_map/ppermute | solution.py:369
  36.3 1.4 %shard_map.85 = (bf16[4,640,128]{2,1,0:T(8,128)(2,1)S(1)}, bf16[464,128]{1,0:T(8,128)(2,1)S(1)}, bf16[464,128]{1,0:T(8,128)(2,1)S(1)}, bf16[72,128]{1,0:T(8,128)(2,1)S(1)}) custom-call(bf16[640,128]{1,0:T(8,128)(2,1)S(1)} %get-tuple-element.34.sp, f32[4,640,128]{2,1,0:T(8,128)S(1)} %get-tuple-element.43.prefix, ...), custom_call_target="tpu_custom_call" | custom-call | bytes 2877440 | tf_op jit(solution)/shard_map/pallas_call | solution.py:350
  37.7 1.9 %collective-permute-start.8 = (bf16[464,128]{1,0:T(8,128)(2,1)S(1)}, bf16[464,128]{1,0:T(8,128)(2,1)S(1)}, u32[]{:S(2)}, u32[]{:S(2)}) collective-permute-start(bf16[464,128]{1,0:T(8,128)(2,1)S(1)} %get-tuple-element.46), channel_id=1, source_target_pairs={{0,16},{1,17},{2,18},{3,19},{4,20},{5,21},{6,22},{7,23},{8,24},{9,... | collective-permute-start | bytes 356360 | tf_op jit(solution)/shard_map/ppermute | solution.py:369
  39.6 0.2 collective-permute-start.9
  39.8 1.8 %collective-permute-start.10 = (bf16[72,128]{1,0:T(8,128)(2,1)S(1)}, bf16[72,128]{1,0:T(8,128)(2,1)S(1)}, u32[]{:S(2)}, u32[]{:S(2)}) collective-permute-start(bf16[72,128]{1,0:T(8,128)(2,1)S(1)} %get-tuple-element.48.mine), channel_id=1, source_target_pairs={{0,32},{1,33},{2,34},{3,35},{4,36},{5,37},{6,38},{7,39},{8,40},{9,... | collective-permute-start | bytes 55304 | tf_op jit(solution)/shard_map/ppermute | solution.py:369
  41.6 3.6 %collective-permute-done.10.far = bf16[72,128]{1,0:T(8,128)(2,1)S(1)} collective-permute-done((bf16[72,128]{1,0:T(8,128)(2,1)S(1)}, bf16[72,128]{1,0:T(8,128)(2,1)S(1)}, u32[]{:S(2)}, u32[]{:S(2)}) %collective-permute-start.10) | collective-permute-done | bytes 18464 | tf_op jit(solution)/shard_map/ppermute | solution.py:369
  45.2 0.0 collective-permute-done.8.above
  45.2 0.7 collective-permute-done.9.below
  45.9 5.1 %shard_map.86.own = bf16[4,640,128]{2,1,0:T(8,128)(2,1)S(1)} custom-call(bf16[4,640,128]{2,1,0:T(8,128)(2,1)S(1)} %get-tuple-element.45.states, bf16[464,128]{1,0:T(8,128)(2,1)S(1)} %collective-permute-done.8.above, bf16[464,128]{1,0:T(8,128)(2,1)S(1)} %collective-permute-done.9.below, bf16[72,128]{1,0:T(8,128)(2,1)S(1)} %collective-permute-done.10.far, ...), custom_call_target="tpu_custom_call" | custom-call | flops 1887436800 | bytes 3635712 | tf_op jit(solution)/shard_map/pallas_call | solution.py:350
  50.9 1.3 %collective-permute-start.12 = (bf16[4,640,128]{2,1,0:T(8,128)(2,1)S(1)}, bf16[4,640,128]{2,1,0:T(8,128)(2,1)S(1)}, u32[]{:S(2)}, u32[]{:S(2)}) collective-permute-start(bf16[4,640,128]{2,1,0:T(8,128)(2,1)S(1)} %shard_map.86.own), channel_id=1, source_target_pairs={{0,15},{1,0},{2,1},{3,2},{4,3},{5,4},{6,5},{7,6},{8,7},{9,8},{10,9... | collective-permute-start | bytes 1966088 | tf_op jit(solution)/shard_map/ppermute | solution.py:369
  52.2 0.0 collective-permute-start.11
  52.2 8.1 %collective-permute-done.12.after = bf16[4,640,128]{2,1,0:T(8,128)(2,1)S(1)} collective-permute-done((bf16[4,640,128]{2,1,0:T(8,128)(2,1)S(1)}, bf16[4,640,128]{2,1,0:T(8,128)(2,1)S(1)}, u32[]{:S(2)}, u32[]{:S(2)}) %collective-permute-start.12) | collective-permute-done | bytes 655392 | tf_op jit(solution)/shard_map/ppermute | solution.py:369
  60.3 3.1 %collective-permute-done.11.before = bf16[4,640,128]{2,1,0:T(8,128)(2,1)S(1)} collective-permute-done((bf16[4,640,128]{2,1,0:T(8,128)(2,1)S(1)}, bf16[4,640,128]{2,1,0:T(8,128)(2,1)S(1)}, u32[]{:S(2)}, u32[]{:S(2)}) %collective-permute-start.11) | collective-permute-done | bytes 655392 | tf_op jit(solution)/shard_map/ppermute | solution.py:369
  63.4 2.0 %shard_map.87 = (bf16[640,128]{1,0:T(8,128)(2,1)S(1)}, f32[4,640,128]{2,1,0:T(8,128)S(1)}) custom-call(bf16[4,640,128]{2,1,0:T(8,128)(2,1)S(1)} %shard_map.86.own, bf16[4,640,128]{2,1,0:T(8,128)(2,1)S(1)} %collective-permute-done.11.before, bf16[4,640,128]{2,1,0:T(8,128)(2,1)S(1)} %collective-permute-done.12.after, ...), custom_call_target="tpu_custom_call" | custom-call | flops 629145600 | bytes 4751360 | tf_op jit(solution)/shard_map/pallas_call | solution.py:350
  65.4 3.3 %collective-permute-start.15 = (bf16[640,128]{1,0:T(8,128)(2,1)S(1)}, bf16[640,128]{1,0:T(8,128)(2,1)S(1)}, u32[]{:S(2)}, u32[]{:S(2)}) collective-permute-start(bf16[640,128]{1,0:T(8,128)(2,1)S(1)} %get-tuple-element.52), channel_id=1, source_target_pairs={{0,192},{1,65},{2,194},{3,67},{4,196},{5,69},{6,198},{7,71},{8,200... | collective-permute-start | bytes 491528 | tf_op jit(solution)/shard_map/ppermute | solution.py:369
  68.7 0.2 collective-permute-start.14
  69.0 0.8 collective-permute-start.13
  69.8 3.6 %collective-permute-done.15.r3 = bf16[640,128]{1,0:T(8,128)(2,1)S(1)} collective-permute-done((bf16[640,128]{1,0:T(8,128)(2,1)S(1)}, bf16[640,128]{1,0:T(8,128)(2,1)S(1)}, u32[]{:S(2)}, u32[]{:S(2)}) %collective-permute-start.15) | collective-permute-done | bytes 163872 | tf_op jit(solution)/shard_map/ppermute | solution.py:369
  73.4 2.3 %collective-permute-done.14.r2 = bf16[640,128]{1,0:T(8,128)(2,1)S(1)} collective-permute-done((bf16[640,128]{1,0:T(8,128)(2,1)S(1)}, bf16[640,128]{1,0:T(8,128)(2,1)S(1)}, u32[]{:S(2)}, u32[]{:S(2)}) %collective-permute-start.14) | collective-permute-done | bytes 163872 | tf_op jit(solution)/shard_map/ppermute | solution.py:369
  75.6 1.6 %collective-permute-done.13.r1 = bf16[640,128]{1,0:T(8,128)(2,1)S(1)} collective-permute-done((bf16[640,128]{1,0:T(8,128)(2,1)S(1)}, bf16[640,128]{1,0:T(8,128)(2,1)S(1)}, u32[]{:S(2)}, u32[]{:S(2)}) %collective-permute-start.13) | collective-permute-done | bytes 163872 | tf_op jit(solution)/shard_map/ppermute | solution.py:369
  77.3 0.2 shard_map.88
  77.5 1.6 %collective-permute-start.16 = (bf16[640,128]{1,0:T(8,128)(2,1)S(1)}, bf16[640,128]{1,0:T(8,128)(2,1)S(1)}, u32[]{:S(2)}, u32[]{:S(2)}) collective-permute-start(bf16[640,128]{1,0:T(8,128)(2,1)S(1)} %get-tuple-element.54), channel_id=1, source_target_pairs={{0,16},{1,49},{2,18},{3,51},{4,20},{5,53},{6,22},{7,55},{8,24},{9,... | collective-permute-start | bytes 491528 | tf_op jit(solution)/shard_map/ppermute | solution.py:369
  79.1 0.7 collective-permute-start.17
  79.8 1.0 %collective-permute-start.18 = (bf16[640,128]{1,0:T(8,128)(2,1)S(1)}, bf16[640,128]{1,0:T(8,128)(2,1)S(1)}, u32[]{:S(2)}, u32[]{:S(2)}) collective-permute-start(bf16[640,128]{1,0:T(8,128)(2,1)S(1)} %get-tuple-element.56), channel_id=1, source_target_pairs={{0,48},{1,17},{2,50},{3,19},{4,52},{5,21},{6,54},{7,23},{8,56},{9,... | collective-permute-start | bytes 491528 | tf_op jit(solution)/shard_map/ppermute | solution.py:369
  80.8 2.1 %collective-permute-done.16.r1 = bf16[640,128]{1,0:T(8,128)(2,1)S(1)} collective-permute-done((bf16[640,128]{1,0:T(8,128)(2,1)S(1)}, bf16[640,128]{1,0:T(8,128)(2,1)S(1)}, u32[]{:S(2)}, u32[]{:S(2)}) %collective-permute-start.16) | collective-permute-done | bytes 163872 | tf_op jit(solution)/shard_map/ppermute | solution.py:369
  82.9 3.1 %collective-permute-done.17.r2 = bf16[640,128]{1,0:T(8,128)(2,1)S(1)} collective-permute-done((bf16[640,128]{1,0:T(8,128)(2,1)S(1)}, bf16[640,128]{1,0:T(8,128)(2,1)S(1)}, u32[]{:S(2)}, u32[]{:S(2)}) %collective-permute-start.17) | collective-permute-done | bytes 163872 | tf_op jit(solution)/shard_map/ppermute | solution.py:369
  86.0 1.7 %collective-permute-done.18.r3 = bf16[640,128]{1,0:T(8,128)(2,1)S(1)} collective-permute-done((bf16[640,128]{1,0:T(8,128)(2,1)S(1)}, bf16[640,128]{1,0:T(8,128)(2,1)S(1)}, u32[]{:S(2)}, u32[]{:S(2)}) %collective-permute-start.18) | collective-permute-done | bytes 163872 | tf_op jit(solution)/shard_map/ppermute | solution.py:369
  87.6 1.0 %shard_map.89 = bf16[1024,320]{1,0:T(8,128)(2,1)} custom-call(bf16[640,128]{1,0:T(8,128)(2,1)S(1)} %get-tuple-element.53.r0, bf16[640,128]{1,0:T(8,128)(2,1)S(1)} %collective-permute-done.16.r1, bf16[640,128]{1,0:T(8,128)(2,1)S(1)} %collective-permute-done.17.r2, bf16[640,128]{1,0:T(8,128)(2,1)S(1)} %collective-permute-done.18.r3), custom_call_target="tpu_custom_call" | custom-call | bytes 1310720 | tf_op jit(solution)/shard_map/pallas_call | solution.py:350
  (1 shorter events, 0.0 us)
Async XLA Ops:
  4.6 14.9 %collective-permute-start.1 = (bf16[3,320,128]{2,1,0:T(8,128)(2,1)S(1)}, bf16[3,320,128]{2,1,0:T(8,128)(2,1)S(1)}, u32[]{:S(2)}, u32[]{:S(2)}) collective-permute-start(bf16[3,320,128]{2,1,0:T(8,128)(2,1)S(1)} %get-tuple-element.35.own), channel_id=1, source_target_pairs={{0,15},{1,0},{2,1},{3,2},{4,3},{5,4},{6,5},{7,6},{8,7},{9,8},{10,9... | collective-permute-start | bytes 737288 | tf_op jit(solution)/shard_map/ppermute | solution.py:369
  9.9 9.6 %collective-permute-start = (bf16[3,320,128]{2,1,0:T(8,128)(2,1)S(1)}, bf16[3,320,128]{2,1,0:T(8,128)(2,1)S(1)}, u32[]{:S(2)}, u32[]{:S(2)}) collective-permute-start(bf16[3,320,128]{2,1,0:T(8,128)(2,1)S(1)} %get-tuple-element.35.own), channel_id=1, source_target_pairs={{0,1},{1,2},{2,3},{3,4},{4,5},{5,6},{6,7},{7,8},{8,9},{9,10},{10,1... | collective-permute-start | bytes 737288 | tf_op jit(solution)/shard_map/ppermute | solution.py:369
  10.0 6.8 %collective-permute-start.2 = (bf16[688,128]{1,0:T(8,128)(2,1)S(1)}, bf16[688,128]{1,0:T(8,128)(2,1)S(1)}, u32[]{:S(2)}, u32[]{:S(2)}) collective-permute-start(bf16[688,128]{1,0:T(8,128)(2,1)S(1)} %get-tuple-element.40), channel_id=1, source_target_pairs={{0,16},{1,49},{2,18},{3,51},{4,20},{5,53},{6,22},{7,55},{8,24},{9,... | collective-permute-start | bytes 528392 | tf_op jit(solution)/shard_map/ppermute | solution.py:369
  10.4 7.0 %collective-permute-start.3 = (bf16[688,128]{1,0:T(8,128)(2,1)S(1)}, bf16[688,128]{1,0:T(8,128)(2,1)S(1)}, u32[]{:S(2)}, u32[]{:S(2)}) collective-permute-start(bf16[688,128]{1,0:T(8,128)(2,1)S(1)} %get-tuple-element.41), channel_id=1, source_target_pairs={{0,32},{1,33},{2,34},{3,35},{4,36},{5,37},{6,38},{7,39},{8,40},{9,... | collective-permute-start | bytes 528392 | tf_op jit(solution)/shard_map/ppermute | solution.py:369
  12.9 6.7 %collective-permute-start.4 = (bf16[688,128]{1,0:T(8,128)(2,1)S(1)}, bf16[688,128]{1,0:T(8,128)(2,1)S(1)}, u32[]{:S(2)}, u32[]{:S(2)}) collective-permute-start(bf16[688,128]{1,0:T(8,128)(2,1)S(1)} %get-tuple-element.42), channel_id=1, source_target_pairs={{0,48},{1,17},{2,50},{3,19},{4,52},{5,21},{6,54},{7,23},{8,56},{9,... | collective-permute-start | bytes 528392 | tf_op jit(solution)/shard_map/ppermute | solution.py:369
  24.6 6.9 %collective-permute-start.7 = (bf16[640,128]{1,0:T(8,128)(2,1)S(1)}, bf16[640,128]{1,0:T(8,128)(2,1)S(1)}, u32[]{:S(2)}, u32[]{:S(2)}) collective-permute-start(bf16[640,128]{1,0:T(8,128)(2,1)S(1)} %get-tuple-element.44), channel_id=1, source_target_pairs={{0,192},{1,65},{2,194},{3,67},{4,196},{5,69},{6,198},{7,71},{8,200... | collective-permute-start | bytes 491528 | tf_op jit(solution)/shard_map/ppermute | solution.py:369
  27.7 6.9 %collective-permute-start.6 = (bf16[640,128]{1,0:T(8,128)(2,1)S(1)}, bf16[640,128]{1,0:T(8,128)(2,1)S(1)}, u32[]{:S(2)}, u32[]{:S(2)}) collective-permute-start(bf16[640,128]{1,0:T(8,128)(2,1)S(1)} %get-tuple-element.44), channel_id=1, source_target_pairs={{0,128},{1,129},{2,130},{3,131},{4,132},{5,133},{6,134},{7,135},{8... | collective-permute-start | bytes 491528 | tf_op jit(solution)/shard_map/ppermute | solution.py:369
  28.3 7.9 %collective-permute-start.5 = (bf16[640,128]{1,0:T(8,128)(2,1)S(1)}, bf16[640,128]{1,0:T(8,128)(2,1)S(1)}, u32[]{:S(2)}, u32[]{:S(2)}) collective-permute-start(bf16[640,128]{1,0:T(8,128)(2,1)S(1)} %get-tuple-element.44), channel_id=1, source_target_pairs={{0,64},{1,193},{2,66},{3,195},{4,68},{5,197},{6,70},{7,199},{8,72}... | collective-permute-start | bytes 491528 | tf_op jit(solution)/shard_map/ppermute | solution.py:369
  37.7 7.5 %collective-permute-start.8 = (bf16[464,128]{1,0:T(8,128)(2,1)S(1)}, bf16[464,128]{1,0:T(8,128)(2,1)S(1)}, u32[]{:S(2)}, u32[]{:S(2)}) collective-permute-start(bf16[464,128]{1,0:T(8,128)(2,1)S(1)} %get-tuple-element.46), channel_id=1, source_target_pairs={{0,16},{1,17},{2,18},{3,19},{4,20},{5,21},{6,22},{7,23},{8,24},{9,... | collective-permute-start | bytes 356360 | tf_op jit(solution)/shard_map/ppermute | solution.py:369
  39.6 6.2 %collective-permute-start.9 = (bf16[464,128]{1,0:T(8,128)(2,1)S(1)}, bf16[464,128]{1,0:T(8,128)(2,1)S(1)}, u32[]{:S(2)}, u32[]{:S(2)}) collective-permute-start(bf16[464,128]{1,0:T(8,128)(2,1)S(1)} %get-tuple-element.47), channel_id=1, source_target_pairs={{0,48},{1,49},{2,50},{3,51},{4,52},{5,53},{6,54},{7,55},{8,56},{9,... | collective-permute-start | bytes 356360 | tf_op jit(solution)/shard_map/ppermute | solution.py:369
  39.8 5.4 %collective-permute-start.10 = (bf16[72,128]{1,0:T(8,128)(2,1)S(1)}, bf16[72,128]{1,0:T(8,128)(2,1)S(1)}, u32[]{:S(2)}, u32[]{:S(2)}) collective-permute-start(bf16[72,128]{1,0:T(8,128)(2,1)S(1)} %get-tuple-element.48.mine), channel_id=1, source_target_pairs={{0,32},{1,33},{2,34},{3,35},{4,36},{5,37},{6,38},{7,39},{8,40},{9,... | collective-permute-start | bytes 55304 | tf_op jit(solution)/shard_map/ppermute | solution.py:369
  50.9 9.4 %collective-permute-start.12 = (bf16[4,640,128]{2,1,0:T(8,128)(2,1)S(1)}, bf16[4,640,128]{2,1,0:T(8,128)(2,1)S(1)}, u32[]{:S(2)}, u32[]{:S(2)}) collective-permute-start(bf16[4,640,128]{2,1,0:T(8,128)(2,1)S(1)} %shard_map.86.own), channel_id=1, source_target_pairs={{0,15},{1,0},{2,1},{3,2},{4,3},{5,4},{6,5},{7,6},{8,7},{9,8},{10,9... | collective-permute-start | bytes 1966088 | tf_op jit(solution)/shard_map/ppermute | solution.py:369
  52.2 11.2 %collective-permute-start.11 = (bf16[4,640,128]{2,1,0:T(8,128)(2,1)S(1)}, bf16[4,640,128]{2,1,0:T(8,128)(2,1)S(1)}, u32[]{:S(2)}, u32[]{:S(2)}) collective-permute-start(bf16[4,640,128]{2,1,0:T(8,128)(2,1)S(1)} %shard_map.86.own), channel_id=1, source_target_pairs={{0,1},{1,2},{2,3},{3,4},{4,5},{5,6},{6,7},{7,8},{8,9},{9,10},{10,1... | collective-permute-start | bytes 1966088 | tf_op jit(solution)/shard_map/ppermute | solution.py:369
  65.4 7.9 %collective-permute-start.15 = (bf16[640,128]{1,0:T(8,128)(2,1)S(1)}, bf16[640,128]{1,0:T(8,128)(2,1)S(1)}, u32[]{:S(2)}, u32[]{:S(2)}) collective-permute-start(bf16[640,128]{1,0:T(8,128)(2,1)S(1)} %get-tuple-element.52), channel_id=1, source_target_pairs={{0,192},{1,65},{2,194},{3,67},{4,196},{5,69},{6,198},{7,71},{8,200... | collective-permute-start | bytes 491528 | tf_op jit(solution)/shard_map/ppermute | solution.py:369
  68.7 6.9 %collective-permute-start.14 = (bf16[640,128]{1,0:T(8,128)(2,1)S(1)}, bf16[640,128]{1,0:T(8,128)(2,1)S(1)}, u32[]{:S(2)}, u32[]{:S(2)}) collective-permute-start(bf16[640,128]{1,0:T(8,128)(2,1)S(1)} %get-tuple-element.52), channel_id=1, source_target_pairs={{0,128},{1,129},{2,130},{3,131},{4,132},{5,133},{6,134},{7,135},{8... | collective-permute-start | bytes 491528 | tf_op jit(solution)/shard_map/ppermute | solution.py:369
  69.0 8.3 %collective-permute-start.13 = (bf16[640,128]{1,0:T(8,128)(2,1)S(1)}, bf16[640,128]{1,0:T(8,128)(2,1)S(1)}, u32[]{:S(2)}, u32[]{:S(2)}) collective-permute-start(bf16[640,128]{1,0:T(8,128)(2,1)S(1)} %get-tuple-element.52), channel_id=1, source_target_pairs={{0,64},{1,193},{2,66},{3,195},{4,68},{5,197},{6,70},{7,199},{8,72}... | collective-permute-start | bytes 491528 | tf_op jit(solution)/shard_map/ppermute | solution.py:369
  77.5 5.4 %collective-permute-start.16 = (bf16[640,128]{1,0:T(8,128)(2,1)S(1)}, bf16[640,128]{1,0:T(8,128)(2,1)S(1)}, u32[]{:S(2)}, u32[]{:S(2)}) collective-permute-start(bf16[640,128]{1,0:T(8,128)(2,1)S(1)} %get-tuple-element.54), channel_id=1, source_target_pairs={{0,16},{1,49},{2,18},{3,51},{4,20},{5,53},{6,22},{7,55},{8,24},{9,... | collective-permute-start | bytes 491528 | tf_op jit(solution)/shard_map/ppermute | solution.py:369
  79.1 6.9 %collective-permute-start.17 = (bf16[640,128]{1,0:T(8,128)(2,1)S(1)}, bf16[640,128]{1,0:T(8,128)(2,1)S(1)}, u32[]{:S(2)}, u32[]{:S(2)}) collective-permute-start(bf16[640,128]{1,0:T(8,128)(2,1)S(1)} %get-tuple-element.55), channel_id=1, source_target_pairs={{0,32},{1,33},{2,34},{3,35},{4,36},{5,37},{6,38},{7,39},{8,40},{9,... | collective-permute-start | bytes 491528 | tf_op jit(solution)/shard_map/ppermute | solution.py:369
  79.8 7.8 %collective-permute-start.18 = (bf16[640,128]{1,0:T(8,128)(2,1)S(1)}, bf16[640,128]{1,0:T(8,128)(2,1)S(1)}, u32[]{:S(2)}, u32[]{:S(2)}) collective-permute-start(bf16[640,128]{1,0:T(8,128)(2,1)S(1)} %get-tuple-element.56), channel_id=1, source_target_pairs={{0,48},{1,17},{2,50},{3,19},{4,52},{5,21},{6,54},{7,23},{8,56},{9,... | collective-permute-start | bytes 491528 | tf_op jit(solution)/shard_map/ppermute | solution.py:369
where the time goes:
time: 88.8 us; the launch traced here: 88.7 us
  waiting for transfers between devices  43.4 us (49%)
  starting transfers between devices  25.7 us (29%)
  Pallas kernels  18.6 us (21%)
    ppermute x19, waiting for transfers between devices, moved(): return lax.ppermute(value, AXES, pairs)  43.4 us
    ppermute x19, starting transfers between devices, moved(): return lax.ppermute(value, AXES, pairs)  25.7 us
    pallas_call x8, Pallas kernels, call(): pl.pallas_call(body, out_shape=shapes, in_specs=[pl.BlockSpec(memory_spac...  18.6 us
  transfers between devices with their start and end apart: 19, of which 16 were waited for; matrix products, arithmetic and copies ran while one was open for 0% of the time, Pallas kernels for 0%

commit v1 on v0

--- a/solution.py
+++ b/solution.py
@@ -1,3 +1,4 @@
+import functools
 import math
 
 import jax
@@ -81,13 +82,30 @@
     return jnp.where(lax.axis_index("core") == 0, slot, (4 - slot) % 4)
 
 
-def prologue_kernel(
-    noise_hbm, start_hbm, sw, tw, tew_hbm, gain_hbm, bias_hbm, emb,
-    o0, o1, o2, o3, start, wp, tp, tew, gain, bias, noise, sems,
+def pack_kernel(noise_hbm, emb, o0, o1, o2, o3, noise, sems):
+    x = lax.axis_index("x")
+    outs = {0: o0, 1: o1, 2: o2, 3: o3}
+    copies = {}
+    for slot in (1, 3, 2, 0):
+        at = pl.multiple_of(lax.rem(x + hop_of(slot), 4) * POS, POS)
+        copies[slot] = pltpu.make_async_copy(noise_hbm.at[pl.ds(at, POS)], noise.at[slot], sems.at[slot])
+        copies[slot].start()
+    for slot, copy in copies.items():
+        out = outs[slot]
+        copy.wait()
+        out[0:256] = noise[slot, :, 0:128]
+        out[256:512] = noise[slot, :, 128:256]
+        out[512:640] = pack_tail(noise[slot, :, 256:320].astype(F32)).astype(BF16)
+        for tile in range(3):
+            out[640 + 16 * tile : 656 + 16 * tile] = emb[:, tile * 128 : tile * 128 + 128]
+
+
+def norm_start_kernel(
+    start_hbm, gain_hbm, bias_hbm, sw, tw, tew_hbm, nq, sp, wp, tp, tew, gain_ref, bias_ref, start, sems
 ):
     x = lax.axis_index("x")
     frame = lax.axis_index("z") * 2 + lax.axis_index("core")
-    moves = [(noise_hbm, noise), (start_hbm, start), (gain_hbm, gain), (bias_hbm, bias)]
+    moves = [(start_hbm, start), (gain_hbm, gain_ref), (bias_hbm, bias_ref)]
     for row in range(4):
         out = tp if row == 3 else wp.at[row]
         for place in range(3):
@@ -98,30 +116,12 @@
     copies = [pltpu.make_async_copy(source, target, sems.at[i]) for i, (source, target) in enumerate(moves)]
     for copy in copies:
         copy.start()
+    members = same_group(320)
     for row in range(3):
         wp[row, 960:1024] = jnp.zeros((64, 320), BF16)
     tp[960:1024] = jnp.zeros((64, 320), BF16)
-    copies[0].wait()
-    for slot, out in enumerate((o0, o1, o2, o3)):
-        at = pl.multiple_of(lax.rem(x + hop_of(slot), 4) * POS, POS)
-        out[0:256] = noise[pl.ds(at, POS), 0:128]
-        out[256:512] = noise[pl.ds(at, POS), 128:256]
-        out[512:640] = pack_tail(noise[pl.ds(at, POS), 256:320].astype(F32)).astype(BF16)
-        for tile in range(3):
-            out[640 + 16 * tile : 656 + 16 * tile] = emb[:, tile * 128 : tile * 128 + 128]
-    for copy in copies[1:]:
+    for copy in copies[:3]:
         copy.wait()
-    for place, missing in ((0, frame == 0), (2, frame == 15)):
-
-        @pl.when(missing)
-        def _():
-            tp[place * 256 : place * 256 + 256] = jnp.zeros((256, 320), BF16)
-            tp[768 + 64 * place : 832 + 64 * place] = jnp.zeros((64, 320), BF16)
-
-
-def norm_start_kernel(start, gain_ref, bias_ref, nq, sp):
-    x = lax.axis_index("x")
-    members = same_group(320)
     values = start[...].astype(F32)
     mean = group_sum(jnp.broadcast_to(jnp.sum(values, axis=0, keepdims=True), (8, 320)), members)[0:1] * (1.0 / 10240)
     centered = start[...].astype(F32) - mean
@@ -147,16 +147,40 @@
     sp[0:256] = start[pl.ds(first, POS), 0:128]
     sp[256:512] = start[pl.ds(first, POS), 128:256]
     sp[512:640] = pack_tail(start[pl.ds(first, POS), 256:320].astype(F32)).astype(BF16)
-
-
-def drift_of(a3, tp, noise, step):
-    update = jnp.dot(a3[...], tp[...], preferred_element_type=F32)
-    packed = (update[:, 0:128], update[:, 128:256], pack_tail(update[:, 256:320]))
-    spans = ((0, 256), (256, 512), (512, 640))
-    return [(a, b, 0.25 * (u + noise[step, a:b].astype(F32))) for u, (a, b) in zip(packed, spans)]
-
-
-def first_sweep_kernel(own, before, after, wp, tp, tew, n0, n1, n2, n3, rt, prefix, noise, tb, taps, pre, a3, run):
+    for copy in copies[3:]:
+        copy.wait()
+    for place, missing in ((0, frame == 0), (2, frame == 15)):
+
+        @pl.when(missing)
+        def _():
+            tp[place * 256 : place * 256 + 256] = jnp.zeros((256, 320), BF16)
+            tp[768 + 64 * place : 832 + 64 * place] = jnp.zeros((64, 320), BF16)
+
+
+def first_conv_kernel(*refs):
+    *normed, wp, pre, taps = refs
+    for place, one in enumerate(normed):
+        store_taps(taps, [one[i].astype(F32) for i in range(3)])
+        pre[place] = conv_rows(taps, wp)
+
+
+SPANS = ((0, 256), (256, 512), (512, 640))
+
+
+def packed_update(a3, tp):
+    update = jnp.dot(a3, tp[...], preferred_element_type=F32)
+    return update[:, 0:128], update[:, 128:256], pack_tail(update[:, 256:320])
+
+
+def store_frames(a3, parts):
+    for place, part in enumerate(parts):
+        a3[:, place * 256 : place * 256 + 256] = part[:, 0:256].astype(BF16)
+    a3[:, 768:896] = jnp.concatenate([parts[0][:, 256:320], parts[1][:, 256:320]], axis=1).astype(BF16)
+    last = parts[2][:, 256:320]
+    a3[:, 896:1024] = jnp.concatenate([last, jnp.zeros_like(last)], axis=1).astype(BF16)
+
+
+def first_total_kernel(here, sides, tp, tew, n0, n1, n2, n3, rt, noise, tb, a3s, sums, a3):
     x = lax.axis_index("x")
     for slot, one in enumerate((n0, n1, n2, n3)):
         step = lax.rem(x + 4 - hop_of(slot), 4)
@@ -167,28 +191,36 @@
             + jnp.dot(one[672:688, 0:64], tew[256:320], preferred_element_type=F32)
         )
         tb[step] = bias / (1.0 + jnp.exp(-bias))
-    for place, normed in enumerate((before, own, after)):
-        store_taps(taps, [normed[i].astype(F32) for i in range(3)])
-        pre[place] = conv_rows(taps, wp)
-    run[...] = jnp.zeros_like(run)
+    sums[...] = jnp.zeros_like(sums)
 
     def one_step(step, carry):
         bias = tb[step][0:1]
-        tails = []
-        for place in range(3):
-            activated = silu(pre[place] + bias)
-            a3[:, place * 256 : place * 256 + 256] = activated[:, 0:256].astype(BF16)
-            tails.append(activated[:, 256:320])
-        a3[:, 768:896] = jnp.concatenate(tails[:2], axis=1).astype(BF16)
-        a3[:, 896:1024] = jnp.concatenate([tails[2], jnp.zeros_like(tails[2])], axis=1).astype(BF16)
-        for a, b, drift in drift_of(a3, tp, noise, step):
-            earlier = run[a:b]
-            prefix[step, a:b] = earlier
-            run[a:b] = earlier + drift
+        parts = []
+        for place, pre in enumerate((sides.at[0], here.at[0], sides.at[1])):
+            activated = silu(pre[...] + bias)
+            sums[place] += activated
+            parts.append(activated)
+        store_frames(a3s.at[step], parts)
         return carry
 
     lax.fori_loop(0, 4, one_step, 0)
-    rt[...] = run[...].astype(BF16)
+    store_frames(a3, [sums[place] for place in range(3)])
+    for update, (a, b) in zip(packed_update(a3[...], tp), SPANS):
+        total = update
+        for step in range(4):
+            total = total + noise[step, a:b].astype(F32)
+        rt[a:b] = (0.25 * total).astype(BF16)
+
+
+def first_prefix_kernel(a3s, tp, noise, prefix):
+    prefix[0] = jnp.zeros((ROWS, LANES), F32)
+
+    def one_step(step, carry):
+        for update, (a, b) in zip(packed_update(a3s[step], tp), SPANS):
+            prefix[step + 1, a:b] = prefix[step, a:b] + 0.25 * (update + noise[step, a:b].astype(F32))
+        return carry
+
+    lax.fori_loop(0, 3, one_step, 0)
 
 
 def dup_third(parts):
@@ -255,7 +287,7 @@
     return jnp.concatenate([vector, vector[:, 256:320]], axis=1)
 
 
-def second_sweep_kernel(states, above, below, far, mine, gain_ref, bias_ref, wp, tb, out, taps, scales):
+def second_sweep_kernel(first, states, above, below, far, mine, gain_ref, bias_ref, wp, tb, out, taps, scales):
     gain, bias = wide(gain_ref), wide(bias_ref)
     x = lax.axis_index("x")
     parts = [stats_of(mine, 0), stats_of(above, 384), stats_of(below, 384), stats_of(far, 0)]
@@ -268,7 +300,8 @@
         scales[step, 0:1] = mean[step : step + 1]
         scales[step, 1:2] = rstd[step : step + 1]
 
-    def one_step(step, carry):
+    def one_step(local_step, carry):
+        step = local_step + first
         here = scales[step]
 
         def normed(value, tile):
@@ -293,34 +326,51 @@
             tiles.append(jnp.concatenate([top, middle, bottom], axis=0))
         store_taps(taps, tiles)
         activated = silu(conv_rows(taps, wp) + tb[step][0:1])
-        out[step, 0:256] = activated[:, 0:128].astype(BF16)
-        out[step, 256:512] = activated[:, 128:256].astype(BF16)
-        out[step, 512:640] = pack_tail(activated[:, 256:320]).astype(BF16)
+        out[local_step, 0:256] = activated[:, 0:128].astype(BF16)
+        out[local_step, 256:512] = activated[:, 128:256].astype(BF16)
+        out[local_step, 512:640] = pack_tail(activated[:, 256:320]).astype(BF16)
         return carry
 
-    lax.fori_loop(0, 4, one_step, 0)
-
-
-def second_drift_kernel(own, before, after, tp, noise, rt, prefix, a3, run):
-    run[...] = jnp.zeros_like(run)
+    lax.fori_loop(0, 2, one_step, 0)
+
+
+def store_packed_frames(a3, tiles):
     low = low_lanes(POS)
-
-    def one_step(step, carry):
-        tails = []
-        for place, one in enumerate((before, own, after)):
-            a3[:, place * 256 : place * 256 + 128] = one[step, 0:256]
-            a3[:, place * 256 + 128 : place * 256 + 256] = one[step, 256:512]
-            tails.append(spread_tail(one[step, 512:640].astype(F32)))
-        a3[:, 768:896] = jnp.where(low, tails[0], tails[1]).astype(BF16)
-        a3[:, 896:1024] = jnp.where(low, tails[2], 0.0).astype(BF16)
-        for a, b, drift in drift_of(a3, tp, noise, step):
-            now = run[a:b] + drift
-            prefix[step, a:b] = now
-            run[a:b] = now
-        return carry
-
-    lax.fori_loop(0, 4, one_step, 0)
-    rt[...] = run[...].astype(BF16)
+    tails = []
+    for place, (first, second, tail) in enumerate(tiles):
+        a3[:, place * 256 : place * 256 + 128] = first.astype(BF16)
+        a3[:, place * 256 + 128 : place * 256 + 256] = second.astype(BF16)
+        tails.append(spread_tail(tail))
+    a3[:, 768:896] = jnp.where(low, tails[0], tails[1]).astype(BF16)
+    a3[:, 896:1024] = jnp.where(low, tails[2], 0.0).astype(BF16)
+
+
+def second_total_kernel(own0, own1, before0, before1, after0, after1, tp, noise, rt, a3):
+    tiles = []
+    for pair in ((before0, before1), (own0, own1), (after0, after1)):
+        parts = []
+        for a, b in SPANS:
+            ones = [half[step, a:b].astype(F32) for half in pair for step in range(2)]
+            parts.append((ones[0] + ones[1]) + (ones[2] + ones[3]))
+        tiles.append(parts)
+    store_packed_frames(a3, tiles)
+    for update, (a, b) in zip(packed_update(a3[...], tp), SPANS):
+        total = update
+        for step in range(4):
+            total = total + noise[step, a:b].astype(F32)
+        rt[a:b] = (0.25 * total).astype(BF16)
+
+
+def second_prefix_kernel(own0, own1, before0, before1, after0, after1, tp, noise, prefix, a3):
+    for step in range(4):
+        tiles = []
+        for pair in ((before0, before1), (own0, own1), (after0, after1)):
+            half = pair[step // 2]
+            tiles.append([half[step % 2, a:b].astype(F32) for a, b in SPANS])
+        store_packed_frames(a3, tiles)
+        for update, (a, b) in zip(packed_update(a3[...], tp), SPANS):
+            now = 0.25 * (update + noise[step, a:b].astype(F32))
+            prefix[step, a:b] = now if step == 0 else prefix[step - 1, a:b] + now
 
 
 def result_kernel(sp, prefix, r1, r2, r3, *outs):
@@ -409,49 +459,54 @@
     packed = (ROWS, LANES)
     four = (4, ROWS, LANES)
 
-    *outgoing, start, wp, tp, tew, gain, bias = call(
-        prologue_kernel,
-        [((688, 128), BF16)] * 4
-        + [((1024, 320), BF16), ((3, 1024, 320), BF16), ((1024, 320), BF16), ((320, 320), BF16), ((320,), F32), ((320,), F32)],
-        noise, start, spatial_weight, temporal_weight, temb_weight, gn_gain, gn_bias, emb,
-        scratch=(((1024, 320), BF16),),
-        hbm=7,
-        sems=29,
+    *outgoing, = call(
+        pack_kernel, [((688, 128), BF16)] * 4, noise, emb, scratch=(((4, 256, 320), BF16),), hbm=1, sems=4
     )
     arrived = swap_x(outgoing)
-    nq, sp = call(norm_start_kernel, [((3, 320, 128), BF16), (packed, BF16)], start, gain, bias)
+    nq, sp, wp, tp, tew, gain, bias = call(
+        norm_start_kernel,
+        [((3, 320, 128), BF16), (packed, BF16), ((3, 1024, 320), BF16), ((1024, 320), BF16), ((320, 320), BF16)]
+        + [((320,), F32)] * 2,
+        start, gn_gain, gn_bias, spatial_weight, temporal_weight, temb_weight,
+        scratch=(((1024, 320), BF16),),
+        hbm=6,
+        sems=28,
+    )
     before, after = along_frame(nq, 1), along_frame(nq, -1)
+    taps = ((320, 1024), BF16)
     a3 = ((256, 1024), BF16)
-    taps = ((320, 1024), BF16)
-    run = (packed, F32)
-    rt, prefix, noises, tb = call(
-        first_sweep_kernel,
-        [(packed, BF16), (four, F32), (four, BF16), ((4, 16, 320), F32)],
-        nq, before, after, wp, tp, tew, *arrived,
-        scratch=(taps, ((3, 256, 320), F32), a3, run),
-        flops=2 * 1024 * 320 * 3200,
+    pre = (256, 320)
+    here = call(first_conv_kernel, [((1,) + pre, F32)], nq, wp, scratch=(taps,), flops=512 * 320 * 2880)[0]
+    sides = call(first_conv_kernel, [((2,) + pre, F32)], before, after, wp, scratch=(taps,), flops=1024 * 320 * 2880)[0]
+    rt, noises, tb, a3s = call(
+        first_total_kernel,
+        [(packed, BF16), (four, BF16), ((4, 16, 320), F32), ((4, 256, 1024), BF16)],
+        here, sides, tp, tew, *arrived,
+        scratch=(((3, 256, 320), F32), a3),
+        flops=512 * 320 * 960,
     )
     totals = gather_y(rt)
+    prefix = call(first_prefix_kernel, [(four, F32)], a3s, tp, noises, flops=3 * 512 * 320 * 960)[0]
     states, up, down, far = call(
         states_kernel,
         [(four, BF16), ((464, 128), BF16), ((464, 128), BF16), ((72, 128), BF16)],
         sp, prefix, *totals,
     )
-    activated = call(
-        second_sweep_kernel,
-        [(four, BF16)],
-        states, along_x(up, 1), along_x(down, -1), along_x(far, 2), far, gain, bias, wp, tb,
-        scratch=(taps, ((4, 8, 384), F32)),
-        flops=2 * 1024 * 320 * 2880,
-    )[0]
-    rt, prefix = call(
-        second_drift_kernel,
-        [(packed, BF16), (four, F32)],
-        activated, along_frame(activated, 1), along_frame(activated, -1), tp, noises,
-        scratch=(a3, run),
-        flops=2 * 1024 * 320 * 960,
-    )
+    edges = along_x(up, 1), along_x(down, -1), along_x(far, 2), far
+    halves = []
+    for half in (0, 1):
+        own = call(
+            functools.partial(second_sweep_kernel, 2 * half),
+            [((2, ROWS, LANES), BF16)],
+            states, *edges, gain, bias, wp, tb,
+            scratch=(taps, ((4, 8, 384), F32)),
+            flops=1024 * 320 * 2880,
+        )[0]
+        halves.append((own, along_frame(own, 1), along_frame(own, -1)))
+    parts = [half[i] for i in range(3) for half in halves]
+    rt = call(second_total_kernel, [(packed, BF16)], *parts, tp, noises, scratch=(a3,), flops=512 * 320 * 960)[0]
     totals = gather_y(rt)
+    prefix = call(second_prefix_kernel, [(four, F32)], *parts, tp, noises, scratch=(a3,), flops=2048 * 320 * 960)[0]
     results = call(result_kernel, [(packed, BF16)] * 4, sp, prefix, *totals)
     out = call(unpack_kernel, [((1024, 320), BF16)], *swap_x(results))[0]
     return out.reshape(1, 1, 32, 32, 320)

time: 88.8 us -> 84.8 us (0.955)
  waiting for transfers between devices: 43.4 us -> 34 us
  starting transfers between devices: 25.7 us -> 29 us
  Pallas kernels: 18.6 us -> 20.8 us
    ppermute x19 -> x21, waiting for transfers between devices: 43.4 us -> 34 us  [moved(): return lax.ppermute(value, AXES, pairs)]
    ppermute x19 -> x21, starting transfers between devices: 25.7 us -> 29 us  [moved(): return lax.ppermute(value, AXES, pairs)]
    pallas_call x8 -> x13, Pallas kernels: 18.6 us -> 20.8 us  [call(): pl.pallas_call(body, out_shape=shapes, in_specs=[pl.BlockSpec(memory_spac...]
  transfers between devices with their start and end apart: 19 -> 21, of which waited for: 16 -> 18; matrix products, arithmetic and copies ran while one was open for 0% -> 0% of each run, Pallas kernels for 0% -> 12%
where the time goes in v1:
time: 84.8 us; the launch traced here: 84.7 us
  waiting for transfers between devices  34 us (40%)
  starting transfers between devices  29 us (34%)
  Pallas kernels  20.8 us (25%)
    ppermute x21, waiting for transfers between devices, moved(): return lax.ppermute(value, AXES, pairs)  34 us
    ppermute x21, starting transfers between devices, moved(): return lax.ppermute(value, AXES, pairs)  29 us
    pallas_call x13, Pallas kernels, call(): pl.pallas_call(body, out_shape=shapes, in_specs=[pl.BlockSpec(memory_spac...  20.8 us
  transfers between devices with their start and end apart: 21, of which 18 were waited for; matrix products, arithmetic and copies ran while one was open for 0% of the time, Pallas kernels for 12%

profile of v1, /device:TPU:6, one launch (start us, length us, event | category | flops | bytes accessed | tf_op | source)
XLA Modules:
  0.0 84.7 jit_solution(10660438313502992529)
XLA Ops:
  0.0 2.6 %shard_map.82 = (bf16[3,320,128]{2,1,0:T(8,128)(2,1)S(1)}, bf16[640,128]{1,0:T(8,128)(2,1)S(1)}, bf16[3,1024,320]{2,1,0:T(8,128)(2,1)S(1)}, bf16[1024,320]{1,0:T...) custom-call(bf16[1024,320]{1,0:T(8,128)(2,1)} %bitcast.5, f32[320]{0:T(512)} %gain_hbm.1, ...), custom_call_target="tpu_custom_call" | custom-call | bytes 6558720 | tf_op jit(solution)/shard_map/pallas_call | solution.py:400
  2.6 5.3 %collective-permute-start.1 = (bf16[3,320,128]{2,1,0:T(8,128)(2,1)S(1)}, bf16[3,320,128]{2,1,0:T(8,128)(2,1)S(1)}, u32[]{:S(2)}, u32[]{:S(2)}) collective-permute-start(bf16[3,320,128]{2,1,0:T(8,128)(2,1)S(1)} %get-tuple-element.29.refs_0_), channel_id=1, source_target_pairs={{0,15},{1,0},{2,1},{3,2},{4,3},{5,4},{6,5},{7,6},{8,7},{9,8},{10,9... | collective-permute-start | bytes 737288 | tf_op jit(solution)/shard_map/ppermute | solution.py:419
  7.9 0.0 collective-permute-start
  8.6 0.1 sine_convert_fusion
  8.6 0.1 fusion.2
  8.7 1.4 %shard_map.85 = (bf16[688,128]{1,0:T(8,128)(2,1)S(1)}, bf16[688,128]{1,0:T(8,128)(2,1)S(1)}, bf16[688,128]{1,0:T(8,128)(2,1)S(1)}, bf16[688,128]{1,0:T(8,128)(2,1)S(1)}) custom-call(bf16[1024,320]{1,0:T(8,128)(2,1)} %bitcast.4, bf16[16,384]{1,0:T(8,128)(2,1)S(1)} %broadcast_in_dim.2.emb), custom_call_target="tpu_custom_call" | custom-call | bytes 1372160 | tf_op jit(solution)/shard_map/pallas_call | solution.py:400
  10.1 0.6 collective-permute-start.2
  10.7 2.4 %collective-permute-start.3 = (bf16[688,128]{1,0:T(8,128)(2,1)S(1)}, bf16[688,128]{1,0:T(8,128)(2,1)S(1)}, u32[]{:S(2)}, u32[]{:S(2)}) collective-permute-start(bf16[688,128]{1,0:T(8,128)(2,1)S(1)} %get-tuple-element.35), channel_id=1, source_target_pairs={{0,32},{1,33},{2,34},{3,35},{4,36},{5,37},{6,38},{7,39},{8,40},{9,... | collective-permute-start | bytes 528392 | tf_op jit(solution)/shard_map/ppermute | solution.py:419
  13.1 0.0 collective-permute-start.4
  13.1 1.0 %shard_map.83.here = f32[1,256,320]{2,1,0:T(8,128)S(1)} custom-call(bf16[3,320,128]{2,1,0:T(8,128)(2,1)S(1)} %get-tuple-element.29.refs_0_, bf16[3,1024,320]{2,1,0:T(8,128)(2,1)S(1)} %get-tuple-element.30.refs_1_.refs_2_.wp), custom_call_target="tpu_custom_call" | custom-call | flops 471859200 | bytes 2539520 | tf_op jit(solution)/shard_map/pallas_call | solution.py:400
  14.1 0.0 collective-permute-done.1.refs_1_
  14.1 0.7 collective-permute-done.refs_0_
  14.8 1.8 %shard_map.84.sides = f32[2,256,320]{2,1,0:T(8,128)S(1)} custom-call(bf16[3,320,128]{2,1,0:T(8,128)(2,1)S(1)} %collective-permute-done.refs_0_, bf16[3,320,128]{2,1,0:T(8,128)(2,1)S(1)} %collective-permute-done.1.refs_1_, bf16[3,1024,320]{2,1,0:T(8,128)(2,1)S(1)} %get-tuple-element.30.refs_1_.refs_2_.wp), custom_call_target="tpu_custom_call" | custom-call | flops 943718400 | bytes 3112960 | tf_op jit(solution)/shard_map/pallas_call | solution.py:400
  16.6 0.4 collective-permute-done.2.n1
  17.0 0.6 collective-permute-done.3.n2
  17.6 2.1 %collective-permute-done.4.n3 = bf16[688,128]{1,0:T(8,128)(2,1)S(1)} collective-permute-done((bf16[688,128]{1,0:T(8,128)(2,1)S(1)}, bf16[688,128]{1,0:T(8,128)(2,1)S(1)}, u32[]{:S(2)}, u32[]{:S(2)}) %collective-permute-start.4) | collective-permute-done | bytes 176160 | tf_op jit(solution)/shard_map/ppermute | solution.py:419
  19.8 2.6 %shard_map.86 = (bf16[640,128]{1,0:T(8,128)(2,1)S(1)}, bf16[4,640,128]{2,1,0:T(8,128)(2,1)S(1)}, f32[4,16,320]{2,1,0:T(8,128)S(1)}, bf16[4,256,1024]{2,1,0:T(8,128)(2,1)S(1)}) custom-call(f32[1,256,320]{2,1,0:T(8,128)S(1)} %shard_map.83.here, f32[2,256,320]{2,1,0:T(8,128)S(1)} %shard_map.84.sides, bf16[1024,320]{1,0:T(8,128)(2,1)S(1)} %get-tuple-element.31.tp, ...), custom_call_target="tpu_custom_call" | custom-call | flops 157286400 | bytes 5545984 | tf_op jit(solution)/shard_map/pallas_call | solution.py:400
  22.4 3.1 %collective-permute-start.7 = (bf16[640,128]{1,0:T(8,128)(2,1)S(1)}, bf16[640,128]{1,0:T(8,128)(2,1)S(1)}, u32[]{:S(2)}, u32[]{:S(2)}) collective-permute-start(bf16[640,128]{1,0:T(8,128)(2,1)S(1)} %get-tuple-element.39), channel_id=1, source_target_pairs={{0,192},{1,65},{2,194},{3,67},{4,196},{5,69},{6,198},{7,71},{8,200... | collective-permute-start | bytes 491528 | tf_op jit(solution)/shard_map/ppermute | solution.py:419
  25.5 0.6 collective-permute-start.6
  26.1 1.0 %collective-permute-start.5 = (bf16[640,128]{1,0:T(8,128)(2,1)S(1)}, bf16[640,128]{1,0:T(8,128)(2,1)S(1)}, u32[]{:S(2)}, u32[]{:S(2)}) collective-permute-start(bf16[640,128]{1,0:T(8,128)(2,1)S(1)} %get-tuple-element.39), channel_id=1, source_target_pairs={{0,64},{1,193},{2,66},{3,195},{4,68},{5,197},{6,70},{7,199},{8,72}... | collective-permute-start | bytes 491528 | tf_op jit(solution)/shard_map/ppermute | solution.py:419
  27.1 1.5 %shard_map.87.prefix = f32[4,640,128]{2,1,0:T(8,128)S(1)} custom-call(bf16[4,256,1024]{2,1,0:T(8,128)(2,1)S(1)} %get-tuple-element.37.a3s, bf16[1024,320]{1,0:T(8,128)(2,1)S(1)} %get-tuple-element.31.tp, bf16[4,640,128]{2,1,0:T(8,128)(2,1)S(1)} %get-tuple-element.38.noise), custom_call_target="tpu_custom_call" | custom-call | flops 471859200 | bytes 4718592 | tf_op jit(solution)/shard_map/pallas_call | solution.py:400
  28.6 0.7 collective-permute-done.7.r3
  29.3 3.1 %collective-permute-done.6.r2 = bf16[640,128]{1,0:T(8,128)(2,1)S(1)} collective-permute-done((bf16[640,128]{1,0:T(8,128)(2,1)S(1)}, bf16[640,128]{1,0:T(8,128)(2,1)S(1)}, u32[]{:S(2)}, u32[]{:S(2)}) %collective-permute-start.6) | collective-permute-done | bytes 163872 | tf_op jit(solution)/shard_map/ppermute | solution.py:419
  32.4 1.7 %collective-permute-done.5.r1 = bf16[640,128]{1,0:T(8,128)(2,1)S(1)} collective-permute-done((bf16[640,128]{1,0:T(8,128)(2,1)S(1)}, bf16[640,128]{1,0:T(8,128)(2,1)S(1)}, u32[]{:S(2)}, u32[]{:S(2)}) %collective-permute-start.5) | collective-permute-done | bytes 163872 | tf_op jit(solution)/shard_map/ppermute | solution.py:419
  34.1 1.4 %shard_map.88 = (bf16[4,640,128]{2,1,0:T(8,128)(2,1)S(1)}, bf16[464,128]{1,0:T(8,128)(2,1)S(1)}, bf16[464,128]{1,0:T(8,128)(2,1)S(1)}, bf16[72,128]{1,0:T(8,128)(2,1)S(1)}) custom-call(bf16[640,128]{1,0:T(8,128)(2,1)S(1)} %get-tuple-element.28.sp, f32[4,640,128]{2,1,0:T(8,128)S(1)} %shard_map.87.prefix, bf16[640,128]{1,0:T(8,128)(2,1)S(1)} %collective-permute-done.5.r1, ...), custom_call_target="tpu_custom_call" | custom-call | bytes 2877440 | tf_op jit(solution)/shard_map/pallas_call | solution.py:400
  35.5 2.1 %collective-permute-start.8 = (bf16[464,128]{1,0:T(8,128)(2,1)S(1)}, bf16[464,128]{1,0:T(8,128)(2,1)S(1)}, u32[]{:S(2)}, u32[]{:S(2)}) collective-permute-start(bf16[464,128]{1,0:T(8,128)(2,1)S(1)} %get-tuple-element.41), channel_id=1, source_target_pairs={{0,16},{1,17},{2,18},{3,19},{4,20},{5,21},{6,22},{7,23},{8,24},{9,... | collective-permute-start | bytes 356360 | tf_op jit(solution)/shard_map/ppermute | solution.py:419
  37.5 0.2 collective-permute-start.9
  37.8 1.8 %collective-permute-start.10 = (bf16[72,128]{1,0:T(8,128)(2,1)S(1)}, bf16[72,128]{1,0:T(8,128)(2,1)S(1)}, u32[]{:S(2)}, u32[]{:S(2)}) collective-permute-start(bf16[72,128]{1,0:T(8,128)(2,1)S(1)} %get-tuple-element.43.mine), channel_id=1, source_target_pairs={{0,32},{1,33},{2,34},{3,35},{4,36},{5,37},{6,38},{7,39},{8,40},{9,... | collective-permute-start | bytes 55304 | tf_op jit(solution)/shard_map/ppermute | solution.py:419
  39.5 3.6 %collective-permute-done.10.far = bf16[72,128]{1,0:T(8,128)(2,1)S(1)} collective-permute-done((bf16[72,128]{1,0:T(8,128)(2,1)S(1)}, bf16[72,128]{1,0:T(8,128)(2,1)S(1)}, u32[]{:S(2)}, u32[]{:S(2)}) %collective-permute-start.10) | collective-permute-done | bytes 18464 | tf_op jit(solution)/shard_map/ppermute | solution.py:419
  43.1 0.0 collective-permute-done.8.above
  43.1 0.6 collective-permute-done.9.below
  43.8 2.5 %shard_map.89.own0 = bf16[2,640,128]{2,1,0:T(8,128)(2,1)S(1)} custom-call(bf16[4,640,128]{2,1,0:T(8,128)(2,1)S(1)} %get-tuple-element.40.states, bf16[464,128]{1,0:T(8,128)(2,1)S(1)} %collective-permute-done.8.above, bf16[464,128]{1,0:T(8,128)(2,1)S(1)} %collective-permute-done.9.below, bf16[72,128]{1,0:T(8,128)(2,1)S(1)} %collective-permute-done.10.far, ...), custom_call_target="tpu_custom_call" | custom-call | flops 943718400 | bytes 3308032 | tf_op jit(solution)/shard_map/pallas_call | solution.py:400
  46.3 1.3 %collective-permute-start.13 = (bf16[2,640,128]{2,1,0:T(8,128)(2,1)S(1)}, bf16[2,640,128]{2,1,0:T(8,128)(2,1)S(1)}, u32[]{:S(2)}, u32[]{:S(2)}) collective-permute-start(bf16[2,640,128]{2,1,0:T(8,128)(2,1)S(1)} %shard_map.89.own0), channel_id=1, source_target_pairs={{0,15},{1,0},{2,1},{3,2},{4,3},{5,4},{6,5},{7,6},{8,7},{9,8},{10,9... | collective-permute-start | bytes 983048 | tf_op jit(solution)/shard_map/ppermute | solution.py:419
  47.6 0.0 collective-permute-start.11
  47.6 2.5 %shard_map.90.own1 = bf16[2,640,128]{2,1,0:T(8,128)(2,1)S(1)} custom-call(bf16[4,640,128]{2,1,0:T(8,128)(2,1)S(1)} %get-tuple-element.40.states, bf16[464,128]{1,0:T(8,128)(2,1)S(1)} %collective-permute-done.8.above, bf16[464,128]{1,0:T(8,128)(2,1)S(1)} %collective-permute-done.9.below, bf16[72,128]{1,0:T(8,128)(2,1)S(1)} %collective-permute-done.10.far, ...), custom_call_target="tpu_custom_call" | custom-call | flops 943718400 | bytes 3308032 | tf_op jit(solution)/shard_map/pallas_call | solution.py:400
  50.1 3.0 %collective-permute-start.14 = (bf16[2,640,128]{2,1,0:T(8,128)(2,1)S(1)}, bf16[2,640,128]{2,1,0:T(8,128)(2,1)S(1)}, u32[]{:S(2)}, u32[]{:S(2)}) collective-permute-start(bf16[2,640,128]{2,1,0:T(8,128)(2,1)S(1)} %shard_map.90.own1), channel_id=1, source_target_pairs={{0,15},{1,0},{2,1},{3,2},{4,3},{5,4},{6,5},{7,6},{8,7},{9,8},{10,9... | collective-permute-start | bytes 983048 | tf_op jit(solution)/shard_map/ppermute | solution.py:419
  53.1 0.0 collective-permute-start.12
  53.1 0.0 collective-permute-done.13.after0
  53.1 2.2 %collective-permute-done.11.before0 = bf16[2,640,128]{2,1,0:T(8,128)(2,1)S(1)} collective-permute-done((bf16[2,640,128]{2,1,0:T(8,128)(2,1)S(1)}, bf16[2,640,128]{2,1,0:T(8,128)(2,1)S(1)}, u32[]{:S(2)}, u32[]{:S(2)}) %collective-permute-start.11) | collective-permute-done | bytes 327712 | tf_op jit(solution)/shard_map/ppermute | solution.py:419
  55.3 2.4 %collective-permute-done.14.after1 = bf16[2,640,128]{2,1,0:T(8,128)(2,1)S(1)} collective-permute-done((bf16[2,640,128]{2,1,0:T(8,128)(2,1)S(1)}, bf16[2,640,128]{2,1,0:T(8,128)(2,1)S(1)}, u32[]{:S(2)}, u32[]{:S(2)}) %collective-permute-start.14) | collective-permute-done | bytes 327712 | tf_op jit(solution)/shard_map/ppermute | solution.py:419
  57.7 3.1 %collective-permute-done.12.before1 = bf16[2,640,128]{2,1,0:T(8,128)(2,1)S(1)} collective-permute-done((bf16[2,640,128]{2,1,0:T(8,128)(2,1)S(1)}, bf16[2,640,128]{2,1,0:T(8,128)(2,1)S(1)}, u32[]{:S(2)}, u32[]{:S(2)}) %collective-permute-start.12) | collective-permute-done | bytes 327712 | tf_op jit(solution)/shard_map/ppermute | solution.py:419
  60.8 0.7 shard_map.92
  61.5 3.3 %collective-permute-start.17 = (bf16[640,128]{1,0:T(8,128)(2,1)S(1)}, bf16[640,128]{1,0:T(8,128)(2,1)S(1)}, u32[]{:S(2)}, u32[]{:S(2)}) collective-permute-start(bf16[640,128]{1,0:T(8,128)(2,1)S(1)} %shard_map.92), channel_id=1, source_target_pairs={{0,192},{1,65},{2,194},{3,67},{4,196},{5,69},{6,198},{7,71},{8,200... | collective-permute-start | bytes 491528 | tf_op jit(solution)/shard_map/ppermute | solution.py:419
  64.8 0.2 collective-permute-start.16
  65.0 0.8 collective-permute-start.15
  65.8 1.5 %shard_map.91.prefix = f32[4,640,128]{2,1,0:T(8,128)S(1)} custom-call(bf16[2,640,128]{2,1,0:T(8,128)(2,1)S(1)} %shard_map.89.own0, bf16[2,640,128]{2,1,0:T(8,128)(2,1)S(1)} %shard_map.90.own1, bf16[2,640,128]{2,1,0:T(8,128)(2,1)S(1)} %collective-permute-done.11.before0, bf16[2,640,128]{2,1,0:T(8,128)(2,1)S(1)} %collective-permute-done.12.before1, ...), custom_call_target="tpu_custom_call" | custom-call | flops 629145600 | bytes 4587520 | tf_op jit(solution)/shard_map/pallas_call | solution.py:400
  67.3 2.1 %collective-permute-done.17.r3 = bf16[640,128]{1,0:T(8,128)(2,1)S(1)} collective-permute-done((bf16[640,128]{1,0:T(8,128)(2,1)S(1)}, bf16[640,128]{1,0:T(8,128)(2,1)S(1)}, u32[]{:S(2)}, u32[]{:S(2)}) %collective-permute-start.17) | collective-permute-done | bytes 163872 | tf_op jit(solution)/shard_map/ppermute | solution.py:419
  69.4 2.3 %collective-permute-done.16.r2 = bf16[640,128]{1,0:T(8,128)(2,1)S(1)} collective-permute-done((bf16[640,128]{1,0:T(8,128)(2,1)S(1)}, bf16[640,128]{1,0:T(8,128)(2,1)S(1)}, u32[]{:S(2)}, u32[]{:S(2)}) %collective-permute-start.16) | collective-permute-done | bytes 163872 | tf_op jit(solution)/shard_map/ppermute | solution.py:419
  71.7 1.6 %collective-permute-done.15.r1 = bf16[640,128]{1,0:T(8,128)(2,1)S(1)} collective-permute-done((bf16[640,128]{1,0:T(8,128)(2,1)S(1)}, bf16[640,128]{1,0:T(8,128)(2,1)S(1)}, u32[]{:S(2)}, u32[]{:S(2)}) %collective-permute-start.15) | collective-permute-done | bytes 163872 | tf_op jit(solution)/shard_map/ppermute | solution.py:419
  73.3 0.2 shard_map.93
  73.5 1.6 %collective-permute-start.18 = (bf16[640,128]{1,0:T(8,128)(2,1)S(1)}, bf16[640,128]{1,0:T(8,128)(2,1)S(1)}, u32[]{:S(2)}, u32[]{:S(2)}) collective-permute-start(bf16[640,128]{1,0:T(8,128)(2,1)S(1)} %get-tuple-element.48), channel_id=1, source_target_pairs={{0,16},{1,49},{2,18},{3,51},{4,20},{5,53},{6,22},{7,55},{8,24},{9,... | collective-permute-start | bytes 491528 | tf_op jit(solution)/shard_map/ppermute | solution.py:419
  75.1 0.8 collective-permute-start.19
  75.9 1.0 %collective-permute-start.20 = (bf16[640,128]{1,0:T(8,128)(2,1)S(1)}, bf16[640,128]{1,0:T(8,128)(2,1)S(1)}, u32[]{:S(2)}, u32[]{:S(2)}) collective-permute-start(bf16[640,128]{1,0:T(8,128)(2,1)S(1)} %get-tuple-element.50), channel_id=1, source_target_pairs={{0,48},{1,17},{2,50},{3,19},{4,52},{5,21},{6,54},{7,23},{8,56},{9,... | collective-permute-start | bytes 491528 | tf_op jit(solution)/shard_map/ppermute | solution.py:419
  76.8 2.1 %collective-permute-done.18.r1 = bf16[640,128]{1,0:T(8,128)(2,1)S(1)} collective-permute-done((bf16[640,128]{1,0:T(8,128)(2,1)S(1)}, bf16[640,128]{1,0:T(8,128)(2,1)S(1)}, u32[]{:S(2)}, u32[]{:S(2)}) %collective-permute-start.18) | collective-permute-done | bytes 163872 | tf_op jit(solution)/shard_map/ppermute | solution.py:419
  78.9 3.1 %collective-permute-done.19.r2 = bf16[640,128]{1,0:T(8,128)(2,1)S(1)} collective-permute-done((bf16[640,128]{1,0:T(8,128)(2,1)S(1)}, bf16[640,128]{1,0:T(8,128)(2,1)S(1)}, u32[]{:S(2)}, u32[]{:S(2)}) %collective-permute-start.19) | collective-permute-done | bytes 163872 | tf_op jit(solution)/shard_map/ppermute | solution.py:419
  82.0 1.7 %collective-permute-done.20.r3 = bf16[640,128]{1,0:T(8,128)(2,1)S(1)} collective-permute-done((bf16[640,128]{1,0:T(8,128)(2,1)S(1)}, bf16[640,128]{1,0:T(8,128)(2,1)S(1)}, u32[]{:S(2)}, u32[]{:S(2)}) %collective-permute-start.20) | collective-permute-done | bytes 163872 | tf_op jit(solution)/shard_map/ppermute | solution.py:419
  83.7 1.0 %shard_map.94 = bf16[1024,320]{1,0:T(8,128)(2,1)} custom-call(bf16[640,128]{1,0:T(8,128)(2,1)S(1)} %get-tuple-element.47.r0, bf16[640,128]{1,0:T(8,128)(2,1)S(1)} %collective-permute-done.18.r1, bf16[640,128]{1,0:T(8,128)(2,1)S(1)} %collective-permute-done.19.r2, bf16[640,128]{1,0:T(8,128)(2,1)S(1)} %collective-permute-done.20.r3), custom_call_target="tpu_custom_call" | custom-call | bytes 1310720 | tf_op jit(solution)/shard_map/pallas_call | solution.py:400
  (1 shorter events, 0.0 us)
Async XLA Ops:
  2.6 11.5 %collective-permute-start.1 = (bf16[3,320,128]{2,1,0:T(8,128)(2,1)S(1)}, bf16[3,320,128]{2,1,0:T(8,128)(2,1)S(1)}, u32[]{:S(2)}, u32[]{:S(2)}) collective-permute-start(bf16[3,320,128]{2,1,0:T(8,128)(2,1)S(1)} %get-tuple-element.29.refs_0_), channel_id=1, source_target_pairs={{0,15},{1,0},{2,1},{3,2},{4,3},{5,4},{6,5},{7,6},{8,7},{9,8},{10,9... | collective-permute-start | bytes 737288 | tf_op jit(solution)/shard_map/ppermute | solution.py:419
  7.9 6.8 %collective-permute-start = (bf16[3,320,128]{2,1,0:T(8,128)(2,1)S(1)}, bf16[3,320,128]{2,1,0:T(8,128)(2,1)S(1)}, u32[]{:S(2)}, u32[]{:S(2)}) collective-permute-start(bf16[3,320,128]{2,1,0:T(8,128)(2,1)S(1)} %get-tuple-element.29.refs_0_), channel_id=1, source_target_pairs={{0,1},{1,2},{2,3},{3,4},{4,5},{5,6},{6,7},{7,8},{8,9},{9,10},{10,1... | collective-permute-start | bytes 737288 | tf_op jit(solution)/shard_map/ppermute | solution.py:419
  10.1 6.9 %collective-permute-start.2 = (bf16[688,128]{1,0:T(8,128)(2,1)S(1)}, bf16[688,128]{1,0:T(8,128)(2,1)S(1)}, u32[]{:S(2)}, u32[]{:S(2)}) collective-permute-start(bf16[688,128]{1,0:T(8,128)(2,1)S(1)} %get-tuple-element.34), channel_id=1, source_target_pairs={{0,16},{1,49},{2,18},{3,51},{4,20},{5,53},{6,22},{7,55},{8,24},{9,... | collective-permute-start | bytes 528392 | tf_op jit(solution)/shard_map/ppermute | solution.py:419
  10.7 7.0 %collective-permute-start.3 = (bf16[688,128]{1,0:T(8,128)(2,1)S(1)}, bf16[688,128]{1,0:T(8,128)(2,1)S(1)}, u32[]{:S(2)}, u32[]{:S(2)}) collective-permute-start(bf16[688,128]{1,0:T(8,128)(2,1)S(1)} %get-tuple-element.35), channel_id=1, source_target_pairs={{0,32},{1,33},{2,34},{3,35},{4,36},{5,37},{6,38},{7,39},{8,40},{9,... | collective-permute-start | bytes 528392 | tf_op jit(solution)/shard_map/ppermute | solution.py:419
  13.1 6.7 %collective-permute-start.4 = (bf16[688,128]{1,0:T(8,128)(2,1)S(1)}, bf16[688,128]{1,0:T(8,128)(2,1)S(1)}, u32[]{:S(2)}, u32[]{:S(2)}) collective-permute-start(bf16[688,128]{1,0:T(8,128)(2,1)S(1)} %get-tuple-element.36), channel_id=1, source_target_pairs={{0,48},{1,17},{2,50},{3,19},{4,52},{5,21},{6,54},{7,23},{8,56},{9,... | collective-permute-start | bytes 528392 | tf_op jit(solution)/shard_map/ppermute | solution.py:419
  22.4 6.9 %collective-permute-start.7 = (bf16[640,128]{1,0:T(8,128)(2,1)S(1)}, bf16[640,128]{1,0:T(8,128)(2,1)S(1)}, u32[]{:S(2)}, u32[]{:S(2)}) collective-permute-start(bf16[640,128]{1,0:T(8,128)(2,1)S(1)} %get-tuple-element.39), channel_id=1, source_target_pairs={{0,192},{1,65},{2,194},{3,67},{4,196},{5,69},{6,198},{7,71},{8,200... | collective-permute-start | bytes 491528 | tf_op jit(solution)/shard_map/ppermute | solution.py:419
  25.5 6.9 %collective-permute-start.6 = (bf16[640,128]{1,0:T(8,128)(2,1)S(1)}, bf16[640,128]{1,0:T(8,128)(2,1)S(1)}, u32[]{:S(2)}, u32[]{:S(2)}) collective-permute-start(bf16[640,128]{1,0:T(8,128)(2,1)S(1)} %get-tuple-element.39), channel_id=1, source_target_pairs={{0,128},{1,129},{2,130},{3,131},{4,132},{5,133},{6,134},{7,135},{8... | collective-permute-start | bytes 491528 | tf_op jit(solution)/shard_map/ppermute | solution.py:419
  26.1 7.9 %collective-permute-start.5 = (bf16[640,128]{1,0:T(8,128)(2,1)S(1)}, bf16[640,128]{1,0:T(8,128)(2,1)S(1)}, u32[]{:S(2)}, u32[]{:S(2)}) collective-permute-start(bf16[640,128]{1,0:T(8,128)(2,1)S(1)} %get-tuple-element.39), channel_id=1, source_target_pairs={{0,64},{1,193},{2,66},{3,195},{4,68},{5,197},{6,70},{7,199},{8,72}... | collective-permute-start | bytes 491528 | tf_op jit(solution)/shard_map/ppermute | solution.py:419
  35.5 7.7 %collective-permute-start.8 = (bf16[464,128]{1,0:T(8,128)(2,1)S(1)}, bf16[464,128]{1,0:T(8,128)(2,1)S(1)}, u32[]{:S(2)}, u32[]{:S(2)}) collective-permute-start(bf16[464,128]{1,0:T(8,128)(2,1)S(1)} %get-tuple-element.41), channel_id=1, source_target_pairs={{0,16},{1,17},{2,18},{3,19},{4,20},{5,21},{6,22},{7,23},{8,24},{9,... | collective-permute-start | bytes 356360 | tf_op jit(solution)/shard_map/ppermute | solution.py:419
  37.5 6.2 %collective-permute-start.9 = (bf16[464,128]{1,0:T(8,128)(2,1)S(1)}, bf16[464,128]{1,0:T(8,128)(2,1)S(1)}, u32[]{:S(2)}, u32[]{:S(2)}) collective-permute-start(bf16[464,128]{1,0:T(8,128)(2,1)S(1)} %get-tuple-element.42), channel_id=1, source_target_pairs={{0,48},{1,49},{2,50},{3,51},{4,52},{5,53},{6,54},{7,55},{8,56},{9,... | collective-permute-start | bytes 356360 | tf_op jit(solution)/shard_map/ppermute | solution.py:419
  37.8 5.4 %collective-permute-start.10 = (bf16[72,128]{1,0:T(8,128)(2,1)S(1)}, bf16[72,128]{1,0:T(8,128)(2,1)S(1)}, u32[]{:S(2)}, u32[]{:S(2)}) collective-permute-start(bf16[72,128]{1,0:T(8,128)(2,1)S(1)} %get-tuple-element.43.mine), channel_id=1, source_target_pairs={{0,32},{1,33},{2,34},{3,35},{4,36},{5,37},{6,38},{7,39},{8,40},{9,... | collective-permute-start | bytes 55304 | tf_op jit(solution)/shard_map/ppermute | solution.py:419
  46.3 6.8 %collective-permute-start.13 = (bf16[2,640,128]{2,1,0:T(8,128)(2,1)S(1)}, bf16[2,640,128]{2,1,0:T(8,128)(2,1)S(1)}, u32[]{:S(2)}, u32[]{:S(2)}) collective-permute-start(bf16[2,640,128]{2,1,0:T(8,128)(2,1)S(1)} %shard_map.89.own0), channel_id=1, source_target_pairs={{0,15},{1,0},{2,1},{3,2},{4,3},{5,4},{6,5},{7,6},{8,7},{9,8},{10,9... | collective-permute-start | bytes 983048 | tf_op jit(solution)/shard_map/ppermute | solution.py:419
  47.6 7.7 %collective-permute-start.11 = (bf16[2,640,128]{2,1,0:T(8,128)(2,1)S(1)}, bf16[2,640,128]{2,1,0:T(8,128)(2,1)S(1)}, u32[]{:S(2)}, u32[]{:S(2)}) collective-permute-start(bf16[2,640,128]{2,1,0:T(8,128)(2,1)S(1)} %shard_map.89.own0), channel_id=1, source_target_pairs={{0,1},{1,2},{2,3},{3,4},{4,5},{5,6},{6,7},{7,8},{8,9},{9,10},{10,1... | collective-permute-start | bytes 983048 | tf_op jit(solution)/shard_map/ppermute | solution.py:419
  50.1 7.6 %collective-permute-start.14 = (bf16[2,640,128]{2,1,0:T(8,128)(2,1)S(1)}, bf16[2,640,128]{2,1,0:T(8,128)(2,1)S(1)}, u32[]{:S(2)}, u32[]{:S(2)}) collective-permute-start(bf16[2,640,128]{2,1,0:T(8,128)(2,1)S(1)} %shard_map.90.own1), channel_id=1, source_target_pairs={{0,15},{1,0},{2,1},{3,2},{4,3},{5,4},{6,5},{7,6},{8,7},{9,8},{10,9... | collective-permute-start | bytes 983048 | tf_op jit(solution)/shard_map/ppermute | solution.py:419
  53.1 7.7 %collective-permute-start.12 = (bf16[2,640,128]{2,1,0:T(8,128)(2,1)S(1)}, bf16[2,640,128]{2,1,0:T(8,128)(2,1)S(1)}, u32[]{:S(2)}, u32[]{:S(2)}) collective-permute-start(bf16[2,640,128]{2,1,0:T(8,128)(2,1)S(1)} %shard_map.90.own1), channel_id=1, source_target_pairs={{0,1},{1,2},{2,3},{3,4},{4,5},{5,6},{6,7},{7,8},{8,9},{9,10},{10,1... | collective-permute-start | bytes 983048 | tf_op jit(solution)/shard_map/ppermute | solution.py:419
  61.5 7.9 %collective-permute-start.17 = (bf16[640,128]{1,0:T(8,128)(2,1)S(1)}, bf16[640,128]{1,0:T(8,128)(2,1)S(1)}, u32[]{:S(2)}, u32[]{:S(2)}) collective-permute-start(bf16[640,128]{1,0:T(8,128)(2,1)S(1)} %shard_map.92), channel_id=1, source_target_pairs={{0,192},{1,65},{2,194},{3,67},{4,196},{5,69},{6,198},{7,71},{8,200... | collective-permute-start | bytes 491528 | tf_op jit(solution)/shard_map/ppermute | solution.py:419
  64.8 6.9 %collective-permute-start.16 = (bf16[640,128]{1,0:T(8,128)(2,1)S(1)}, bf16[640,128]{1,0:T(8,128)(2,1)S(1)}, u32[]{:S(2)}, u32[]{:S(2)}) collective-permute-start(bf16[640,128]{1,0:T(8,128)(2,1)S(1)} %shard_map.92), channel_id=1, source_target_pairs={{0,128},{1,129},{2,130},{3,131},{4,132},{5,133},{6,134},{7,135},{8... | collective-permute-start | bytes 491528 | tf_op jit(solution)/shard_map/ppermute | solution.py:419
  65.0 8.3 %collective-permute-start.15 = (bf16[640,128]{1,0:T(8,128)(2,1)S(1)}, bf16[640,128]{1,0:T(8,128)(2,1)S(1)}, u32[]{:S(2)}, u32[]{:S(2)}) collective-permute-start(bf16[640,128]{1,0:T(8,128)(2,1)S(1)} %shard_map.92), channel_id=1, source_target_pairs={{0,64},{1,193},{2,66},{3,195},{4,68},{5,197},{6,70},{7,199},{8,72}... | collective-permute-start | bytes 491528 | tf_op jit(solution)/shard_map/ppermute | solution.py:419
  73.5 5.4 %collective-permute-start.18 = (bf16[640,128]{1,0:T(8,128)(2,1)S(1)}, bf16[640,128]{1,0:T(8,128)(2,1)S(1)}, u32[]{:S(2)}, u32[]{:S(2)}) collective-permute-start(bf16[640,128]{1,0:T(8,128)(2,1)S(1)} %get-tuple-element.48), channel_id=1, source_target_pairs={{0,16},{1,49},{2,18},{3,51},{4,20},{5,53},{6,22},{7,55},{8,24},{9,... | collective-permute-start | bytes 491528 | tf_op jit(solution)/shard_map/ppermute | solution.py:419
  75.1 6.9 %collective-permute-start.19 = (bf16[640,128]{1,0:T(8,128)(2,1)S(1)}, bf16[640,128]{1,0:T(8,128)(2,1)S(1)}, u32[]{:S(2)}, u32[]{:S(2)}) collective-permute-start(bf16[640,128]{1,0:T(8,128)(2,1)S(1)} %get-tuple-element.49), channel_id=1, source_target_pairs={{0,32},{1,33},{2,34},{3,35},{4,36},{5,37},{6,38},{7,39},{8,40},{9,... | collective-permute-start | bytes 491528 | tf_op jit(solution)/shard_map/ppermute | solution.py:419
  75.9 7.8 %collective-permute-start.20 = (bf16[640,128]{1,0:T(8,128)(2,1)S(1)}, bf16[640,128]{1,0:T(8,128)(2,1)S(1)}, u32[]{:S(2)}, u32[]{:S(2)}) collective-permute-start(bf16[640,128]{1,0:T(8,128)(2,1)S(1)} %get-tuple-element.50), channel_id=1, source_target_pairs={{0,48},{1,17},{2,50},{3,19},{4,52},{5,21},{6,54},{7,23},{8,56},{9,... | collective-permute-start | bytes 491528 | tf_op jit(solution)/shard_map/ppermute | solution.py:419

commit v2 on v1

--- a/solution.py
+++ b/solution.py
@@ -30,15 +30,12 @@
 
 
 def pack_tail(tail):
-    return jnp.concatenate([tail[:128], tail[128:]], axis=1)
-
-
-def twice(tail):
-    return jnp.concatenate([tail, tail], axis=1)
+    half = tail.shape[0] // 2
+    return jnp.concatenate([tail[:half], tail[half:]], axis=1)
 
 
 def spread_tail(tile):
-    low, other = low_lanes(128), swapped(tile)
+    low, other = low_lanes(tile.shape[0]), swapped(tile)
     return jnp.concatenate([jnp.where(low, tile, other), jnp.where(low, other, tile)], axis=0)
 
 
@@ -82,14 +79,20 @@
     return jnp.where(lax.axis_index("core") == 0, slot, (4 - slot) % 4)
 
 
-def pack_kernel(noise_hbm, emb, o0, o1, o2, o3, noise, sems):
+def pack_kernel(noise_hbm, start_hbm, gain_hbm, bias_hbm, emb, o0, o1, o2, o3, start, gain, bias, noise, sems):
     x = lax.axis_index("x")
     outs = {0: o0, 1: o1, 2: o2, 3: o3}
     copies = {}
-    for slot in (1, 3, 2, 0):
+    for slot in (2, 1, 3, 0):
         at = pl.multiple_of(lax.rem(x + hop_of(slot), 4) * POS, POS)
         copies[slot] = pltpu.make_async_copy(noise_hbm.at[pl.ds(at, POS)], noise.at[slot], sems.at[slot])
         copies[slot].start()
+    rest = [
+        pltpu.make_async_copy(source, target, sems.at[4 + i])
+        for i, (source, target) in enumerate(((start_hbm, start), (gain_hbm, gain), (bias_hbm, bias)))
+    ]
+    for copy in rest:
+        copy.start()
     for slot, copy in copies.items():
         out = outs[slot]
         copy.wait()
@@ -98,14 +101,14 @@
         out[512:640] = pack_tail(noise[slot, :, 256:320].astype(F32)).astype(BF16)
         for tile in range(3):
             out[640 + 16 * tile : 656 + 16 * tile] = emb[:, tile * 128 : tile * 128 + 128]
-
-
-def norm_start_kernel(
-    start_hbm, gain_hbm, bias_hbm, sw, tw, tew_hbm, nq, sp, wp, tp, tew, gain_ref, bias_ref, start, sems
-):
+    for copy in rest:
+        copy.wait()
+
+
+def norm_start_kernel(sw, tw, tew_hbm, start, gain_ref, bias_ref, nq, sp, wp, tp, tew, sems):
     x = lax.axis_index("x")
     frame = lax.axis_index("z") * 2 + lax.axis_index("core")
-    moves = [(start_hbm, start), (gain_hbm, gain_ref), (bias_hbm, bias_ref)]
+    moves = []
     for row in range(4):
         out = tp if row == 3 else wp.at[row]
         for place in range(3):
@@ -120,8 +123,6 @@
     for row in range(3):
         wp[row, 960:1024] = jnp.zeros((64, 320), BF16)
     tp[960:1024] = jnp.zeros((64, 320), BF16)
-    for copy in copies[:3]:
-        copy.wait()
     values = start[...].astype(F32)
     mean = group_sum(jnp.broadcast_to(jnp.sum(values, axis=0, keepdims=True), (8, 320)), members)[0:1] * (1.0 / 10240)
     centered = start[...].astype(F32) - mean
@@ -132,22 +133,19 @@
     first = pl.multiple_of(x * POS, POS)
     above = pl.multiple_of(jnp.maximum(x * POS - 32, 0), 32)
     below = pl.multiple_of(jnp.minimum(x * POS + POS, 992), 32)
-    for at, size, rows, kept in (
-        (above, 32, 0, x > 0),
-        (first, POS, 32, None),
-        (below, 32, 288, x < 3),
-    ):
+    pieces = []
+    for at, size, kept in ((above, 32, x > 0), (first, POS, None), (below, 32, x < 3)):
         block = start[pl.ds(at, size), :].astype(F32)
         normed = silu((block - mean) * scale * gain + bias)
-        if kept is not None:
-            normed = jnp.where(kept, normed, 0.0)
-        nq[0, rows : rows + size] = normed[:, 0:128].astype(BF16)
-        nq[1, rows : rows + size] = normed[:, 128:256].astype(BF16)
-        nq[2, rows : rows + size] = twice(normed[:, 256:320]).astype(BF16)
+        pieces.append(normed if kept is None else jnp.where(kept, normed, 0.0))
+    normed = jnp.concatenate(pieces, axis=0)
+    nq[0:320] = normed[:, 0:128].astype(BF16)
+    nq[320:640] = normed[:, 128:256].astype(BF16)
+    nq[640:800] = pack_tail(normed[:, 256:320]).astype(BF16)
     sp[0:256] = start[pl.ds(first, POS), 0:128]
     sp[256:512] = start[pl.ds(first, POS), 128:256]
     sp[512:640] = pack_tail(start[pl.ds(first, POS), 256:320].astype(F32)).astype(BF16)
-    for copy in copies[3:]:
+    for copy in copies:
         copy.wait()
     for place, missing in ((0, frame == 0), (2, frame == 15)):
 
@@ -160,7 +158,7 @@
 def first_conv_kernel(*refs):
     *normed, wp, pre, taps = refs
     for place, one in enumerate(normed):
-        store_taps(taps, [one[i].astype(F32) for i in range(3)])
+        store_taps(taps, [one[0:320].astype(F32), one[320:640].astype(F32), spread_tail(one[640:800].astype(F32))])
         pre[place] = conv_rows(taps, wp)
 
 
@@ -182,15 +180,17 @@
 
 def first_total_kernel(here, sides, tp, tew, n0, n1, n2, n3, rt, noise, tb, a3s, sums, a3):
     x = lax.axis_index("x")
-    for slot, one in enumerate((n0, n1, n2, n3)):
+    arrived = (n0, n1, n2, n3)
+    bias = None
+    for at, rows in ((640, slice(0, 128)), (656, slice(128, 256)), (672, slice(256, 320))):
+        emb = jnp.concatenate([one[at : at + 16, 0 : rows.stop - rows.start] for one in arrived], axis=0)
+        term = jnp.dot(emb, tew[rows], preferred_element_type=F32)
+        bias = term if bias is None else bias + term
+    bias = bias / (1.0 + jnp.exp(-bias))
+    for slot, one in enumerate(arrived):
         step = lax.rem(x + 4 - hop_of(slot), 4)
         noise[step] = one[0:640]
-        bias = (
-            jnp.dot(one[640:656], tew[0:128], preferred_element_type=F32)
-            + jnp.dot(one[656:672], tew[128:256], preferred_element_type=F32)
-            + jnp.dot(one[672:688, 0:64], tew[256:320], preferred_element_type=F32)
-        )
-        tb[step] = bias / (1.0 + jnp.exp(-bias))
+        tb[step] = bias[slot * 16 : slot * 16 + 16]
     sums[...] = jnp.zeros_like(sums)
 
     def one_step(step, carry):
@@ -287,7 +287,11 @@
     return jnp.concatenate([vector, vector[:, 256:320]], axis=1)
 
 
-def second_sweep_kernel(first, states, above, below, far, mine, gain_ref, bias_ref, wp, tb, out, taps, scales):
+def second_sweep_kernel(first, states, above, below, far, mine, gain_ref, bias_ref, wp, tb, *refs):
+    if first:
+        earlier, out, total, taps, scales = refs
+    else:
+        out, taps, scales = refs
     gain, bias = wide(gain_ref), wide(bias_ref)
     x = lax.axis_index("x")
     parts = [stats_of(mine, 0), stats_of(above, 384), stats_of(below, 384), stats_of(far, 0)]
@@ -332,6 +336,9 @@
         return carry
 
     lax.fori_loop(0, 2, one_step, 0)
+    if first:
+        ones = [half[step].astype(F32) for half in (earlier, out) for step in range(2)]
+        total[...] = ((ones[0] + ones[1]) + (ones[2] + ones[3])).astype(BF16)
 
 
 def store_packed_frames(a3, tiles):
@@ -345,15 +352,8 @@
     a3[:, 896:1024] = jnp.where(low, tails[2], 0.0).astype(BF16)
 
 
-def second_total_kernel(own0, own1, before0, before1, after0, after1, tp, noise, rt, a3):
-    tiles = []
-    for pair in ((before0, before1), (own0, own1), (after0, after1)):
-        parts = []
-        for a, b in SPANS:
-            ones = [half[step, a:b].astype(F32) for half in pair for step in range(2)]
-            parts.append((ones[0] + ones[1]) + (ones[2] + ones[3]))
-        tiles.append(parts)
-    store_packed_frames(a3, tiles)
+def second_total_kernel(own, before, after, tp, noise, rt, a3):
+    store_packed_frames(a3, [[one[a:b].astype(F32) for a, b in SPANS] for one in (before, own, after)])
     for update, (a, b) in zip(packed_update(a3[...], tp), SPANS):
         total = update
         for step in range(4):
@@ -459,18 +459,21 @@
     packed = (ROWS, LANES)
     four = (4, ROWS, LANES)
 
-    *outgoing, = call(
-        pack_kernel, [((688, 128), BF16)] * 4, noise, emb, scratch=(((4, 256, 320), BF16),), hbm=1, sems=4
+    *outgoing, start, gain, bias = call(
+        pack_kernel,
+        [((688, 128), BF16)] * 4 + [((1024, 320), BF16), ((320,), F32), ((320,), F32)],
+        noise, start, gn_gain, gn_bias, emb,
+        scratch=(((4, 256, 320), BF16),),
+        hbm=4,
+        sems=7,
     )
     arrived = swap_x(outgoing)
-    nq, sp, wp, tp, tew, gain, bias = call(
+    nq, sp, wp, tp, tew = call(
         norm_start_kernel,
-        [((3, 320, 128), BF16), (packed, BF16), ((3, 1024, 320), BF16), ((1024, 320), BF16), ((320, 320), BF16)]
-        + [((320,), F32)] * 2,
-        start, gn_gain, gn_bias, spatial_weight, temporal_weight, temb_weight,
-        scratch=(((1024, 320), BF16),),
-        hbm=6,
-        sems=28,
+        [((800, 128), BF16), (packed, BF16), ((3, 1024, 320), BF16), ((1024, 320), BF16), ((320, 320), BF16)],
+        spatial_weight, temporal_weight, temb_weight, start, gain, bias,
+        hbm=3,
+        sems=25,
     )
     before, after = along_frame(nq, 1), along_frame(nq, -1)
     taps = ((320, 1024), BF16)
@@ -493,18 +496,20 @@
         sp, prefix, *totals,
     )
     edges = along_x(up, 1), along_x(down, -1), along_x(far, 2), far
-    halves = []
+    halves, earlier, outs = [], (), [((2, ROWS, LANES), BF16)]
     for half in (0, 1):
-        own = call(
+        own, *total = call(
             functools.partial(second_sweep_kernel, 2 * half),
-            [((2, ROWS, LANES), BF16)],
-            states, *edges, gain, bias, wp, tb,
+            outs + [(packed, BF16)] * half,
+            states, *edges, gain, bias, wp, tb, *earlier,
             scratch=(taps, ((4, 8, 384), F32)),
             flops=1024 * 320 * 2880,
-        )[0]
+        )
         halves.append((own, along_frame(own, 1), along_frame(own, -1)))
+        earlier = (own,)
     parts = [half[i] for i in range(3) for half in halves]
-    rt = call(second_total_kernel, [(packed, BF16)], *parts, tp, noises, scratch=(a3,), flops=512 * 320 * 960)[0]
+    sums = total[0], along_frame(total[0], 1), along_frame(total[0], -1)
+    rt = call(second_total_kernel, [(packed, BF16)], *sums, tp, noises, scratch=(a3,), flops=512 * 320 * 960)[0]
     totals = gather_y(rt)
     prefix = call(second_prefix_kernel, [(four, F32)], *parts, tp, noises, scratch=(a3,), flops=2048 * 320 * 960)[0]
     results = call(result_kernel, [(packed, BF16)] * 4, sp, prefix, *totals)

time: 84.8 us -> 89.5 us (1.055)
  waiting for transfers between devices: 34 us -> 36.4 us
  starting transfers between devices: 29 us -> 30.7 us
    ppermute x21 -> x23, waiting for transfers between devices: 34 us -> 36.4 us  [moved(): return lax.ppermute(value, AXES, pairs)]
    ppermute x21 -> x23, starting transfers between devices: 29 us -> 30.7 us  [moved(): return lax.ppermute(value, AXES, pairs)]
  transfers between devices with their start and end apart: 21 -> 23, of which waited for: 18 -> 14; matrix products, arithmetic and copies ran while one was open for 0% -> 0% of each run, Pallas kernels for 12% -> 7%
where the time goes in v2:
time: 89.5 us; the launch traced here: 89.4 us
  waiting for transfers between devices  36.4 us (41%)
  starting transfers between devices  30.7 us (34%)
  Pallas kernels  21.4 us (24%)
    ppermute x23, waiting for transfers between devices, moved(): return lax.ppermute(value, AXES, pairs)  36.4 us
    ppermute x23, starting transfers between devices, moved(): return lax.ppermute(value, AXES, pairs)  30.7 us
    pallas_call x13, Pallas kernels, call(): pl.pallas_call(body, out_shape=shapes, in_specs=[pl.BlockSpec(memory_spac...  21.4 us
  transfers between devices with their start and end apart: 23, of which 14 were waited for; matrix products, arithmetic and copies ran while one was open for 0% of the time, Pallas kernels for 7%

profile of v2, /device:TPU:6, one launch (start us, length us, event | category | flops | bytes accessed | tf_op | source)
XLA Modules:
  0.0 89.4 jit_solution(13788229095418699884)
XLA Ops:
  0.7 0.1 sine_convert_fusion
  0.7 0.1 fusion.2
  0.8 1.6 %shard_map.82 = (bf16[688,128]{1,0:T(8,128)(2,1)S(1)}, bf16[688,128]{1,0:T(8,128)(2,1)S(1)}, bf16[688,128]{1,0:T(8,128)(2,1)S(1)}, bf16[688,128]{1,0:T(8,128)(2,...) custom-call(bf16[1024,320]{1,0:T(8,128)(2,1)} %bitcast.4, bf16[1024,320]{1,0:T(8,128)(2,1)} %bitcast.5, ...), custom_call_target="tpu_custom_call" | custom-call | bytes 2688000 | tf_op jit(solution)/shard_map/pallas_call | solution.py:400
  2.4 3.2 %shard_map.83 = (bf16[800,128]{1,0:T(8,128)(2,1)S(1)}, bf16[640,128]{1,0:T(8,128)(2,1)S(1)}, bf16[3,1024,320]{2,1,0:T(8,128)(2,1)S(1)}, bf16[1024,320]{1,0:T(8,128)(2,1)S(1)}, bf16[320,320]{1,0:T(8,128)(2,1)S(1)}) custom-call(bf16[3,3,320,320]{3,2,1,0:T(8,128)(2,1)} %sw.1, bf16[3,320,320]{2,1,0:T(8,128)(2,1)} %tw.1, bf16[320,320]{1,0:T(8,128)(2,1)} %tew_hbm.1, ...), custom_call_target="tpu_custom_call" | custom-call | bytes 6515200 | tf_op jit(solution)/shard_map/pallas_call | solution.py:400
  5.6 5.3 %collective-permute-start.1 = (bf16[800,128]{1,0:T(8,128)(2,1)S(1)}, bf16[800,128]{1,0:T(8,128)(2,1)S(1)}, u32[]{:S(2)}, u32[]{:S(2)}) collective-permute-start(bf16[800,128]{1,0:T(8,128)(2,1)S(1)} %get-tuple-element.35.refs_0_), channel_id=1, source_target_pairs={{0,15},{1,0},{2,1},{3,2},{4,3},{5,4},{6,5},{7,6},{8,7},{9,8},{10,9... | collective-permute-start | bytes 614408 | tf_op jit(solution)/shard_map/ppermute | solution.py:419
  10.9 0.0 collective-permute-start
  10.9 0.5 collective-permute-start.2
  11.4 2.4 %collective-permute-start.3 = (bf16[688,128]{1,0:T(8,128)(2,1)S(1)}, bf16[688,128]{1,0:T(8,128)(2,1)S(1)}, u32[]{:S(2)}, u32[]{:S(2)}) collective-permute-start(bf16[688,128]{1,0:T(8,128)(2,1)S(1)} %get-tuple-element.41), channel_id=1, source_target_pairs={{0,32},{1,33},{2,34},{3,35},{4,36},{5,37},{6,38},{7,39},{8,40},{9,... | collective-permute-start | bytes 528392 | tf_op jit(solution)/shard_map/ppermute | solution.py:419
  13.8 0.0 collective-permute-start.4
  13.8 1.0 %shard_map.84.here = f32[1,256,320]{2,1,0:T(8,128)S(1)} custom-call(bf16[800,128]{1,0:T(8,128)(2,1)S(1)} %get-tuple-element.35.refs_0_, bf16[3,1024,320]{2,1,0:T(8,128)(2,1)S(1)} %get-tuple-element.36.refs_1_.refs_2_.wp), custom_call_target="tpu_custom_call" | custom-call | flops 471859200 | bytes 2498560 | tf_op jit(solution)/shard_map/pallas_call | solution.py:400
  14.8 0.0 collective-permute-done.1.refs_1_
  14.8 2.5 %collective-permute-done.refs_0_ = bf16[800,128]{1,0:T(8,128)(2,1)S(1)} collective-permute-done((bf16[800,128]{1,0:T(8,128)(2,1)S(1)}, bf16[800,128]{1,0:T(8,128)(2,1)S(1)}, u32[]{:S(2)}, u32[]{:S(2)}) %collective-permute-start) | collective-permute-done | bytes 204832 | tf_op jit(solution)/shard_map/ppermute | solution.py:419
  17.3 1.8 %shard_map.85.sides = f32[2,256,320]{2,1,0:T(8,128)S(1)} custom-call(bf16[800,128]{1,0:T(8,128)(2,1)S(1)} %collective-permute-done.refs_0_, bf16[800,128]{1,0:T(8,128)(2,1)S(1)} %collective-permute-done.1.refs_1_, bf16[3,1024,320]{2,1,0:T(8,128)(2,1)S(1)} %get-tuple-element.36.refs_1_.refs_2_.wp), custom_call_target="tpu_custom_call" | custom-call | flops 943718400 | bytes 3031040 | tf_op jit(solution)/shard_map/pallas_call | solution.py:400
  19.1 0.0 collective-permute-done.2.n1
  19.1 0.0 collective-permute-done.3.n2
  19.1 1.3 %collective-permute-done.4.n3 = bf16[688,128]{1,0:T(8,128)(2,1)S(1)} collective-permute-done((bf16[688,128]{1,0:T(8,128)(2,1)S(1)}, bf16[688,128]{1,0:T(8,128)(2,1)S(1)}, u32[]{:S(2)}, u32[]{:S(2)}) %collective-permute-start.4) | collective-permute-done | bytes 176160 | tf_op jit(solution)/shard_map/ppermute | solution.py:419
  20.4 2.5 %shard_map.86 = (bf16[640,128]{1,0:T(8,128)(2,1)S(1)}, bf16[4,640,128]{2,1,0:T(8,128)(2,1)S(1)}, f32[4,16,320]{2,1,0:T(8,128)S(1)}, bf16[4,256,1024]{2,1,0:T(8,128)(2,1)S(1)}) custom-call(f32[1,256,320]{2,1,0:T(8,128)S(1)} %shard_map.84.here, f32[2,256,320]{2,1,0:T(8,128)S(1)} %shard_map.85.sides, bf16[1024,320]{1,0:T(8,128)(2,1)S(1)} %get-tuple-element.37.tp, ...), custom_call_target="tpu_custom_call" | custom-call | flops 157286400 | bytes 5545984 | tf_op jit(solution)/shard_map/pallas_call | solution.py:400
  23.0 3.1 %collective-permute-start.7 = (bf16[640,128]{1,0:T(8,128)(2,1)S(1)}, bf16[640,128]{1,0:T(8,128)(2,1)S(1)}, u32[]{:S(2)}, u32[]{:S(2)}) collective-permute-start(bf16[640,128]{1,0:T(8,128)(2,1)S(1)} %get-tuple-element.45), channel_id=1, source_target_pairs={{0,192},{1,65},{2,194},{3,67},{4,196},{5,69},{6,198},{7,71},{8,200... | collective-permute-start | bytes 491528 | tf_op jit(solution)/shard_map/ppermute | solution.py:419
  26.1 0.6 collective-permute-start.6
  26.7 1.0 %collective-permute-start.5 = (bf16[640,128]{1,0:T(8,128)(2,1)S(1)}, bf16[640,128]{1,0:T(8,128)(2,1)S(1)}, u32[]{:S(2)}, u32[]{:S(2)}) collective-permute-start(bf16[640,128]{1,0:T(8,128)(2,1)S(1)} %get-tuple-element.45), channel_id=1, source_target_pairs={{0,64},{1,193},{2,66},{3,195},{4,68},{5,197},{6,70},{7,199},{8,72}... | collective-permute-start | bytes 491528 | tf_op jit(solution)/shard_map/ppermute | solution.py:419
  27.7 1.5 %shard_map.87.prefix = f32[4,640,128]{2,1,0:T(8,128)S(1)} custom-call(bf16[4,256,1024]{2,1,0:T(8,128)(2,1)S(1)} %get-tuple-element.43.a3s, bf16[1024,320]{1,0:T(8,128)(2,1)S(1)} %get-tuple-element.37.tp, bf16[4,640,128]{2,1,0:T(8,128)(2,1)S(1)} %get-tuple-element.44.noise), custom_call_target="tpu_custom_call" | custom-call | flops 471859200 | bytes 4718592 | tf_op jit(solution)/shard_map/pallas_call | solution.py:400
  29.2 0.7 collective-permute-done.7.r3
  29.9 3.1 %collective-permute-done.6.r2 = bf16[640,128]{1,0:T(8,128)(2,1)S(1)} collective-permute-done((bf16[640,128]{1,0:T(8,128)(2,1)S(1)}, bf16[640,128]{1,0:T(8,128)(2,1)S(1)}, u32[]{:S(2)}, u32[]{:S(2)}) %collective-permute-start.6) | collective-permute-done | bytes 163872 | tf_op jit(solution)/shard_map/ppermute | solution.py:419
  33.0 1.7 %collective-permute-done.5.r1 = bf16[640,128]{1,0:T(8,128)(2,1)S(1)} collective-permute-done((bf16[640,128]{1,0:T(8,128)(2,1)S(1)}, bf16[640,128]{1,0:T(8,128)(2,1)S(1)}, u32[]{:S(2)}, u32[]{:S(2)}) %collective-permute-start.5) | collective-permute-done | bytes 163872 | tf_op jit(solution)/shard_map/ppermute | solution.py:419
  34.6 1.4 %shard_map.88 = (bf16[4,640,128]{2,1,0:T(8,128)(2,1)S(1)}, bf16[464,128]{1,0:T(8,128)(2,1)S(1)}, bf16[464,128]{1,0:T(8,128)(2,1)S(1)}, bf16[72,128]{1,0:T(8,128)(2,1)S(1)}) custom-call(bf16[640,128]{1,0:T(8,128)(2,1)S(1)} %get-tuple-element.34.sp, f32[4,640,128]{2,1,0:T(8,128)S(1)} %shard_map.87.prefix, bf16[640,128]{1,0:T(8,128)(2,1)S(1)} %collective-permute-done.5.r1, ...), custom_call_target="tpu_custom_call" | custom-call | bytes 2877440 | tf_op jit(solution)/shard_map/pallas_call | solution.py:400
  36.1 1.9 %collective-permute-start.8 = (bf16[464,128]{1,0:T(8,128)(2,1)S(1)}, bf16[464,128]{1,0:T(8,128)(2,1)S(1)}, u32[]{:S(2)}, u32[]{:S(2)}) collective-permute-start(bf16[464,128]{1,0:T(8,128)(2,1)S(1)} %get-tuple-element.47), channel_id=1, source_target_pairs={{0,16},{1,17},{2,18},{3,19},{4,20},{5,21},{6,22},{7,23},{8,24},{9,... | collective-permute-start | bytes 356360 | tf_op jit(solution)/shard_map/ppermute | solution.py:419
  38.0 0.2 collective-permute-start.9
  38.2 1.8 %collective-permute-start.10 = (bf16[72,128]{1,0:T(8,128)(2,1)S(1)}, bf16[72,128]{1,0:T(8,128)(2,1)S(1)}, u32[]{:S(2)}, u32[]{:S(2)}) collective-permute-start(bf16[72,128]{1,0:T(8,128)(2,1)S(1)} %get-tuple-element.49.mine), channel_id=1, source_target_pairs={{0,32},{1,33},{2,34},{3,35},{4,36},{5,37},{6,38},{7,39},{8,40},{9,... | collective-permute-start | bytes 55304 | tf_op jit(solution)/shard_map/ppermute | solution.py:419
  40.0 3.6 %collective-permute-done.10.far = bf16[72,128]{1,0:T(8,128)(2,1)S(1)} collective-permute-done((bf16[72,128]{1,0:T(8,128)(2,1)S(1)}, bf16[72,128]{1,0:T(8,128)(2,1)S(1)}, u32[]{:S(2)}, u32[]{:S(2)}) %collective-permute-start.10) | collective-permute-done | bytes 18464 | tf_op jit(solution)/shard_map/ppermute | solution.py:419
  43.5 0.0 collective-permute-done.8.above
  43.5 0.7 collective-permute-done.9.below
  44.2 2.5 %shard_map.89.refs_0_.own0 = bf16[2,640,128]{2,1,0:T(8,128)(2,1)S(1)} custom-call(bf16[4,640,128]{2,1,0:T(8,128)(2,1)S(1)} %get-tuple-element.46.states, bf16[464,128]{1,0:T(8,128)(2,1)S(1)} %collective-permute-done.8.above, bf16[464,128]{1,0:T(8,128)(2,1)S(1)} %collective-permute-done.9.below, bf16[72,128]{1,0:T(8,128)(2,1)S(1)} %collective-permute-done.10.far, ...), custom_call_target="tpu_custom_call" | custom-call | flops 943718400 | bytes 3308032 | tf_op jit(solution)/shard_map/pallas_call | solution.py:400
  46.7 2.6 %shard_map.90 = (bf16[2,640,128]{2,1,0:T(8,128)(2,1)S(1)}, bf16[640,128]{1,0:T(8,128)(2,1)S(1)}) custom-call(bf16[4,640,128]{2,1,0:T(8,128)(2,1)S(1)} %get-tuple-element.46.states, bf16[464,128]{1,0:T(8,128)(2,1)S(1)} %collective-permute-done.8.above, bf16[464,128]{1,0:T(8,128)(2,1)S(1)} %collective-permute-done.9.below, ...), custom_call_target="tpu_custom_call" | custom-call | flops 943718400 | bytes 3799552 | tf_op jit(solution)/shard_map/pallas_call | solution.py:400
  49.3 1.3 %collective-permute-start.16 = (bf16[640,128]{1,0:T(8,128)(2,1)S(1)}, bf16[640,128]{1,0:T(8,128)(2,1)S(1)}, u32[]{:S(2)}, u32[]{:S(2)}) collective-permute-start(bf16[640,128]{1,0:T(8,128)(2,1)S(1)} %get-tuple-element.52.own), channel_id=1, source_target_pairs={{0,15},{1,0},{2,1},{3,2},{4,3},{5,4},{6,5},{7,6},{8,7},{9,8},{10,9... | collective-permute-start | bytes 491528 | tf_op jit(solution)/shard_map/ppermute | solution.py:419
  50.7 2.9 %collective-permute-start.14 = (bf16[2,640,128]{2,1,0:T(8,128)(2,1)S(1)}, bf16[2,640,128]{2,1,0:T(8,128)(2,1)S(1)}, u32[]{:S(2)}, u32[]{:S(2)}) collective-permute-start(bf16[2,640,128]{2,1,0:T(8,128)(2,1)S(1)} %get-tuple-element.51.own1), channel_id=1, source_target_pairs={{0,15},{1,0},{2,1},{3,2},{4,3},{5,4},{6,5},{7,6},{8,7},{9,8},{10,9... | collective-permute-start | bytes 983048 | tf_op jit(solution)/shard_map/ppermute | solution.py:419
  53.6 0.0 collective-permute-start.12
  53.6 3.0 %collective-permute-start.13 = (bf16[2,640,128]{2,1,0:T(8,128)(2,1)S(1)}, bf16[2,640,128]{2,1,0:T(8,128)(2,1)S(1)}, u32[]{:S(2)}, u32[]{:S(2)}) collective-permute-start(bf16[2,640,128]{2,1,0:T(8,128)(2,1)S(1)} %shard_map.89.refs_0_.own0), channel_id=1, source_target_pairs={{0,15},{1,0},{2,1},{3,2},{4,3},{5,4},{6,5},{7,6},{8,7},{9,8},{10,9... | collective-permute-start | bytes 983048 | tf_op jit(solution)/shard_map/ppermute | solution.py:419
  56.5 0.0 collective-permute-start.11
  56.5 0.0 collective-permute-done.16.after
  56.5 0.0 collective-permute-start.15
  56.5 10.0 %collective-permute-done.15.before = bf16[640,128]{1,0:T(8,128)(2,1)S(1)} collective-permute-done((bf16[640,128]{1,0:T(8,128)(2,1)S(1)}, bf16[640,128]{1,0:T(8,128)(2,1)S(1)}, u32[]{:S(2)}, u32[]{:S(2)}) %collective-permute-start.15) | collective-permute-done | bytes 163872 | tf_op jit(solution)/shard_map/ppermute | solution.py:419
  66.5 0.5 shard_map.92
  67.1 2.4 %collective-permute-start.19 = (bf16[640,128]{1,0:T(8,128)(2,1)S(1)}, bf16[640,128]{1,0:T(8,128)(2,1)S(1)}, u32[]{:S(2)}, u32[]{:S(2)}) collective-permute-start(bf16[640,128]{1,0:T(8,128)(2,1)S(1)} %shard_map.92), channel_id=1, source_target_pairs={{0,192},{1,65},{2,194},{3,67},{4,196},{5,69},{6,198},{7,71},{8,200... | collective-permute-start | bytes 491528 | tf_op jit(solution)/shard_map/ppermute | solution.py:419
  69.4 0.0 collective-permute-done.14.after1
  69.4 1.2 %collective-permute-start.18 = (bf16[640,128]{1,0:T(8,128)(2,1)S(1)}, bf16[640,128]{1,0:T(8,128)(2,1)S(1)}, u32[]{:S(2)}, u32[]{:S(2)}) collective-permute-start(bf16[640,128]{1,0:T(8,128)(2,1)S(1)} %shard_map.92), channel_id=1, source_target_pairs={{0,128},{1,129},{2,130},{3,131},{4,132},{5,133},{6,134},{7,135},{8... | collective-permute-start | bytes 491528 | tf_op jit(solution)/shard_map/ppermute | solution.py:419
  70.6 0.0 collective-permute-done.12.before1
  70.6 0.0 collective-permute-start.17
  70.6 0.0 collective-permute-done.13.after0
  70.7 0.0 collective-permute-done.11.before0
  70.7 1.5 %shard_map.91.prefix = f32[4,640,128]{2,1,0:T(8,128)S(1)} custom-call(bf16[2,640,128]{2,1,0:T(8,128)(2,1)S(1)} %shard_map.89.refs_0_.own0, bf16[2,640,128]{2,1,0:T(8,128)(2,1)S(1)} %get-tuple-element.51.own1, bf16[2,640,128]{2,1,0:T(8,128)(2,1)S(1)} %collective-permute-done.11.before0, bf16[2,640,128]{2,1,0:T(8,128)(2,1)S(1)} %collective-permute-done.12.before1, ...), custom_call_target="tpu_custom_call" | custom-call | flops 629145600 | bytes 4587520 | tf_op jit(solution)/shard_map/pallas_call | solution.py:400
  72.2 1.9 %collective-permute-done.19.r3 = bf16[640,128]{1,0:T(8,128)(2,1)S(1)} collective-permute-done((bf16[640,128]{1,0:T(8,128)(2,1)S(1)}, bf16[640,128]{1,0:T(8,128)(2,1)S(1)}, u32[]{:S(2)}, u32[]{:S(2)}) %collective-permute-start.19) | collective-permute-done | bytes 163872 | tf_op jit(solution)/shard_map/ppermute | solution.py:419
  74.1 2.3 %collective-permute-done.18.r2 = bf16[640,128]{1,0:T(8,128)(2,1)S(1)} collective-permute-done((bf16[640,128]{1,0:T(8,128)(2,1)S(1)}, bf16[640,128]{1,0:T(8,128)(2,1)S(1)}, u32[]{:S(2)}, u32[]{:S(2)}) %collective-permute-start.18) | collective-permute-done | bytes 163872 | tf_op jit(solution)/shard_map/ppermute | solution.py:419
  76.4 1.7 %collective-permute-done.17.r1 = bf16[640,128]{1,0:T(8,128)(2,1)S(1)} collective-permute-done((bf16[640,128]{1,0:T(8,128)(2,1)S(1)}, bf16[640,128]{1,0:T(8,128)(2,1)S(1)}, u32[]{:S(2)}, u32[]{:S(2)}) %collective-permute-start.17) | collective-permute-done | bytes 163872 | tf_op jit(solution)/shard_map/ppermute | solution.py:419
  78.0 0.2 shard_map.93
  78.2 1.6 %collective-permute-start.20 = (bf16[640,128]{1,0:T(8,128)(2,1)S(1)}, bf16[640,128]{1,0:T(8,128)(2,1)S(1)}, u32[]{:S(2)}, u32[]{:S(2)}) collective-permute-start(bf16[640,128]{1,0:T(8,128)(2,1)S(1)} %get-tuple-element.54), channel_id=1, source_target_pairs={{0,16},{1,49},{2,18},{3,51},{4,20},{5,53},{6,22},{7,55},{8,24},{9,... | collective-permute-start | bytes 491528 | tf_op jit(solution)/shard_map/ppermute | solution.py:419
  79.8 0.6 collective-permute-start.21
  80.4 1.0 %collective-permute-start.22 = (bf16[640,128]{1,0:T(8,128)(2,1)S(1)}, bf16[640,128]{1,0:T(8,128)(2,1)S(1)}, u32[]{:S(2)}, u32[]{:S(2)}) collective-permute-start(bf16[640,128]{1,0:T(8,128)(2,1)S(1)} %get-tuple-element.56), channel_id=1, source_target_pairs={{0,48},{1,17},{2,50},{3,19},{4,52},{5,21},{6,54},{7,23},{8,56},{9,... | collective-permute-start | bytes 491528 | tf_op jit(solution)/shard_map/ppermute | solution.py:419
  81.3 2.3 %collective-permute-done.20.r1 = bf16[640,128]{1,0:T(8,128)(2,1)S(1)} collective-permute-done((bf16[640,128]{1,0:T(8,128)(2,1)S(1)}, bf16[640,128]{1,0:T(8,128)(2,1)S(1)}, u32[]{:S(2)}, u32[]{:S(2)}) %collective-permute-start.20) | collective-permute-done | bytes 163872 | tf_op jit(solution)/shard_map/ppermute | solution.py:419
  83.6 3.1 %collective-permute-done.21.r2 = bf16[640,128]{1,0:T(8,128)(2,1)S(1)} collective-permute-done((bf16[640,128]{1,0:T(8,128)(2,1)S(1)}, bf16[640,128]{1,0:T(8,128)(2,1)S(1)}, u32[]{:S(2)}, u32[]{:S(2)}) %collective-permute-start.21) | collective-permute-done | bytes 163872 | tf_op jit(solution)/shard_map/ppermute | solution.py:419
  86.7 1.7 %collective-permute-done.22.r3 = bf16[640,128]{1,0:T(8,128)(2,1)S(1)} collective-permute-done((bf16[640,128]{1,0:T(8,128)(2,1)S(1)}, bf16[640,128]{1,0:T(8,128)(2,1)S(1)}, u32[]{:S(2)}, u32[]{:S(2)}) %collective-permute-start.22) | collective-permute-done | bytes 163872 | tf_op jit(solution)/shard_map/ppermute | solution.py:419
  88.4 1.0 %shard_map.94 = bf16[1024,320]{1,0:T(8,128)(2,1)} custom-call(bf16[640,128]{1,0:T(8,128)(2,1)S(1)} %get-tuple-element.53.r0, bf16[640,128]{1,0:T(8,128)(2,1)S(1)} %collective-permute-done.20.r1, bf16[640,128]{1,0:T(8,128)(2,1)S(1)} %collective-permute-done.21.r2, bf16[640,128]{1,0:T(8,128)(2,1)S(1)} %collective-permute-done.22.r3), custom_call_target="tpu_custom_call" | custom-call | bytes 1310720 | tf_op jit(solution)/shard_map/pallas_call | solution.py:400
  (1 shorter events, 0.0 us)
Async XLA Ops:
  5.6 9.2 %collective-permute-start.1 = (bf16[800,128]{1,0:T(8,128)(2,1)S(1)}, bf16[800,128]{1,0:T(8,128)(2,1)S(1)}, u32[]{:S(2)}, u32[]{:S(2)}) collective-permute-start(bf16[800,128]{1,0:T(8,128)(2,1)S(1)} %get-tuple-element.35.refs_0_), channel_id=1, source_target_pairs={{0,15},{1,0},{2,1},{3,2},{4,3},{5,4},{6,5},{7,6},{8,7},{9,8},{10,9... | collective-permute-start | bytes 614408 | tf_op jit(solution)/shard_map/ppermute | solution.py:419
  10.9 6.4 %collective-permute-start = (bf16[800,128]{1,0:T(8,128)(2,1)S(1)}, bf16[800,128]{1,0:T(8,128)(2,1)S(1)}, u32[]{:S(2)}, u32[]{:S(2)}) collective-permute-start(bf16[800,128]{1,0:T(8,128)(2,1)S(1)} %get-tuple-element.35.refs_0_), channel_id=1, source_target_pairs={{0,1},{1,2},{2,3},{3,4},{4,5},{5,6},{6,7},{7,8},{8,9},{9,10},{10,1... | collective-permute-start | bytes 614408 | tf_op jit(solution)/shard_map/ppermute | solution.py:419
  10.9 8.2 %collective-permute-start.2 = (bf16[688,128]{1,0:T(8,128)(2,1)S(1)}, bf16[688,128]{1,0:T(8,128)(2,1)S(1)}, u32[]{:S(2)}, u32[]{:S(2)}) collective-permute-start(bf16[688,128]{1,0:T(8,128)(2,1)S(1)} %get-tuple-element.40), channel_id=1, source_target_pairs={{0,16},{1,49},{2,18},{3,51},{4,20},{5,53},{6,22},{7,55},{8,24},{9,... | collective-permute-start | bytes 528392 | tf_op jit(solution)/shard_map/ppermute | solution.py:419
  11.4 7.8 %collective-permute-start.3 = (bf16[688,128]{1,0:T(8,128)(2,1)S(1)}, bf16[688,128]{1,0:T(8,128)(2,1)S(1)}, u32[]{:S(2)}, u32[]{:S(2)}) collective-permute-start(bf16[688,128]{1,0:T(8,128)(2,1)S(1)} %get-tuple-element.41), channel_id=1, source_target_pairs={{0,32},{1,33},{2,34},{3,35},{4,36},{5,37},{6,38},{7,39},{8,40},{9,... | collective-permute-start | bytes 528392 | tf_op jit(solution)/shard_map/ppermute | solution.py:419
  13.8 6.7 %collective-permute-start.4 = (bf16[688,128]{1,0:T(8,128)(2,1)S(1)}, bf16[688,128]{1,0:T(8,128)(2,1)S(1)}, u32[]{:S(2)}, u32[]{:S(2)}) collective-permute-start(bf16[688,128]{1,0:T(8,128)(2,1)S(1)} %get-tuple-element.42), channel_id=1, source_target_pairs={{0,48},{1,17},{2,50},{3,19},{4,52},{5,21},{6,54},{7,23},{8,56},{9,... | collective-permute-start | bytes 528392 | tf_op jit(solution)/shard_map/ppermute | solution.py:419
  23.0 6.9 %collective-permute-start.7 = (bf16[640,128]{1,0:T(8,128)(2,1)S(1)}, bf16[640,128]{1,0:T(8,128)(2,1)S(1)}, u32[]{:S(2)}, u32[]{:S(2)}) collective-permute-start(bf16[640,128]{1,0:T(8,128)(2,1)S(1)} %get-tuple-element.45), channel_id=1, source_target_pairs={{0,192},{1,65},{2,194},{3,67},{4,196},{5,69},{6,198},{7,71},{8,200... | collective-permute-start | bytes 491528 | tf_op jit(solution)/shard_map/ppermute | solution.py:419
  26.1 6.9 %collective-permute-start.6 = (bf16[640,128]{1,0:T(8,128)(2,1)S(1)}, bf16[640,128]{1,0:T(8,128)(2,1)S(1)}, u32[]{:S(2)}, u32[]{:S(2)}) collective-permute-start(bf16[640,128]{1,0:T(8,128)(2,1)S(1)} %get-tuple-element.45), channel_id=1, source_target_pairs={{0,128},{1,129},{2,130},{3,131},{4,132},{5,133},{6,134},{7,135},{8... | collective-permute-start | bytes 491528 | tf_op jit(solution)/shard_map/ppermute | solution.py:419
  26.7 7.9 %collective-permute-start.5 = (bf16[640,128]{1,0:T(8,128)(2,1)S(1)}, bf16[640,128]{1,0:T(8,128)(2,1)S(1)}, u32[]{:S(2)}, u32[]{:S(2)}) collective-permute-start(bf16[640,128]{1,0:T(8,128)(2,1)S(1)} %get-tuple-element.45), channel_id=1, source_target_pairs={{0,64},{1,193},{2,66},{3,195},{4,68},{5,197},{6,70},{7,199},{8,72}... | collective-permute-start | bytes 491528 | tf_op jit(solution)/shard_map/ppermute | solution.py:419
  36.1 7.5 %collective-permute-start.8 = (bf16[464,128]{1,0:T(8,128)(2,1)S(1)}, bf16[464,128]{1,0:T(8,128)(2,1)S(1)}, u32[]{:S(2)}, u32[]{:S(2)}) collective-permute-start(bf16[464,128]{1,0:T(8,128)(2,1)S(1)} %get-tuple-element.47), channel_id=1, source_target_pairs={{0,16},{1,17},{2,18},{3,19},{4,20},{5,21},{6,22},{7,23},{8,24},{9,... | collective-permute-start | bytes 356360 | tf_op jit(solution)/shard_map/ppermute | solution.py:419
  38.0 6.2 %collective-permute-start.9 = (bf16[464,128]{1,0:T(8,128)(2,1)S(1)}, bf16[464,128]{1,0:T(8,128)(2,1)S(1)}, u32[]{:S(2)}, u32[]{:S(2)}) collective-permute-start(bf16[464,128]{1,0:T(8,128)(2,1)S(1)} %get-tuple-element.48), channel_id=1, source_target_pairs={{0,48},{1,49},{2,50},{3,51},{4,52},{5,53},{6,54},{7,55},{8,56},{9,... | collective-permute-start | bytes 356360 | tf_op jit(solution)/shard_map/ppermute | solution.py:419
  38.2 5.4 %collective-permute-start.10 = (bf16[72,128]{1,0:T(8,128)(2,1)S(1)}, bf16[72,128]{1,0:T(8,128)(2,1)S(1)}, u32[]{:S(2)}, u32[]{:S(2)}) collective-permute-start(bf16[72,128]{1,0:T(8,128)(2,1)S(1)} %get-tuple-element.49.mine), channel_id=1, source_target_pairs={{0,32},{1,33},{2,34},{3,35},{4,36},{5,37},{6,38},{7,39},{8,40},{9,... | collective-permute-start | bytes 55304 | tf_op jit(solution)/shard_map/ppermute | solution.py:419
  49.3 7.2 %collective-permute-start.16 = (bf16[640,128]{1,0:T(8,128)(2,1)S(1)}, bf16[640,128]{1,0:T(8,128)(2,1)S(1)}, u32[]{:S(2)}, u32[]{:S(2)}) collective-permute-start(bf16[640,128]{1,0:T(8,128)(2,1)S(1)} %get-tuple-element.52.own), channel_id=1, source_target_pairs={{0,15},{1,0},{2,1},{3,2},{4,3},{5,4},{6,5},{7,6},{8,7},{9,8},{10,9... | collective-permute-start | bytes 491528 | tf_op jit(solution)/shard_map/ppermute | solution.py:419
  50.7 18.8 %collective-permute-start.14 = (bf16[2,640,128]{2,1,0:T(8,128)(2,1)S(1)}, bf16[2,640,128]{2,1,0:T(8,128)(2,1)S(1)}, u32[]{:S(2)}, u32[]{:S(2)}) collective-permute-start(bf16[2,640,128]{2,1,0:T(8,128)(2,1)S(1)} %get-tuple-element.51.own1), channel_id=1, source_target_pairs={{0,15},{1,0},{2,1},{3,2},{4,3},{5,4},{6,5},{7,6},{8,7},{9,8},{10,9... | collective-permute-start | bytes 983048 | tf_op jit(solution)/shard_map/ppermute | solution.py:419
  53.6 17.1 %collective-permute-start.12 = (bf16[2,640,128]{2,1,0:T(8,128)(2,1)S(1)}, bf16[2,640,128]{2,1,0:T(8,128)(2,1)S(1)}, u32[]{:S(2)}, u32[]{:S(2)}) collective-permute-start(bf16[2,640,128]{2,1,0:T(8,128)(2,1)S(1)} %get-tuple-element.51.own1), channel_id=1, source_target_pairs={{0,1},{1,2},{2,3},{3,4},{4,5},{5,6},{6,7},{7,8},{8,9},{9,10},{10,1... | collective-permute-start | bytes 983048 | tf_op jit(solution)/shard_map/ppermute | solution.py:419
  53.6 17.1 %collective-permute-start.13 = (bf16[2,640,128]{2,1,0:T(8,128)(2,1)S(1)}, bf16[2,640,128]{2,1,0:T(8,128)(2,1)S(1)}, u32[]{:S(2)}, u32[]{:S(2)}) collective-permute-start(bf16[2,640,128]{2,1,0:T(8,128)(2,1)S(1)} %shard_map.89.refs_0_.own0), channel_id=1, source_target_pairs={{0,15},{1,0},{2,1},{3,2},{4,3},{5,4},{6,5},{7,6},{8,7},{9,8},{10,9... | collective-permute-start | bytes 983048 | tf_op jit(solution)/shard_map/ppermute | solution.py:419
  56.5 14.1 %collective-permute-start.11 = (bf16[2,640,128]{2,1,0:T(8,128)(2,1)S(1)}, bf16[2,640,128]{2,1,0:T(8,128)(2,1)S(1)}, u32[]{:S(2)}, u32[]{:S(2)}) collective-permute-start(bf16[2,640,128]{2,1,0:T(8,128)(2,1)S(1)} %shard_map.89.refs_0_.own0), channel_id=1, source_target_pairs={{0,1},{1,2},{2,3},{3,4},{4,5},{5,6},{6,7},{7,8},{8,9},{9,10},{10,1... | collective-permute-start | bytes 983048 | tf_op jit(solution)/shard_map/ppermute | solution.py:419
  56.5 10.0 %collective-permute-start.15 = (bf16[640,128]{1,0:T(8,128)(2,1)S(1)}, bf16[640,128]{1,0:T(8,128)(2,1)S(1)}, u32[]{:S(2)}, u32[]{:S(2)}) collective-permute-start(bf16[640,128]{1,0:T(8,128)(2,1)S(1)} %get-tuple-element.52.own), channel_id=1, source_target_pairs={{0,1},{1,2},{2,3},{3,4},{4,5},{5,6},{6,7},{7,8},{8,9},{9,10},{10,1... | collective-permute-start | bytes 491528 | tf_op jit(solution)/shard_map/ppermute | solution.py:419
  67.1 7.0 %collective-permute-start.19 = (bf16[640,128]{1,0:T(8,128)(2,1)S(1)}, bf16[640,128]{1,0:T(8,128)(2,1)S(1)}, u32[]{:S(2)}, u32[]{:S(2)}) collective-permute-start(bf16[640,128]{1,0:T(8,128)(2,1)S(1)} %shard_map.92), channel_id=1, source_target_pairs={{0,192},{1,65},{2,194},{3,67},{4,196},{5,69},{6,198},{7,71},{8,200... | collective-permute-start | bytes 491528 | tf_op jit(solution)/shard_map/ppermute | solution.py:419
  69.4 6.9 %collective-permute-start.18 = (bf16[640,128]{1,0:T(8,128)(2,1)S(1)}, bf16[640,128]{1,0:T(8,128)(2,1)S(1)}, u32[]{:S(2)}, u32[]{:S(2)}) collective-permute-start(bf16[640,128]{1,0:T(8,128)(2,1)S(1)} %shard_map.92), channel_id=1, source_target_pairs={{0,128},{1,129},{2,130},{3,131},{4,132},{5,133},{6,134},{7,135},{8... | collective-permute-start | bytes 491528 | tf_op jit(solution)/shard_map/ppermute | solution.py:419
  70.6 7.4 %collective-permute-start.17 = (bf16[640,128]{1,0:T(8,128)(2,1)S(1)}, bf16[640,128]{1,0:T(8,128)(2,1)S(1)}, u32[]{:S(2)}, u32[]{:S(2)}) collective-permute-start(bf16[640,128]{1,0:T(8,128)(2,1)S(1)} %shard_map.92), channel_id=1, source_target_pairs={{0,64},{1,193},{2,66},{3,195},{4,68},{5,197},{6,70},{7,199},{8,72}... | collective-permute-start | bytes 491528 | tf_op jit(solution)/shard_map/ppermute | solution.py:419
  78.2 5.4 %collective-permute-start.20 = (bf16[640,128]{1,0:T(8,128)(2,1)S(1)}, bf16[640,128]{1,0:T(8,128)(2,1)S(1)}, u32[]{:S(2)}, u32[]{:S(2)}) collective-permute-start(bf16[640,128]{1,0:T(8,128)(2,1)S(1)} %get-tuple-element.54), channel_id=1, source_target_pairs={{0,16},{1,49},{2,18},{3,51},{4,20},{5,53},{6,22},{7,55},{8,24},{9,... | collective-permute-start | bytes 491528 | tf_op jit(solution)/shard_map/ppermute | solution.py:419
  79.8 6.9 %collective-permute-start.21 = (bf16[640,128]{1,0:T(8,128)(2,1)S(1)}, bf16[640,128]{1,0:T(8,128)(2,1)S(1)}, u32[]{:S(2)}, u32[]{:S(2)}) collective-permute-start(bf16[640,128]{1,0:T(8,128)(2,1)S(1)} %get-tuple-element.55), channel_id=1, source_target_pairs={{0,32},{1,33},{2,34},{3,35},{4,36},{5,37},{6,38},{7,39},{8,40},{9,... | collective-permute-start | bytes 491528 | tf_op jit(solution)/shard_map/ppermute | solution.py:419
  80.4 8.0 %collective-permute-start.22 = (bf16[640,128]{1,0:T(8,128)(2,1)S(1)}, bf16[640,128]{1,0:T(8,128)(2,1)S(1)}, u32[]{:S(2)}, u32[]{:S(2)}) collective-permute-start(bf16[640,128]{1,0:T(8,128)(2,1)S(1)} %get-tuple-element.56), channel_id=1, source_target_pairs={{0,48},{1,17},{2,50},{3,19},{4,52},{5,21},{6,54},{7,23},{8,56},{9,... | collective-permute-start | bytes 491528 | tf_op jit(solution)/shard_map/ppermute | solution.py:419

commit v3 on v2

--- a/solution.py
+++ b/solution.py
@@ -11,7 +11,6 @@
 
 F32, BF16 = jnp.float32, jnp.bfloat16
 AXES = ("y", "x", "z", "core")
-HIGHEST = lax.Precision.HIGHEST
 
 POS, ROWS, LANES = 256, 640, 128
 
@@ -42,11 +41,21 @@
 def same_group(size):
     rows = lax.broadcasted_iota(jnp.int32, (size, size), 0)
     columns = lax.broadcasted_iota(jnp.int32, (size, size), 1)
-    return (((rows * 6554) >> 16) == ((columns * 6554) >> 16)).astype(F32)
+    return (((rows * 6554) >> 16) == ((columns * 6554) >> 16)).astype(F32).astype(BF16)
+
+
+def thirds(value):
+    parts = []
+    for _ in range(3):
+        part = value.astype(BF16).astype(F32)
+        value = value - part
+        parts.append(part)
+    return parts
 
 
 def group_sum(sums, members):
-    return jnp.dot(sums, members, precision=HIGHEST, preferred_element_type=F32)
+    wide = jnp.dot(jnp.concatenate(thirds(sums), axis=0).astype(BF16), members, preferred_element_type=F32)
+    return (wide[0:8] + wide[8:16]) + wide[16:24]
 
 
 def store_taps(taps, tiles):
@@ -67,12 +76,13 @@
     taps[:, 896:1024] = jnp.where(low, shifted[2], 0.0).astype(BF16)
 
 
-def conv_rows(taps, wp):
-    total = None
-    for row in range(3):
-        term = jnp.dot(taps[row * 32 : row * 32 + POS, :], wp[row], preferred_element_type=F32)
-        total = term if total is None else total + term
-    return total
+def conv_tail(taps, wt):
+    wide = jnp.dot(taps[...], wt[...], preferred_element_type=F32)
+    return (wide[0:256, 0:64] + wide[32:288, 64:128]) + wide[64:320, 128:192]
+
+
+def conv_row(taps, wp, row):
+    return jnp.dot(taps[row * 32 : row * 32 + POS, :], wp[row, :, 0:256], preferred_element_type=F32)
 
 
 def hop_of(slot):
@@ -105,24 +115,9 @@
         copy.wait()
 
 
-def norm_start_kernel(sw, tw, tew_hbm, start, gain_ref, bias_ref, nq, sp, wp, tp, tew, sems):
+def norm_start_kernel(start, gain_ref, bias_ref, nq, sp):
     x = lax.axis_index("x")
-    frame = lax.axis_index("z") * 2 + lax.axis_index("core")
-    moves = []
-    for row in range(4):
-        out = tp if row == 3 else wp.at[row]
-        for place in range(3):
-            one = tw.at[place] if row == 3 else sw.at[row, place]
-            moves.append((one.at[0:256], out.at[place * 256 : place * 256 + 256]))
-            moves.append((one.at[256:320], out.at[768 + 64 * place : 832 + 64 * place]))
-    moves.append((tew_hbm, tew))
-    copies = [pltpu.make_async_copy(source, target, sems.at[i]) for i, (source, target) in enumerate(moves)]
-    for copy in copies:
-        copy.start()
     members = same_group(320)
-    for row in range(3):
-        wp[row, 960:1024] = jnp.zeros((64, 320), BF16)
-    tp[960:1024] = jnp.zeros((64, 320), BF16)
     values = start[...].astype(F32)
     mean = group_sum(jnp.broadcast_to(jnp.sum(values, axis=0, keepdims=True), (8, 320)), members)[0:1] * (1.0 / 10240)
     centered = start[...].astype(F32) - mean
@@ -145,7 +140,50 @@
     sp[0:256] = start[pl.ds(first, POS), 0:128]
     sp[256:512] = start[pl.ds(first, POS), 128:256]
     sp[512:640] = pack_tail(start[pl.ds(first, POS), 256:320].astype(F32)).astype(BF16)
+
+
+def conv_frame(normed, wp, wt, pre, taps, before_row=None):
+    store_taps(taps, [normed[0:320].astype(F32), normed[320:640].astype(F32), spread_tail(normed[640:800].astype(F32))])
+    main = None
+    for row in range(3):
+        if before_row is not None:
+            before_row(row)
+        term = conv_row(taps, wp, row)
+        main = term if main is None else main + term
+    if before_row is not None:
+        before_row(3)
+    pre[:, 0:256] = 0.5 * main
+    pre[:, 256:320] = 0.5 * conv_tail(taps, wt)
+
+
+def first_own_kernel(sw, tw, tew_hbm, normed, pre, wp, wt, tp, tew, taps, sems):
+    frame = lax.axis_index("z") * 2 + lax.axis_index("core")
+    copies = []
+    for row in range(4):
+        out = tp if row == 3 else wp.at[row]
+        for place in range(3):
+            one = tw.at[place] if row == 3 else sw.at[row, place]
+            for source, target in (
+                (one.at[0:256], out.at[place * 256 : place * 256 + 256]),
+                (one.at[256:320], out.at[768 + 64 * place : 832 + 64 * place]),
+            ):
+                copies.append(pltpu.make_async_copy(source, target, sems.at[len(copies)]))
+    copies.append(pltpu.make_async_copy(tew_hbm, tew, sems.at[24]))
     for copy in copies:
+        copy.start()
+    for row in range(3):
+        wp[row, 960:1024] = jnp.zeros((64, 320), BF16)
+    tp[960:1024] = jnp.zeros((64, 320), BF16)
+
+    def before_row(row):
+        if row < 3:
+            for copy in copies[6 * row : 6 * row + 6]:
+                copy.wait()
+        else:
+            wt[...] = jnp.concatenate([wp[i, :, 256:320].astype(F32) for i in range(3)], axis=1).astype(BF16)
+
+    conv_frame(normed, wp, wt, pre.at[0], taps, before_row)
+    for copy in copies[18:]:
         copy.wait()
     for place, missing in ((0, frame == 0), (2, frame == 15)):
 
@@ -155,11 +193,13 @@
             tp[768 + 64 * place : 832 + 64 * place] = jnp.zeros((64, 320), BF16)
 
 
-def first_conv_kernel(*refs):
-    *normed, wp, pre, taps = refs
-    for place, one in enumerate(normed):
-        store_taps(taps, [one[0:320].astype(F32), one[320:640].astype(F32), spread_tail(one[640:800].astype(F32))])
-        pre[place] = conv_rows(taps, wp)
+def first_sides_kernel(before, after, wp, wt, pre, taps):
+    for place, normed in enumerate((before, after)):
+        conv_frame(normed, wp, wt, pre.at[place], taps)
+
+
+def silu_half(half):
+    return half + half * jnp.tanh(half)
 
 
 SPANS = ((0, 256), (256, 512), (512, 640))
@@ -178,7 +218,7 @@
     a3[:, 896:1024] = jnp.concatenate([last, jnp.zeros_like(last)], axis=1).astype(BF16)
 
 
-def first_total_kernel(here, sides, tp, tew, n0, n1, n2, n3, rt, noise, tb, a3s, sums, a3):
+def first_total_kernel(here, sides, tp, tew, n0, n1, n2, n3, rt, noise, tb, a3, tails):
     x = lax.axis_index("x")
     arrived = (n0, n1, n2, n3)
     bias = None
@@ -191,20 +231,21 @@
         step = lax.rem(x + 4 - hop_of(slot), 4)
         noise[step] = one[0:640]
         tb[step] = bias[slot * 16 : slot * 16 + 16]
-    sums[...] = jnp.zeros_like(sums)
-
-    def one_step(step, carry):
-        bias = tb[step][0:1]
-        parts = []
+    halves = [0.5 * bias[slot * 16 : slot * 16 + 1] for slot in range(4)]
+
+    def some_rows(block, carry):
+        rows = pl.ds(pl.multiple_of(block * 32, 32), 32)
         for place, pre in enumerate((sides.at[0], here.at[0], sides.at[1])):
-            activated = silu(pre[...] + bias)
-            sums[place] += activated
-            parts.append(activated)
-        store_frames(a3s.at[step], parts)
+            half = pre[rows, :]
+            ones = [silu_half(half + one) for one in halves]
+            total = (ones[0] + ones[1]) + (ones[2] + ones[3])
+            a3[rows, place * 256 : place * 256 + 256] = total[:, 0:256].astype(BF16)
+            tails[place, rows, :] = total[:, 256:320]
         return carry
 
-    lax.fori_loop(0, 4, one_step, 0)
-    store_frames(a3, [sums[place] for place in range(3)])
+    lax.fori_loop(0, 8, some_rows, 0)
+    a3[:, 768:896] = jnp.concatenate([tails[0], tails[1]], axis=1).astype(BF16)
+    a3[:, 896:1024] = jnp.concatenate([tails[2], jnp.zeros((POS, 64), F32)], axis=1).astype(BF16)
     for update, (a, b) in zip(packed_update(a3[...], tp), SPANS):
         total = update
         for step in range(4):
@@ -212,11 +253,13 @@
         rt[a:b] = (0.25 * total).astype(BF16)
 
 
-def first_prefix_kernel(a3s, tp, noise, prefix):
+def first_prefix_kernel(here, sides, tb, tp, noise, prefix, a3):
     prefix[0] = jnp.zeros((ROWS, LANES), F32)
 
     def one_step(step, carry):
-        for update, (a, b) in zip(packed_update(a3s[step], tp), SPANS):
+        half = 0.5 * tb[step][0:1]
+        store_frames(a3, [silu_half(pre[...] + half) for pre in (sides.at[0], here.at[0], sides.at[1])])
+        for update, (a, b) in zip(packed_update(a3[...], tp), SPANS):
             prefix[step + 1, a:b] = prefix[step, a:b] + 0.25 * (update + noise[step, a:b].astype(F32))
         return carry
 
@@ -287,7 +330,7 @@
     return jnp.concatenate([vector, vector[:, 256:320]], axis=1)
 
 
-def second_sweep_kernel(first, states, above, below, far, mine, gain_ref, bias_ref, wp, tb, *refs):
+def second_sweep_kernel(first, states, above, below, far, mine, gain_ref, bias_ref, wp, wt, tb, *refs):
     if first:
         earlier, out, total, taps, scales = refs
     else:
@@ -329,10 +372,13 @@
             bottom = jnp.where(x < 3, bottom, 0.0)
             tiles.append(jnp.concatenate([top, middle, bottom], axis=0))
         store_taps(taps, tiles)
-        activated = silu(conv_rows(taps, wp) + tb[step][0:1])
+        bias_here = tb[step][0:1]
+        main = (conv_row(taps, wp, 0) + conv_row(taps, wp, 1)) + conv_row(taps, wp, 2)
+        activated = silu(main + bias_here[:, 0:256])
+        tail = silu(conv_tail(taps, wt) + bias_here[:, 256:320])
         out[local_step, 0:256] = activated[:, 0:128].astype(BF16)
         out[local_step, 256:512] = activated[:, 128:256].astype(BF16)
-        out[local_step, 512:640] = pack_tail(activated[:, 256:320]).astype(BF16)
+        out[local_step, 512:640] = pack_tail(tail).astype(BF16)
         return carry
 
     lax.fori_loop(0, 2, one_step, 0)
@@ -468,28 +514,34 @@
         sems=7,
     )
     arrived = swap_x(outgoing)
-    nq, sp, wp, tp, tew = call(
-        norm_start_kernel,
-        [((800, 128), BF16), (packed, BF16), ((3, 1024, 320), BF16), ((1024, 320), BF16), ((320, 320), BF16)],
-        spatial_weight, temporal_weight, temb_weight, start, gain, bias,
-        hbm=3,
-        sems=25,
-    )
+    nq, sp = call(norm_start_kernel, [((800, 128), BF16), (packed, BF16)], start, gain, bias)
     before, after = along_frame(nq, 1), along_frame(nq, -1)
     taps = ((320, 1024), BF16)
     a3 = ((256, 1024), BF16)
     pre = (256, 320)
-    here = call(first_conv_kernel, [((1,) + pre, F32)], nq, wp, scratch=(taps,), flops=512 * 320 * 2880)[0]
-    sides = call(first_conv_kernel, [((2,) + pre, F32)], before, after, wp, scratch=(taps,), flops=1024 * 320 * 2880)[0]
-    rt, noises, tb, a3s = call(
+    here, wp, wt, tp, tew = call(
+        first_own_kernel,
+        [((1,) + pre, F32), ((3, 1024, 320), BF16), ((1024, 192), BF16), ((1024, 320), BF16), ((320, 320), BF16)],
+        spatial_weight, temporal_weight, temb_weight, nq,
+        scratch=(taps,),
+        flops=512 * 320 * 2880,
+        hbm=3,
+        sems=25,
+    )
+    sides = call(
+        first_sides_kernel, [((2,) + pre, F32)], before, after, wp, wt, scratch=(taps,), flops=1024 * 320 * 2880
+    )[0]
+    rt, noises, tb = call(
         first_total_kernel,
-        [(packed, BF16), (four, BF16), ((4, 16, 320), F32), ((4, 256, 1024), BF16)],
+        [(packed, BF16), (four, BF16), ((4, 16, 320), F32)],
         here, sides, tp, tew, *arrived,
-        scratch=(((3, 256, 320), F32), a3),
+        scratch=(a3, ((3, 256, 64), F32)),
         flops=512 * 320 * 960,
     )
     totals = gather_y(rt)
-    prefix = call(first_prefix_kernel, [(four, F32)], a3s, tp, noises, flops=3 * 512 * 320 * 960)[0]
+    prefix = call(
+        first_prefix_kernel, [(four, F32)], here, sides, tb, tp, noises, scratch=(a3,), flops=1536 * 320 * 960
+    )[0]
     states, up, down, far = call(
         states_kernel,
         [(four, BF16), ((464, 128), BF16), ((464, 128), BF16), ((72, 128), BF16)],
@@ -501,7 +553,7 @@
         own, *total = call(
             functools.partial(second_sweep_kernel, 2 * half),
             outs + [(packed, BF16)] * half,
-            states, *edges, gain, bias, wp, tb, *earlier,
+            states, *edges, gain, bias, wp, wt, tb, *earlier,
             scratch=(taps, ((4, 8, 384), F32)),
             flops=1024 * 320 * 2880,
         )

time: 89.5 us -> 85.4 us (0.954)
  Pallas kernels: 21.4 us -> 19.1 us
  waiting for transfers between devices: 36.4 us -> 34.7 us
    pallas_call x13, Pallas kernels: 21.4 us -> 19.1 us  [call(): pl.pallas_call(body, out_shape=shapes, in_specs=[pl.BlockSpec(memory_spac...]
    ppermute x23, waiting for transfers between devices: 36.4 us -> 34.7 us  [moved(): return lax.ppermute(value, AXES, pairs)]
  transfers between devices with their start and end apart: 23 -> 23, of which waited for: 14 -> 14; matrix products, arithmetic and copies ran while one was open for 0% -> 0% of each run, Pallas kernels for 7% -> 9%
where the time goes in v3:
time: 85.4 us; the launch traced here: 85.3 us
  waiting for transfers between devices  34.7 us (41%)
  starting transfers between devices  30.6 us (36%)
  Pallas kernels  19.1 us (22%)
    ppermute x23, waiting for transfers between devices, moved(): return lax.ppermute(value, AXES, pairs)  34.7 us
    ppermute x23, starting transfers between devices, moved(): return lax.ppermute(value, AXES, pairs)  30.6 us
    pallas_call x13, Pallas kernels, call(): pl.pallas_call(body, out_shape=shapes, in_specs=[pl.BlockSpec(memory_spac...  19.1 us
  transfers between devices with their start and end apart: 23, of which 14 were waited for; matrix products, arithmetic and copies ran while one was open for 0% of the time, Pallas kernels for 9%

profile of v3, /device:TPU:6, one launch (start us, length us, event | category | flops | bytes accessed | tf_op | source)
XLA Modules:
  0.0 85.3 jit_solution(9458924620356903082)
XLA Ops:
  0.7 0.1 sine_convert_fusion
  0.7 0.1 fusion.2
  0.8 1.6 %shard_map.82 = (bf16[688,128]{1,0:T(8,128)(2,1)S(1)}, bf16[688,128]{1,0:T(8,128)(2,1)S(1)}, bf16[688,128]{1,0:T(8,128)(2,1)S(1)}, bf16[688,128]{1,0:T(8,128)(2,...) custom-call(bf16[1024,320]{1,0:T(8,128)(2,1)} %bitcast.4, bf16[1024,320]{1,0:T(8,128)(2,1)} %bitcast.5, ...), custom_call_target="tpu_custom_call" | custom-call | bytes 2688000 | tf_op jit(solution)/shard_map/pallas_call | solution.py:446
  2.4 0.9 %shard_map.83 = (bf16[800,128]{1,0:T(8,128)(2,1)S(1)}, bf16[640,128]{1,0:T(8,128)(2,1)S(1)}) custom-call(bf16[1024,320]{1,0:T(8,128)(2,1)S(1)} %get-tuple-element.32.start, f32[320]{0:T(512)S(1)} %get-tuple-element.33.gain_ref, f32[320]{0:T(512)S(1)} %get-tuple-element.34.bias_ref), custom_call_target="tpu_custom_call" | custom-call | bytes 1026560 | tf_op jit(solution)/shard_map/pallas_call | solution.py:446
  3.3 5.3 %collective-permute-start.1 = (bf16[800,128]{1,0:T(8,128)(2,1)S(1)}, bf16[800,128]{1,0:T(8,128)(2,1)S(1)}, u32[]{:S(2)}, u32[]{:S(2)}) collective-permute-start(bf16[800,128]{1,0:T(8,128)(2,1)S(1)} %get-tuple-element.36.normed), channel_id=1, source_target_pairs={{0,15},{1,0},{2,1},{3,2},{4,3},{5,4},{6,5},{7,6},{8,7},{9,8},{10,9... | collective-permute-start | bytes 614408 | tf_op jit(solution)/shard_map/ppermute | solution.py:465
  8.6 0.0 collective-permute-start
  8.6 0.5 collective-permute-start.2
  9.1 2.4 %collective-permute-start.3 = (bf16[688,128]{1,0:T(8,128)(2,1)S(1)}, bf16[688,128]{1,0:T(8,128)(2,1)S(1)}, u32[]{:S(2)}, u32[]{:S(2)}) collective-permute-start(bf16[688,128]{1,0:T(8,128)(2,1)S(1)} %get-tuple-element.44), channel_id=1, source_target_pairs={{0,32},{1,33},{2,34},{3,35},{4,36},{5,37},{6,38},{7,39},{8,40},{9,... | collective-permute-start | bytes 528392 | tf_op jit(solution)/shard_map/ppermute | solution.py:465
  11.5 0.0 collective-permute-start.4
  11.5 2.8 %shard_map.84 = (f32[1,256,320]{2,1,0:T(8,128)S(1)}, bf16[3,1024,320]{2,1,0:T(8,128)(2,1)S(1)}, bf16[1024,192]{1,0:T(8,128)(2,1)S(1)}, bf16[1024,320]{1,0:T(8,128)(2,1)S(1)}, bf16[320,320]{1,0:T(8,128)(2,1)S(1)}) custom-call(bf16[3,3,320,320]{3,2,1,0:T(8,128)(2,1)} %sw.1, bf16[3,320,320]{2,1,0:T(8,128)(2,1)} %tw.1, bf16[320,320]{1,0:T(8,128)(2,1)} %tew_hbm.1, ...), custom_call_target="tpu_custom_call" | custom-call | flops 471859200 | bytes 6414336 | tf_op jit(solution)/shard_map/pallas_call | solution.py:446
  14.3 0.0 collective-permute-done.1.after
  14.3 0.7 collective-permute-done.before
  15.0 1.6 %shard_map.85.sides = f32[2,256,320]{2,1,0:T(8,128)S(1)} custom-call(bf16[800,128]{1,0:T(8,128)(2,1)S(1)} %collective-permute-done.before, bf16[800,128]{1,0:T(8,128)(2,1)S(1)} %collective-permute-done.1.after, bf16[3,1024,320]{2,1,0:T(8,128)(2,1)S(1)} %get-tuple-element.38.wp, bf16[1024,192]{1,0:T(8,128)(2,1)S(1)} %get-tuple-element.39.wt), custom_call_target="tpu_custom_call" | custom-call | flops 943718400 | bytes 3424256 | tf_op jit(solution)/shard_map/pallas_call | solution.py:446
  16.6 0.0 collective-permute-done.2.n1
  16.6 0.0 collective-permute-done.3.n2
  16.6 1.6 %collective-permute-done.4.n3 = bf16[688,128]{1,0:T(8,128)(2,1)S(1)} collective-permute-done((bf16[688,128]{1,0:T(8,128)(2,1)S(1)}, bf16[688,128]{1,0:T(8,128)(2,1)S(1)}, u32[]{:S(2)}, u32[]{:S(2)}) %collective-permute-start.4) | collective-permute-done | bytes 176160 | tf_op jit(solution)/shard_map/ppermute | solution.py:465
  18.2 1.6 %shard_map.86 = (bf16[640,128]{1,0:T(8,128)(2,1)S(1)}, bf16[4,640,128]{2,1,0:T(8,128)(2,1)S(1)}, f32[4,16,320]{2,1,0:T(8,128)S(1)}) custom-call(f32[1,256,320]{2,1,0:T(8,128)S(1)} %get-tuple-element.37.here, f32[2,256,320]{2,1,0:T(8,128)S(1)} %shard_map.85.sides, bf16[1024,320]{1,0:T(8,128)(2,1)S(1)} %get-tuple-element.40.tp, ...), custom_call_target="tpu_custom_call" | custom-call | flops 157286400 | bytes 3448832 | tf_op jit(solution)/shard_map/pallas_call | solution.py:446
  19.8 3.1 %collective-permute-start.7 = (bf16[640,128]{1,0:T(8,128)(2,1)S(1)}, bf16[640,128]{1,0:T(8,128)(2,1)S(1)}, u32[]{:S(2)}, u32[]{:S(2)}) collective-permute-start(bf16[640,128]{1,0:T(8,128)(2,1)S(1)} %get-tuple-element.48), channel_id=1, source_target_pairs={{0,192},{1,65},{2,194},{3,67},{4,196},{5,69},{6,198},{7,71},{8,200... | collective-permute-start | bytes 491528 | tf_op jit(solution)/shard_map/ppermute | solution.py:465
  22.8 0.6 collective-permute-start.6
  23.5 1.0 %collective-permute-start.5 = (bf16[640,128]{1,0:T(8,128)(2,1)S(1)}, bf16[640,128]{1,0:T(8,128)(2,1)S(1)}, u32[]{:S(2)}, u32[]{:S(2)}) collective-permute-start(bf16[640,128]{1,0:T(8,128)(2,1)S(1)} %get-tuple-element.48), channel_id=1, source_target_pairs={{0,64},{1,193},{2,66},{3,195},{4,68},{5,197},{6,70},{7,199},{8,72}... | collective-permute-start | bytes 491528 | tf_op jit(solution)/shard_map/ppermute | solution.py:465
  24.4 1.5 %shard_map.87.prefix = f32[4,640,128]{2,1,0:T(8,128)S(1)} custom-call(f32[1,256,320]{2,1,0:T(8,128)S(1)} %get-tuple-element.37.here, f32[2,256,320]{2,1,0:T(8,128)S(1)} %shard_map.85.sides, f32[4,16,320]{2,1,0:T(8,128)S(1)} %get-tuple-element.46.tb, bf16[1024,320]{1,0:T(8,128)(2,1)S(1)} %get-tuple-element.40.tp, bf16[4,640,128]{2,1,0:T(8,128)(2,1)S(1)} %get-tuple-element.47.noise), custom_call_target="tpu_custom_call" | custom-call | flops 471859200 | bytes 3686400 | tf_op jit(solution)/shard_map/pallas_call | solution.py:446
  26.0 0.7 collective-permute-done.7.r3
  26.7 3.0 %collective-permute-done.6.r2 = bf16[640,128]{1,0:T(8,128)(2,1)S(1)} collective-permute-done((bf16[640,128]{1,0:T(8,128)(2,1)S(1)}, bf16[640,128]{1,0:T(8,128)(2,1)S(1)}, u32[]{:S(2)}, u32[]{:S(2)}) %collective-permute-start.6) | collective-permute-done | bytes 163872 | tf_op jit(solution)/shard_map/ppermute | solution.py:465
  29.8 1.7 %collective-permute-done.5.r1 = bf16[640,128]{1,0:T(8,128)(2,1)S(1)} collective-permute-done((bf16[640,128]{1,0:T(8,128)(2,1)S(1)}, bf16[640,128]{1,0:T(8,128)(2,1)S(1)}, u32[]{:S(2)}, u32[]{:S(2)}) %collective-permute-start.5) | collective-permute-done | bytes 163872 | tf_op jit(solution)/shard_map/ppermute | solution.py:465
  31.4 1.1 %shard_map.88 = (bf16[4,640,128]{2,1,0:T(8,128)(2,1)S(1)}, bf16[464,128]{1,0:T(8,128)(2,1)S(1)}, bf16[464,128]{1,0:T(8,128)(2,1)S(1)}, bf16[72,128]{1,0:T(8,128)(2,1)S(1)}) custom-call(bf16[640,128]{1,0:T(8,128)(2,1)S(1)} %get-tuple-element.35.sp, f32[4,640,128]{2,1,0:T(8,128)S(1)} %shard_map.87.prefix, bf16[640,128]{1,0:T(8,128)(2,1)S(1)} %collective-permute-done.5.r1, ...), custom_call_target="tpu_custom_call" | custom-call | bytes 2877440 | tf_op jit(solution)/shard_map/pallas_call | solution.py:446
  32.5 1.9 %collective-permute-start.8 = (bf16[464,128]{1,0:T(8,128)(2,1)S(1)}, bf16[464,128]{1,0:T(8,128)(2,1)S(1)}, u32[]{:S(2)}, u32[]{:S(2)}) collective-permute-start(bf16[464,128]{1,0:T(8,128)(2,1)S(1)} %get-tuple-element.50), channel_id=1, source_target_pairs={{0,16},{1,17},{2,18},{3,19},{4,20},{5,21},{6,22},{7,23},{8,24},{9,... | collective-permute-start | bytes 356360 | tf_op jit(solution)/shard_map/ppermute | solution.py:465
  34.3 0.2 collective-permute-start.9
  34.5 1.8 %collective-permute-start.10 = (bf16[72,128]{1,0:T(8,128)(2,1)S(1)}, bf16[72,128]{1,0:T(8,128)(2,1)S(1)}, u32[]{:S(2)}, u32[]{:S(2)}) collective-permute-start(bf16[72,128]{1,0:T(8,128)(2,1)S(1)} %get-tuple-element.52.mine), channel_id=1, source_target_pairs={{0,32},{1,33},{2,34},{3,35},{4,36},{5,37},{6,38},{7,39},{8,40},{9,... | collective-permute-start | bytes 55304 | tf_op jit(solution)/shard_map/ppermute | solution.py:465
  36.3 3.6 %collective-permute-done.10.far = bf16[72,128]{1,0:T(8,128)(2,1)S(1)} collective-permute-done((bf16[72,128]{1,0:T(8,128)(2,1)S(1)}, bf16[72,128]{1,0:T(8,128)(2,1)S(1)}, u32[]{:S(2)}, u32[]{:S(2)}) %collective-permute-start.10) | collective-permute-done | bytes 18464 | tf_op jit(solution)/shard_map/ppermute | solution.py:465
  39.9 0.0 collective-permute-done.8.above
  39.9 0.7 collective-permute-done.9.below
  40.6 2.3 %shard_map.89.refs_0_.own0 = bf16[2,640,128]{2,1,0:T(8,128)(2,1)S(1)} custom-call(bf16[4,640,128]{2,1,0:T(8,128)(2,1)S(1)} %get-tuple-element.49.states, bf16[464,128]{1,0:T(8,128)(2,1)S(1)} %collective-permute-done.8.above, bf16[464,128]{1,0:T(8,128)(2,1)S(1)} %collective-permute-done.9.below, bf16[72,128]{1,0:T(8,128)(2,1)S(1)} %collective-permute-done.10.far, ...), custom_call_target="tpu_custom_call" | custom-call | flops 943718400 | bytes 3701248 | tf_op jit(solution)/shard_map/pallas_call | solution.py:446
  42.9 2.4 %shard_map.90 = (bf16[2,640,128]{2,1,0:T(8,128)(2,1)S(1)}, bf16[640,128]{1,0:T(8,128)(2,1)S(1)}) custom-call(bf16[4,640,128]{2,1,0:T(8,128)(2,1)S(1)} %get-tuple-element.49.states, bf16[464,128]{1,0:T(8,128)(2,1)S(1)} %collective-permute-done.8.above, bf16[464,128]{1,0:T(8,128)(2,1)S(1)} %collective-permute-done.9.below, ...), custom_call_target="tpu_custom_call" | custom-call | flops 943718400 | bytes 4192768 | tf_op jit(solution)/shard_map/pallas_call | solution.py:446
  45.3 1.3 %collective-permute-start.16 = (bf16[640,128]{1,0:T(8,128)(2,1)S(1)}, bf16[640,128]{1,0:T(8,128)(2,1)S(1)}, u32[]{:S(2)}, u32[]{:S(2)}) collective-permute-start(bf16[640,128]{1,0:T(8,128)(2,1)S(1)} %get-tuple-element.54.own), channel_id=1, source_target_pairs={{0,15},{1,0},{2,1},{3,2},{4,3},{5,4},{6,5},{7,6},{8,7},{9,8},{10,9... | collective-permute-start | bytes 491528 | tf_op jit(solution)/shard_map/ppermute | solution.py:465
  46.6 2.9 %collective-permute-start.14 = (bf16[2,640,128]{2,1,0:T(8,128)(2,1)S(1)}, bf16[2,640,128]{2,1,0:T(8,128)(2,1)S(1)}, u32[]{:S(2)}, u32[]{:S(2)}) collective-permute-start(bf16[2,640,128]{2,1,0:T(8,128)(2,1)S(1)} %get-tuple-element.53.own1), channel_id=1, source_target_pairs={{0,15},{1,0},{2,1},{3,2},{4,3},{5,4},{6,5},{7,6},{8,7},{9,8},{10,9... | collective-permute-start | bytes 983048 | tf_op jit(solution)/shard_map/ppermute | solution.py:465
  49.5 0.0 collective-permute-start.12
  49.5 3.0 %collective-permute-start.13 = (bf16[2,640,128]{2,1,0:T(8,128)(2,1)S(1)}, bf16[2,640,128]{2,1,0:T(8,128)(2,1)S(1)}, u32[]{:S(2)}, u32[]{:S(2)}) collective-permute-start(bf16[2,640,128]{2,1,0:T(8,128)(2,1)S(1)} %shard_map.89.refs_0_.own0), channel_id=1, source_target_pairs={{0,15},{1,0},{2,1},{3,2},{4,3},{5,4},{6,5},{7,6},{8,7},{9,8},{10,9... | collective-permute-start | bytes 983048 | tf_op jit(solution)/shard_map/ppermute | solution.py:465
  52.4 0.0 collective-permute-start.11
  52.4 0.0 collective-permute-done.16.after
  52.4 0.0 collective-permute-start.15
  52.5 10.0 %collective-permute-done.15.before = bf16[640,128]{1,0:T(8,128)(2,1)S(1)} collective-permute-done((bf16[640,128]{1,0:T(8,128)(2,1)S(1)}, bf16[640,128]{1,0:T(8,128)(2,1)S(1)}, u32[]{:S(2)}, u32[]{:S(2)}) %collective-permute-start.15) | collective-permute-done | bytes 163872 | tf_op jit(solution)/shard_map/ppermute | solution.py:465
  62.5 0.5 shard_map.92
  63.0 2.4 %collective-permute-start.19 = (bf16[640,128]{1,0:T(8,128)(2,1)S(1)}, bf16[640,128]{1,0:T(8,128)(2,1)S(1)}, u32[]{:S(2)}, u32[]{:S(2)}) collective-permute-start(bf16[640,128]{1,0:T(8,128)(2,1)S(1)} %shard_map.92), channel_id=1, source_target_pairs={{0,192},{1,65},{2,194},{3,67},{4,196},{5,69},{6,198},{7,71},{8,200... | collective-permute-start | bytes 491528 | tf_op jit(solution)/shard_map/ppermute | solution.py:465
  65.4 0.0 collective-permute-done.14.after1
  65.4 1.2 %collective-permute-start.18 = (bf16[640,128]{1,0:T(8,128)(2,1)S(1)}, bf16[640,128]{1,0:T(8,128)(2,1)S(1)}, u32[]{:S(2)}, u32[]{:S(2)}) collective-permute-start(bf16[640,128]{1,0:T(8,128)(2,1)S(1)} %shard_map.92), channel_id=1, source_target_pairs={{0,128},{1,129},{2,130},{3,131},{4,132},{5,133},{6,134},{7,135},{8... | collective-permute-start | bytes 491528 | tf_op jit(solution)/shard_map/ppermute | solution.py:465
  66.6 0.0 collective-permute-done.12.before1
  66.6 0.0 collective-permute-start.17
  66.6 0.0 collective-permute-done.13.after0
  66.6 0.0 collective-permute-done.11.before0
  66.6 1.6 %shard_map.91.prefix = f32[4,640,128]{2,1,0:T(8,128)S(1)} custom-call(bf16[2,640,128]{2,1,0:T(8,128)(2,1)S(1)} %shard_map.89.refs_0_.own0, bf16[2,640,128]{2,1,0:T(8,128)(2,1)S(1)} %get-tuple-element.53.own1, bf16[2,640,128]{2,1,0:T(8,128)(2,1)S(1)} %collective-permute-done.11.before0, bf16[2,640,128]{2,1,0:T(8,128)(2,1)S(1)} %collective-permute-done.12.before1, ...), custom_call_target="tpu_custom_call" | custom-call | flops 629145600 | bytes 4587520 | tf_op jit(solution)/shard_map/pallas_call | solution.py:446
  68.2 1.8 %collective-permute-done.19.r3 = bf16[640,128]{1,0:T(8,128)(2,1)S(1)} collective-permute-done((bf16[640,128]{1,0:T(8,128)(2,1)S(1)}, bf16[640,128]{1,0:T(8,128)(2,1)S(1)}, u32[]{:S(2)}, u32[]{:S(2)}) %collective-permute-start.19) | collective-permute-done | bytes 163872 | tf_op jit(solution)/shard_map/ppermute | solution.py:465
  70.0 2.3 %collective-permute-done.18.r2 = bf16[640,128]{1,0:T(8,128)(2,1)S(1)} collective-permute-done((bf16[640,128]{1,0:T(8,128)(2,1)S(1)}, bf16[640,128]{1,0:T(8,128)(2,1)S(1)}, u32[]{:S(2)}, u32[]{:S(2)}) %collective-permute-start.18) | collective-permute-done | bytes 163872 | tf_op jit(solution)/shard_map/ppermute | solution.py:465
  72.3 1.7 %collective-permute-done.17.r1 = bf16[640,128]{1,0:T(8,128)(2,1)S(1)} collective-permute-done((bf16[640,128]{1,0:T(8,128)(2,1)S(1)}, bf16[640,128]{1,0:T(8,128)(2,1)S(1)}, u32[]{:S(2)}, u32[]{:S(2)}) %collective-permute-start.17) | collective-permute-done | bytes 163872 | tf_op jit(solution)/shard_map/ppermute | solution.py:465
  73.9 0.2 shard_map.93
  74.2 1.5 %collective-permute-start.20 = (bf16[640,128]{1,0:T(8,128)(2,1)S(1)}, bf16[640,128]{1,0:T(8,128)(2,1)S(1)}, u32[]{:S(2)}, u32[]{:S(2)}) collective-permute-start(bf16[640,128]{1,0:T(8,128)(2,1)S(1)} %get-tuple-element.56), channel_id=1, source_target_pairs={{0,16},{1,49},{2,18},{3,51},{4,20},{5,53},{6,22},{7,55},{8,24},{9,... | collective-permute-start | bytes 491528 | tf_op jit(solution)/shard_map/ppermute | solution.py:465
  75.7 0.6 collective-permute-start.21
  76.3 1.0 %collective-permute-start.22 = (bf16[640,128]{1,0:T(8,128)(2,1)S(1)}, bf16[640,128]{1,0:T(8,128)(2,1)S(1)}, u32[]{:S(2)}, u32[]{:S(2)}) collective-permute-start(bf16[640,128]{1,0:T(8,128)(2,1)S(1)} %get-tuple-element.58), channel_id=1, source_target_pairs={{0,48},{1,17},{2,50},{3,19},{4,52},{5,21},{6,54},{7,23},{8,56},{9,... | collective-permute-start | bytes 491528 | tf_op jit(solution)/shard_map/ppermute | solution.py:465
  77.3 2.3 %collective-permute-done.20.r1 = bf16[640,128]{1,0:T(8,128)(2,1)S(1)} collective-permute-done((bf16[640,128]{1,0:T(8,128)(2,1)S(1)}, bf16[640,128]{1,0:T(8,128)(2,1)S(1)}, u32[]{:S(2)}, u32[]{:S(2)}) %collective-permute-start.20) | collective-permute-done | bytes 163872 | tf_op jit(solution)/shard_map/ppermute | solution.py:465
  79.6 3.0 %collective-permute-done.21.r2 = bf16[640,128]{1,0:T(8,128)(2,1)S(1)} collective-permute-done((bf16[640,128]{1,0:T(8,128)(2,1)S(1)}, bf16[640,128]{1,0:T(8,128)(2,1)S(1)}, u32[]{:S(2)}, u32[]{:S(2)}) %collective-permute-start.21) | collective-permute-done | bytes 163872 | tf_op jit(solution)/shard_map/ppermute | solution.py:465
  82.6 1.7 %collective-permute-done.22.r3 = bf16[640,128]{1,0:T(8,128)(2,1)S(1)} collective-permute-done((bf16[640,128]{1,0:T(8,128)(2,1)S(1)}, bf16[640,128]{1,0:T(8,128)(2,1)S(1)}, u32[]{:S(2)}, u32[]{:S(2)}) %collective-permute-start.22) | collective-permute-done | bytes 163872 | tf_op jit(solution)/shard_map/ppermute | solution.py:465
  84.2 1.0 %shard_map.94 = bf16[1024,320]{1,0:T(8,128)(2,1)} custom-call(bf16[640,128]{1,0:T(8,128)(2,1)S(1)} %get-tuple-element.55.r0, bf16[640,128]{1,0:T(8,128)(2,1)S(1)} %collective-permute-done.20.r1, bf16[640,128]{1,0:T(8,128)(2,1)S(1)} %collective-permute-done.21.r2, bf16[640,128]{1,0:T(8,128)(2,1)S(1)} %collective-permute-done.22.r3), custom_call_target="tpu_custom_call" | custom-call | bytes 1310720 | tf_op jit(solution)/shard_map/pallas_call | solution.py:446
  (1 shorter events, 0.0 us)
Async XLA Ops:
  3.3 11.0 %collective-permute-start.1 = (bf16[800,128]{1,0:T(8,128)(2,1)S(1)}, bf16[800,128]{1,0:T(8,128)(2,1)S(1)}, u32[]{:S(2)}, u32[]{:S(2)}) collective-permute-start(bf16[800,128]{1,0:T(8,128)(2,1)S(1)} %get-tuple-element.36.normed), channel_id=1, source_target_pairs={{0,15},{1,0},{2,1},{3,2},{4,3},{5,4},{6,5},{7,6},{8,7},{9,8},{10,9... | collective-permute-start | bytes 614408 | tf_op jit(solution)/shard_map/ppermute | solution.py:465
  8.6 6.4 %collective-permute-start = (bf16[800,128]{1,0:T(8,128)(2,1)S(1)}, bf16[800,128]{1,0:T(8,128)(2,1)S(1)}, u32[]{:S(2)}, u32[]{:S(2)}) collective-permute-start(bf16[800,128]{1,0:T(8,128)(2,1)S(1)} %get-tuple-element.36.normed), channel_id=1, source_target_pairs={{0,1},{1,2},{2,3},{3,4},{4,5},{5,6},{6,7},{7,8},{8,9},{9,10},{10,1... | collective-permute-start | bytes 614408 | tf_op jit(solution)/shard_map/ppermute | solution.py:465
  8.6 8.0 %collective-permute-start.2 = (bf16[688,128]{1,0:T(8,128)(2,1)S(1)}, bf16[688,128]{1,0:T(8,128)(2,1)S(1)}, u32[]{:S(2)}, u32[]{:S(2)}) collective-permute-start(bf16[688,128]{1,0:T(8,128)(2,1)S(1)} %get-tuple-element.43), channel_id=1, source_target_pairs={{0,16},{1,49},{2,18},{3,51},{4,20},{5,53},{6,22},{7,55},{8,24},{9,... | collective-permute-start | bytes 528392 | tf_op jit(solution)/shard_map/ppermute | solution.py:465
  9.1 7.5 %collective-permute-start.3 = (bf16[688,128]{1,0:T(8,128)(2,1)S(1)}, bf16[688,128]{1,0:T(8,128)(2,1)S(1)}, u32[]{:S(2)}, u32[]{:S(2)}) collective-permute-start(bf16[688,128]{1,0:T(8,128)(2,1)S(1)} %get-tuple-element.44), channel_id=1, source_target_pairs={{0,32},{1,33},{2,34},{3,35},{4,36},{5,37},{6,38},{7,39},{8,40},{9,... | collective-permute-start | bytes 528392 | tf_op jit(solution)/shard_map/ppermute | solution.py:465
  11.5 6.7 %collective-permute-start.4 = (bf16[688,128]{1,0:T(8,128)(2,1)S(1)}, bf16[688,128]{1,0:T(8,128)(2,1)S(1)}, u32[]{:S(2)}, u32[]{:S(2)}) collective-permute-start(bf16[688,128]{1,0:T(8,128)(2,1)S(1)} %get-tuple-element.45), channel_id=1, source_target_pairs={{0,48},{1,17},{2,50},{3,19},{4,52},{5,21},{6,54},{7,23},{8,56},{9,... | collective-permute-start | bytes 528392 | tf_op jit(solution)/shard_map/ppermute | solution.py:465
  19.8 7.0 %collective-permute-start.7 = (bf16[640,128]{1,0:T(8,128)(2,1)S(1)}, bf16[640,128]{1,0:T(8,128)(2,1)S(1)}, u32[]{:S(2)}, u32[]{:S(2)}) collective-permute-start(bf16[640,128]{1,0:T(8,128)(2,1)S(1)} %get-tuple-element.48), channel_id=1, source_target_pairs={{0,192},{1,65},{2,194},{3,67},{4,196},{5,69},{6,198},{7,71},{8,200... | collective-permute-start | bytes 491528 | tf_op jit(solution)/shard_map/ppermute | solution.py:465
  22.8 6.9 %collective-permute-start.6 = (bf16[640,128]{1,0:T(8,128)(2,1)S(1)}, bf16[640,128]{1,0:T(8,128)(2,1)S(1)}, u32[]{:S(2)}, u32[]{:S(2)}) collective-permute-start(bf16[640,128]{1,0:T(8,128)(2,1)S(1)} %get-tuple-element.48), channel_id=1, source_target_pairs={{0,128},{1,129},{2,130},{3,131},{4,132},{5,133},{6,134},{7,135},{8... | collective-permute-start | bytes 491528 | tf_op jit(solution)/shard_map/ppermute | solution.py:465
  23.5 8.0 %collective-permute-start.5 = (bf16[640,128]{1,0:T(8,128)(2,1)S(1)}, bf16[640,128]{1,0:T(8,128)(2,1)S(1)}, u32[]{:S(2)}, u32[]{:S(2)}) collective-permute-start(bf16[640,128]{1,0:T(8,128)(2,1)S(1)} %get-tuple-element.48), channel_id=1, source_target_pairs={{0,64},{1,193},{2,66},{3,195},{4,68},{5,197},{6,70},{7,199},{8,72}... | collective-permute-start | bytes 491528 | tf_op jit(solution)/shard_map/ppermute | solution.py:465
  32.5 7.4 %collective-permute-start.8 = (bf16[464,128]{1,0:T(8,128)(2,1)S(1)}, bf16[464,128]{1,0:T(8,128)(2,1)S(1)}, u32[]{:S(2)}, u32[]{:S(2)}) collective-permute-start(bf16[464,128]{1,0:T(8,128)(2,1)S(1)} %get-tuple-element.50), channel_id=1, source_target_pairs={{0,16},{1,17},{2,18},{3,19},{4,20},{5,21},{6,22},{7,23},{8,24},{9,... | collective-permute-start | bytes 356360 | tf_op jit(solution)/shard_map/ppermute | solution.py:465
  34.3 6.2 %collective-permute-start.9 = (bf16[464,128]{1,0:T(8,128)(2,1)S(1)}, bf16[464,128]{1,0:T(8,128)(2,1)S(1)}, u32[]{:S(2)}, u32[]{:S(2)}) collective-permute-start(bf16[464,128]{1,0:T(8,128)(2,1)S(1)} %get-tuple-element.51), channel_id=1, source_target_pairs={{0,48},{1,49},{2,50},{3,51},{4,52},{5,53},{6,54},{7,55},{8,56},{9,... | collective-permute-start | bytes 356360 | tf_op jit(solution)/shard_map/ppermute | solution.py:465
  34.5 5.4 %collective-permute-start.10 = (bf16[72,128]{1,0:T(8,128)(2,1)S(1)}, bf16[72,128]{1,0:T(8,128)(2,1)S(1)}, u32[]{:S(2)}, u32[]{:S(2)}) collective-permute-start(bf16[72,128]{1,0:T(8,128)(2,1)S(1)} %get-tuple-element.52.mine), channel_id=1, source_target_pairs={{0,32},{1,33},{2,34},{3,35},{4,36},{5,37},{6,38},{7,39},{8,40},{9,... | collective-permute-start | bytes 55304 | tf_op jit(solution)/shard_map/ppermute | solution.py:465
  45.3 7.2 %collective-permute-start.16 = (bf16[640,128]{1,0:T(8,128)(2,1)S(1)}, bf16[640,128]{1,0:T(8,128)(2,1)S(1)}, u32[]{:S(2)}, u32[]{:S(2)}) collective-permute-start(bf16[640,128]{1,0:T(8,128)(2,1)S(1)} %get-tuple-element.54.own), channel_id=1, source_target_pairs={{0,15},{1,0},{2,1},{3,2},{4,3},{5,4},{6,5},{7,6},{8,7},{9,8},{10,9... | collective-permute-start | bytes 491528 | tf_op jit(solution)/shard_map/ppermute | solution.py:465
  46.6 18.8 %collective-permute-start.14 = (bf16[2,640,128]{2,1,0:T(8,128)(2,1)S(1)}, bf16[2,640,128]{2,1,0:T(8,128)(2,1)S(1)}, u32[]{:S(2)}, u32[]{:S(2)}) collective-permute-start(bf16[2,640,128]{2,1,0:T(8,128)(2,1)S(1)} %get-tuple-element.53.own1), channel_id=1, source_target_pairs={{0,15},{1,0},{2,1},{3,2},{4,3},{5,4},{6,5},{7,6},{8,7},{9,8},{10,9... | collective-permute-start | bytes 983048 | tf_op jit(solution)/shard_map/ppermute | solution.py:465
  49.5 17.1 %collective-permute-start.12 = (bf16[2,640,128]{2,1,0:T(8,128)(2,1)S(1)}, bf16[2,640,128]{2,1,0:T(8,128)(2,1)S(1)}, u32[]{:S(2)}, u32[]{:S(2)}) collective-permute-start(bf16[2,640,128]{2,1,0:T(8,128)(2,1)S(1)} %get-tuple-element.53.own1), channel_id=1, source_target_pairs={{0,1},{1,2},{2,3},{3,4},{4,5},{5,6},{6,7},{7,8},{8,9},{9,10},{10,1... | collective-permute-start | bytes 983048 | tf_op jit(solution)/shard_map/ppermute | solution.py:465
  49.5 17.1 %collective-permute-start.13 = (bf16[2,640,128]{2,1,0:T(8,128)(2,1)S(1)}, bf16[2,640,128]{2,1,0:T(8,128)(2,1)S(1)}, u32[]{:S(2)}, u32[]{:S(2)}) collective-permute-start(bf16[2,640,128]{2,1,0:T(8,128)(2,1)S(1)} %shard_map.89.refs_0_.own0), channel_id=1, source_target_pairs={{0,15},{1,0},{2,1},{3,2},{4,3},{5,4},{6,5},{7,6},{8,7},{9,8},{10,9... | collective-permute-start | bytes 983048 | tf_op jit(solution)/shard_map/ppermute | solution.py:465
  52.4 14.2 %collective-permute-start.11 = (bf16[2,640,128]{2,1,0:T(8,128)(2,1)S(1)}, bf16[2,640,128]{2,1,0:T(8,128)(2,1)S(1)}, u32[]{:S(2)}, u32[]{:S(2)}) collective-permute-start(bf16[2,640,128]{2,1,0:T(8,128)(2,1)S(1)} %shard_map.89.refs_0_.own0), channel_id=1, source_target_pairs={{0,1},{1,2},{2,3},{3,4},{4,5},{5,6},{6,7},{7,8},{8,9},{9,10},{10,1... | collective-permute-start | bytes 983048 | tf_op jit(solution)/shard_map/ppermute | solution.py:465
  52.4 10.0 %collective-permute-start.15 = (bf16[640,128]{1,0:T(8,128)(2,1)S(1)}, bf16[640,128]{1,0:T(8,128)(2,1)S(1)}, u32[]{:S(2)}, u32[]{:S(2)}) collective-permute-start(bf16[640,128]{1,0:T(8,128)(2,1)S(1)} %get-tuple-element.54.own), channel_id=1, source_target_pairs={{0,1},{1,2},{2,3},{3,4},{4,5},{5,6},{6,7},{7,8},{8,9},{9,10},{10,1... | collective-permute-start | bytes 491528 | tf_op jit(solution)/shard_map/ppermute | solution.py:465
  63.0 7.0 %collective-permute-start.19 = (bf16[640,128]{1,0:T(8,128)(2,1)S(1)}, bf16[640,128]{1,0:T(8,128)(2,1)S(1)}, u32[]{:S(2)}, u32[]{:S(2)}) collective-permute-start(bf16[640,128]{1,0:T(8,128)(2,1)S(1)} %shard_map.92), channel_id=1, source_target_pairs={{0,192},{1,65},{2,194},{3,67},{4,196},{5,69},{6,198},{7,71},{8,200... | collective-permute-start | bytes 491528 | tf_op jit(solution)/shard_map/ppermute | solution.py:465
  65.4 6.9 %collective-permute-start.18 = (bf16[640,128]{1,0:T(8,128)(2,1)S(1)}, bf16[640,128]{1,0:T(8,128)(2,1)S(1)}, u32[]{:S(2)}, u32[]{:S(2)}) collective-permute-start(bf16[640,128]{1,0:T(8,128)(2,1)S(1)} %shard_map.92), channel_id=1, source_target_pairs={{0,128},{1,129},{2,130},{3,131},{4,132},{5,133},{6,134},{7,135},{8... | collective-permute-start | bytes 491528 | tf_op jit(solution)/shard_map/ppermute | solution.py:465
  66.6 7.4 %collective-permute-start.17 = (bf16[640,128]{1,0:T(8,128)(2,1)S(1)}, bf16[640,128]{1,0:T(8,128)(2,1)S(1)}, u32[]{:S(2)}, u32[]{:S(2)}) collective-permute-start(bf16[640,128]{1,0:T(8,128)(2,1)S(1)} %shard_map.92), channel_id=1, source_target_pairs={{0,64},{1,193},{2,66},{3,195},{4,68},{5,197},{6,70},{7,199},{8,72}... | collective-permute-start | bytes 491528 | tf_op jit(solution)/shard_map/ppermute | solution.py:465
  74.2 5.4 %collective-permute-start.20 = (bf16[640,128]{1,0:T(8,128)(2,1)S(1)}, bf16[640,128]{1,0:T(8,128)(2,1)S(1)}, u32[]{:S(2)}, u32[]{:S(2)}) collective-permute-start(bf16[640,128]{1,0:T(8,128)(2,1)S(1)} %get-tuple-element.56), channel_id=1, source_target_pairs={{0,16},{1,49},{2,18},{3,51},{4,20},{5,53},{6,22},{7,55},{8,24},{9,... | collective-permute-start | bytes 491528 | tf_op jit(solution)/shard_map/ppermute | solution.py:465
  75.7 6.9 %collective-permute-start.21 = (bf16[640,128]{1,0:T(8,128)(2,1)S(1)}, bf16[640,128]{1,0:T(8,128)(2,1)S(1)}, u32[]{:S(2)}, u32[]{:S(2)}) collective-permute-start(bf16[640,128]{1,0:T(8,128)(2,1)S(1)} %get-tuple-element.57), channel_id=1, source_target_pairs={{0,32},{1,33},{2,34},{3,35},{4,36},{5,37},{6,38},{7,39},{8,40},{9,... | collective-permute-start | bytes 491528 | tf_op jit(solution)/shard_map/ppermute | solution.py:465
  76.3 7.9 %collective-permute-start.22 = (bf16[640,128]{1,0:T(8,128)(2,1)S(1)}, bf16[640,128]{1,0:T(8,128)(2,1)S(1)}, u32[]{:S(2)}, u32[]{:S(2)}) collective-permute-start(bf16[640,128]{1,0:T(8,128)(2,1)S(1)} %get-tuple-element.58), channel_id=1, source_target_pairs={{0,48},{1,17},{2,50},{3,19},{4,52},{5,21},{6,54},{7,23},{8,56},{9,... | collective-permute-start | bytes 491528 | tf_op jit(solution)/shard_map/ppermute | solution.py:465

commit v4 on v3

--- a/solution.py
+++ b/solution.py
@@ -1,4 +1,3 @@
-import functools
 import math
 
 import jax
@@ -330,11 +329,7 @@
     return jnp.concatenate([vector, vector[:, 256:320]], axis=1)
 
 
-def second_sweep_kernel(first, states, above, below, far, mine, gain_ref, bias_ref, wp, wt, tb, *refs):
-    if first:
-        earlier, out, total, taps, scales = refs
-    else:
-        out, taps, scales = refs
+def second_sweep_kernel(states, above, below, far, mine, gain_ref, bias_ref, wp, wt, tb, out, total, taps, scales):
     gain, bias = wide(gain_ref), wide(bias_ref)
     x = lax.axis_index("x")
     parts = [stats_of(mine, 0), stats_of(above, 384), stats_of(below, 384), stats_of(far, 0)]
@@ -347,8 +342,7 @@
         scales[step, 0:1] = mean[step : step + 1]
         scales[step, 1:2] = rstd[step : step + 1]
 
-    def one_step(local_step, carry):
-        step = local_step + first
+    def one_step(step, carry):
         here = scales[step]
 
         def normed(value, tile):
@@ -376,15 +370,14 @@
         main = (conv_row(taps, wp, 0) + conv_row(taps, wp, 1)) + conv_row(taps, wp, 2)
         activated = silu(main + bias_here[:, 0:256])
         tail = silu(conv_tail(taps, wt) + bias_here[:, 256:320])
-        out[local_step, 0:256] = activated[:, 0:128].astype(BF16)
-        out[local_step, 256:512] = activated[:, 128:256].astype(BF16)
-        out[local_step, 512:640] = pack_tail(tail).astype(BF16)
+        out[step, 0:256] = activated[:, 0:128].astype(BF16)
+        out[step, 256:512] = activated[:, 128:256].astype(BF16)
+        out[step, 512:640] = pack_tail(tail).astype(BF16)
         return carry
 
-    lax.fori_loop(0, 2, one_step, 0)
-    if first:
-        ones = [half[step].astype(F32) for half in (earlier, out) for step in range(2)]
-        total[...] = ((ones[0] + ones[1]) + (ones[2] + ones[3])).astype(BF16)
+    lax.fori_loop(0, 4, one_step, 0)
+    ones = [out[step].astype(F32) for step in range(4)]
+    total[...] = ((ones[0] + ones[1]) + (ones[2] + ones[3])).astype(BF16)
 
 
 def store_packed_frames(a3, tiles):
@@ -407,13 +400,9 @@
         rt[a:b] = (0.25 * total).astype(BF16)
 
 
-def second_prefix_kernel(own0, own1, before0, before1, after0, after1, tp, noise, prefix, a3):
+def second_prefix_kernel(own, before, after, tp, noise, prefix, a3):
     for step in range(4):
-        tiles = []
-        for pair in ((before0, before1), (own0, own1), (after0, after1)):
-            half = pair[step // 2]
-            tiles.append([half[step % 2, a:b].astype(F32) for a, b in SPANS])
-        store_packed_frames(a3, tiles)
+        store_packed_frames(a3, [[one[step, a:b].astype(F32) for a, b in SPANS] for one in (before, own, after)])
         for update, (a, b) in zip(packed_update(a3[...], tp), SPANS):
             now = 0.25 * (update + noise[step, a:b].astype(F32))
             prefix[step, a:b] = now if step == 0 else prefix[step - 1, a:b] + now
@@ -548,19 +537,15 @@
         sp, prefix, *totals,
     )
     edges = along_x(up, 1), along_x(down, -1), along_x(far, 2), far
-    halves, earlier, outs = [], (), [((2, ROWS, LANES), BF16)]
-    for half in (0, 1):
-        own, *total = call(
-            functools.partial(second_sweep_kernel, 2 * half),
-            outs + [(packed, BF16)] * half,
-            states, *edges, gain, bias, wp, wt, tb, *earlier,
-            scratch=(taps, ((4, 8, 384), F32)),
-            flops=1024 * 320 * 2880,
-        )
-        halves.append((own, along_frame(own, 1), along_frame(own, -1)))
-        earlier = (own,)
-    parts = [half[i] for i in range(3) for half in halves]
-    sums = total[0], along_frame(total[0], 1), along_frame(total[0], -1)
+    own, total = call(
+        second_sweep_kernel,
+        [(four, BF16), (packed, BF16)],
+        states, *edges, gain, bias, wp, wt, tb,
+        scratch=(taps, ((4, 8, 384), F32)),
+        flops=2048 * 320 * 2880,
+    )
+    sums = total, along_frame(total, 1), along_frame(total, -1)
+    parts = own, along_frame(own, 1), along_frame(own, -1)
     rt = call(second_total_kernel, [(packed, BF16)], *sums, tp, noises, scratch=(a3,), flops=512 * 320 * 960)[0]
     totals = gather_y(rt)
     prefix = call(second_prefix_kernel, [(four, F32)], *parts, tp, noises, scratch=(a3,), flops=2048 * 320 * 960)[0]

time: 85.4 us -> 83.4 us (0.977)
  starting transfers between devices: 30.6 us -> 28.7 us
    ppermute x23 -> x21, starting transfers between devices: 30.6 us -> 28.7 us  [moved(): return lax.ppermute(value, AXES, pairs)]
    pallas_call x13 -> x12, Pallas kernels: 19.1 us -> 19 us  [call(): pl.pallas_call(body, out_shape=shapes, in_specs=[pl.BlockSpec(memory_spac...]
    ppermute x23 -> x21, waiting for transfers between devices: 34.7 us -> 34.7 us  [moved(): return lax.ppermute(value, AXES, pairs)]
  transfers between devices with their start and end apart: 23 -> 21, of which waited for: 14 -> 15; matrix products, arithmetic and copies ran while one was open for 0% -> 0% of each run, Pallas kernels for 9% -> 10%
where the time goes in v4:
time: 83.4 us; the launch traced here: 83.2 us
  waiting for transfers between devices  34.7 us (42%)
  starting transfers between devices  28.7 us (34%)
  Pallas kernels  19 us (23%)
    ppermute x21, waiting for transfers between devices, moved(): return lax.ppermute(value, AXES, pairs)  34.7 us
    ppermute x21, starting transfers between devices, moved(): return lax.ppermute(value, AXES, pairs)  28.7 us
    pallas_call x12, Pallas kernels, call(): pl.pallas_call(body, out_shape=shapes, in_specs=[pl.BlockSpec(memory_spac...  19 us
  transfers between devices with their start and end apart: 21, of which 15 were waited for; matrix products, arithmetic and copies ran while one was open for 0% of the time, Pallas kernels for 10%

profile of v4, /device:TPU:6, one launch (start us, length us, event | category | flops | bytes accessed | tf_op | source)
XLA Modules:
  0.0 83.2 jit_solution(3602625919453282195)
XLA Ops:
  0.7 0.1 sine_convert_fusion
  0.7 0.1 fusion.2
  0.8 1.6 %shard_map.82 = (bf16[688,128]{1,0:T(8,128)(2,1)S(1)}, bf16[688,128]{1,0:T(8,128)(2,1)S(1)}, bf16[688,128]{1,0:T(8,128)(2,1)S(1)}, bf16[688,128]{1,0:T(8,128)(2,...) custom-call(bf16[1024,320]{1,0:T(8,128)(2,1)} %bitcast.4, bf16[1024,320]{1,0:T(8,128)(2,1)} %bitcast.5, ...), custom_call_target="tpu_custom_call" | custom-call | bytes 2688000 | tf_op jit(solution)/shard_map/pallas_call | solution.py:435
  2.4 0.9 %shard_map.83 = (bf16[800,128]{1,0:T(8,128)(2,1)S(1)}, bf16[640,128]{1,0:T(8,128)(2,1)S(1)}) custom-call(bf16[1024,320]{1,0:T(8,128)(2,1)S(1)} %get-tuple-element.32.start, f32[320]{0:T(512)S(1)} %get-tuple-element.33.gain_ref, f32[320]{0:T(512)S(1)} %get-tuple-element.34.bias_ref), custom_call_target="tpu_custom_call" | custom-call | bytes 1026560 | tf_op jit(solution)/shard_map/pallas_call | solution.py:435
  3.3 5.3 %collective-permute-start.1 = (bf16[800,128]{1,0:T(8,128)(2,1)S(1)}, bf16[800,128]{1,0:T(8,128)(2,1)S(1)}, u32[]{:S(2)}, u32[]{:S(2)}) collective-permute-start(bf16[800,128]{1,0:T(8,128)(2,1)S(1)} %get-tuple-element.36.normed), channel_id=1, source_target_pairs={{0,15},{1,0},{2,1},{3,2},{4,3},{5,4},{6,5},{7,6},{8,7},{9,8},{10,9... | collective-permute-start | bytes 614408 | tf_op jit(solution)/shard_map/ppermute | solution.py:454
  8.6 0.0 collective-permute-start
  8.6 0.5 collective-permute-start.2
  9.1 2.4 %collective-permute-start.3 = (bf16[688,128]{1,0:T(8,128)(2,1)S(1)}, bf16[688,128]{1,0:T(8,128)(2,1)S(1)}, u32[]{:S(2)}, u32[]{:S(2)}) collective-permute-start(bf16[688,128]{1,0:T(8,128)(2,1)S(1)} %get-tuple-element.44), channel_id=1, source_target_pairs={{0,32},{1,33},{2,34},{3,35},{4,36},{5,37},{6,38},{7,39},{8,40},{9,... | collective-permute-start | bytes 528392 | tf_op jit(solution)/shard_map/ppermute | solution.py:454
  11.5 0.0 collective-permute-start.4
  11.5 2.8 %shard_map.84 = (f32[1,256,320]{2,1,0:T(8,128)S(1)}, bf16[3,1024,320]{2,1,0:T(8,128)(2,1)S(1)}, bf16[1024,192]{1,0:T(8,128)(2,1)S(1)}, bf16[1024,320]{1,0:T(8,128)(2,1)S(1)}, bf16[320,320]{1,0:T(8,128)(2,1)S(1)}) custom-call(bf16[3,3,320,320]{3,2,1,0:T(8,128)(2,1)} %sw.1, bf16[3,320,320]{2,1,0:T(8,128)(2,1)} %tw.1, bf16[320,320]{1,0:T(8,128)(2,1)} %tew_hbm.1, ...), custom_call_target="tpu_custom_call" | custom-call | flops 471859200 | bytes 6414336 | tf_op jit(solution)/shard_map/pallas_call | solution.py:435
  14.3 0.0 collective-permute-done.1.after
  14.3 0.7 collective-permute-done.before
  15.0 1.6 %shard_map.85.sides = f32[2,256,320]{2,1,0:T(8,128)S(1)} custom-call(bf16[800,128]{1,0:T(8,128)(2,1)S(1)} %collective-permute-done.before, bf16[800,128]{1,0:T(8,128)(2,1)S(1)} %collective-permute-done.1.after, bf16[3,1024,320]{2,1,0:T(8,128)(2,1)S(1)} %get-tuple-element.38.wp, bf16[1024,192]{1,0:T(8,128)(2,1)S(1)} %get-tuple-element.39.wt), custom_call_target="tpu_custom_call" | custom-call | flops 943718400 | bytes 3424256 | tf_op jit(solution)/shard_map/pallas_call | solution.py:435
  16.6 0.0 collective-permute-done.2.n1
  16.6 0.0 collective-permute-done.3.n2
  16.6 1.6 %collective-permute-done.4.n3 = bf16[688,128]{1,0:T(8,128)(2,1)S(1)} collective-permute-done((bf16[688,128]{1,0:T(8,128)(2,1)S(1)}, bf16[688,128]{1,0:T(8,128)(2,1)S(1)}, u32[]{:S(2)}, u32[]{:S(2)}) %collective-permute-start.4) | collective-permute-done | bytes 176160 | tf_op jit(solution)/shard_map/ppermute | solution.py:454
  18.2 1.6 %shard_map.86 = (bf16[640,128]{1,0:T(8,128)(2,1)S(1)}, bf16[4,640,128]{2,1,0:T(8,128)(2,1)S(1)}, f32[4,16,320]{2,1,0:T(8,128)S(1)}) custom-call(f32[1,256,320]{2,1,0:T(8,128)S(1)} %get-tuple-element.37.here, f32[2,256,320]{2,1,0:T(8,128)S(1)} %shard_map.85.sides, bf16[1024,320]{1,0:T(8,128)(2,1)S(1)} %get-tuple-element.40.tp, ...), custom_call_target="tpu_custom_call" | custom-call | flops 157286400 | bytes 3448832 | tf_op jit(solution)/shard_map/pallas_call | solution.py:435
  19.8 3.1 %collective-permute-start.7 = (bf16[640,128]{1,0:T(8,128)(2,1)S(1)}, bf16[640,128]{1,0:T(8,128)(2,1)S(1)}, u32[]{:S(2)}, u32[]{:S(2)}) collective-permute-start(bf16[640,128]{1,0:T(8,128)(2,1)S(1)} %get-tuple-element.48), channel_id=1, source_target_pairs={{0,192},{1,65},{2,194},{3,67},{4,196},{5,69},{6,198},{7,71},{8,200... | collective-permute-start | bytes 491528 | tf_op jit(solution)/shard_map/ppermute | solution.py:454
  22.8 0.6 collective-permute-start.6
  23.5 1.0 %collective-permute-start.5 = (bf16[640,128]{1,0:T(8,128)(2,1)S(1)}, bf16[640,128]{1,0:T(8,128)(2,1)S(1)}, u32[]{:S(2)}, u32[]{:S(2)}) collective-permute-start(bf16[640,128]{1,0:T(8,128)(2,1)S(1)} %get-tuple-element.48), channel_id=1, source_target_pairs={{0,64},{1,193},{2,66},{3,195},{4,68},{5,197},{6,70},{7,199},{8,72}... | collective-permute-start | bytes 491528 | tf_op jit(solution)/shard_map/ppermute | solution.py:454
  24.4 1.5 %shard_map.87.prefix = f32[4,640,128]{2,1,0:T(8,128)S(1)} custom-call(f32[1,256,320]{2,1,0:T(8,128)S(1)} %get-tuple-element.37.here, f32[2,256,320]{2,1,0:T(8,128)S(1)} %shard_map.85.sides, f32[4,16,320]{2,1,0:T(8,128)S(1)} %get-tuple-element.46.tb, bf16[1024,320]{1,0:T(8,128)(2,1)S(1)} %get-tuple-element.40.tp, bf16[4,640,128]{2,1,0:T(8,128)(2,1)S(1)} %get-tuple-element.47.noise), custom_call_target="tpu_custom_call" | custom-call | flops 471859200 | bytes 3686400 | tf_op jit(solution)/shard_map/pallas_call | solution.py:435
  26.0 0.7 collective-permute-done.7.r3
  26.7 3.0 %collective-permute-done.6.r2 = bf16[640,128]{1,0:T(8,128)(2,1)S(1)} collective-permute-done((bf16[640,128]{1,0:T(8,128)(2,1)S(1)}, bf16[640,128]{1,0:T(8,128)(2,1)S(1)}, u32[]{:S(2)}, u32[]{:S(2)}) %collective-permute-start.6) | collective-permute-done | bytes 163872 | tf_op jit(solution)/shard_map/ppermute | solution.py:454
  29.8 1.7 %collective-permute-done.5.r1 = bf16[640,128]{1,0:T(8,128)(2,1)S(1)} collective-permute-done((bf16[640,128]{1,0:T(8,128)(2,1)S(1)}, bf16[640,128]{1,0:T(8,128)(2,1)S(1)}, u32[]{:S(2)}, u32[]{:S(2)}) %collective-permute-start.5) | collective-permute-done | bytes 163872 | tf_op jit(solution)/shard_map/ppermute | solution.py:454
  31.4 1.1 %shard_map.88 = (bf16[4,640,128]{2,1,0:T(8,128)(2,1)S(1)}, bf16[464,128]{1,0:T(8,128)(2,1)S(1)}, bf16[464,128]{1,0:T(8,128)(2,1)S(1)}, bf16[72,128]{1,0:T(8,128)(2,1)S(1)}) custom-call(bf16[640,128]{1,0:T(8,128)(2,1)S(1)} %get-tuple-element.35.sp, f32[4,640,128]{2,1,0:T(8,128)S(1)} %shard_map.87.prefix, bf16[640,128]{1,0:T(8,128)(2,1)S(1)} %collective-permute-done.5.r1, ...), custom_call_target="tpu_custom_call" | custom-call | bytes 2877440 | tf_op jit(solution)/shard_map/pallas_call | solution.py:435
  32.5 1.9 %collective-permute-start.8 = (bf16[464,128]{1,0:T(8,128)(2,1)S(1)}, bf16[464,128]{1,0:T(8,128)(2,1)S(1)}, u32[]{:S(2)}, u32[]{:S(2)}) collective-permute-start(bf16[464,128]{1,0:T(8,128)(2,1)S(1)} %get-tuple-element.50), channel_id=1, source_target_pairs={{0,16},{1,17},{2,18},{3,19},{4,20},{5,21},{6,22},{7,23},{8,24},{9,... | collective-permute-start | bytes 356360 | tf_op jit(solution)/shard_map/ppermute | solution.py:454
  34.3 0.2 collective-permute-start.9
  34.5 1.8 %collective-permute-start.10 = (bf16[72,128]{1,0:T(8,128)(2,1)S(1)}, bf16[72,128]{1,0:T(8,128)(2,1)S(1)}, u32[]{:S(2)}, u32[]{:S(2)}) collective-permute-start(bf16[72,128]{1,0:T(8,128)(2,1)S(1)} %get-tuple-element.52.mine), channel_id=1, source_target_pairs={{0,32},{1,33},{2,34},{3,35},{4,36},{5,37},{6,38},{7,39},{8,40},{9,... | collective-permute-start | bytes 55304 | tf_op jit(solution)/shard_map/ppermute | solution.py:454
  36.3 3.6 %collective-permute-done.10.far = bf16[72,128]{1,0:T(8,128)(2,1)S(1)} collective-permute-done((bf16[72,128]{1,0:T(8,128)(2,1)S(1)}, bf16[72,128]{1,0:T(8,128)(2,1)S(1)}, u32[]{:S(2)}, u32[]{:S(2)}) %collective-permute-start.10) | collective-permute-done | bytes 18464 | tf_op jit(solution)/shard_map/ppermute | solution.py:454
  39.9 0.0 collective-permute-done.8.above
  39.9 0.7 collective-permute-done.9.below
  40.6 4.6 %shard_map.89 = (bf16[4,640,128]{2,1,0:T(8,128)(2,1)S(1)}, bf16[640,128]{1,0:T(8,128)(2,1)S(1)}) custom-call(bf16[4,640,128]{2,1,0:T(8,128)(2,1)S(1)} %get-tuple-element.49.states, bf16[464,128]{1,0:T(8,128)(2,1)S(1)} %collective-permute-done.8.above, bf16[464,128]{1,0:T(8,128)(2,1)S(1)} %collective-permute-done.9.below, ...), custom_call_target="tpu_custom_call" | custom-call | flops 1887436800 | bytes 4192768 | tf_op jit(solution)/shard_map/pallas_call | solution.py:435
  45.2 1.3 %collective-permute-start.12 = (bf16[4,640,128]{2,1,0:T(8,128)(2,1)S(1)}, bf16[4,640,128]{2,1,0:T(8,128)(2,1)S(1)}, u32[]{:S(2)}, u32[]{:S(2)}) collective-permute-start(bf16[4,640,128]{2,1,0:T(8,128)(2,1)S(1)} %get-tuple-element.53.own), channel_id=1, source_target_pairs={{0,15},{1,0},{2,1},{3,2},{4,3},{5,4},{6,5},{7,6},{8,7},{9,8},{10,9... | collective-permute-start | bytes 1966088 | tf_op jit(solution)/shard_map/ppermute | solution.py:454
  46.5 0.0 collective-permute-start.11
  46.5 3.0 %collective-permute-start.14 = (bf16[640,128]{1,0:T(8,128)(2,1)S(1)}, bf16[640,128]{1,0:T(8,128)(2,1)S(1)}, u32[]{:S(2)}, u32[]{:S(2)}) collective-permute-start(bf16[640,128]{1,0:T(8,128)(2,1)S(1)} %get-tuple-element.54.own), channel_id=1, source_target_pairs={{0,15},{1,0},{2,1},{3,2},{4,3},{5,4},{6,5},{7,6},{8,7},{9,8},{10,9... | collective-permute-start | bytes 491528 | tf_op jit(solution)/shard_map/ppermute | solution.py:454
  49.4 0.0 collective-permute-start.13
  49.4 6.9 %collective-permute-done.14.after = bf16[640,128]{1,0:T(8,128)(2,1)S(1)} collective-permute-done((bf16[640,128]{1,0:T(8,128)(2,1)S(1)}, bf16[640,128]{1,0:T(8,128)(2,1)S(1)}, u32[]{:S(2)}, u32[]{:S(2)}) %collective-permute-start.14) | collective-permute-done | bytes 163872 | tf_op jit(solution)/shard_map/ppermute | solution.py:454
  56.3 3.1 %collective-permute-done.13.before = bf16[640,128]{1,0:T(8,128)(2,1)S(1)} collective-permute-done((bf16[640,128]{1,0:T(8,128)(2,1)S(1)}, bf16[640,128]{1,0:T(8,128)(2,1)S(1)}, u32[]{:S(2)}, u32[]{:S(2)}) %collective-permute-start.13) | collective-permute-done | bytes 163872 | tf_op jit(solution)/shard_map/ppermute | solution.py:454
  59.5 0.5 shard_map.91
  60.0 3.3 %collective-permute-start.17 = (bf16[640,128]{1,0:T(8,128)(2,1)S(1)}, bf16[640,128]{1,0:T(8,128)(2,1)S(1)}, u32[]{:S(2)}, u32[]{:S(2)}) collective-permute-start(bf16[640,128]{1,0:T(8,128)(2,1)S(1)} %shard_map.91), channel_id=1, source_target_pairs={{0,192},{1,65},{2,194},{3,67},{4,196},{5,69},{6,198},{7,71},{8,200... | collective-permute-start | bytes 491528 | tf_op jit(solution)/shard_map/ppermute | solution.py:454
  63.3 0.3 collective-permute-start.16
  63.5 0.8 collective-permute-start.15
  64.3 0.0 collective-permute-done.12.after
  64.3 0.0 collective-permute-done.11.before
  64.3 1.6 %shard_map.90.prefix = f32[4,640,128]{2,1,0:T(8,128)S(1)} custom-call(bf16[4,640,128]{2,1,0:T(8,128)(2,1)S(1)} %get-tuple-element.53.own, bf16[4,640,128]{2,1,0:T(8,128)(2,1)S(1)} %collective-permute-done.11.before, bf16[4,640,128]{2,1,0:T(8,128)(2,1)S(1)} %collective-permute-done.12.after, bf16[1024,320]{1,0:T(8,128)(2,1)S(1)} %get-tuple-element.40.tp, ...), custom_call_target="tpu_custom_call" | custom-call | flops 629145600 | bytes 4587520 | tf_op jit(solution)/shard_map/pallas_call | solution.py:435
  65.9 2.0 %collective-permute-done.17.r3 = bf16[640,128]{1,0:T(8,128)(2,1)S(1)} collective-permute-done((bf16[640,128]{1,0:T(8,128)(2,1)S(1)}, bf16[640,128]{1,0:T(8,128)(2,1)S(1)}, u32[]{:S(2)}, u32[]{:S(2)}) %collective-permute-start.17) | collective-permute-done | bytes 163872 | tf_op jit(solution)/shard_map/ppermute | solution.py:454
  67.9 2.3 %collective-permute-done.16.r2 = bf16[640,128]{1,0:T(8,128)(2,1)S(1)} collective-permute-done((bf16[640,128]{1,0:T(8,128)(2,1)S(1)}, bf16[640,128]{1,0:T(8,128)(2,1)S(1)}, u32[]{:S(2)}, u32[]{:S(2)}) %collective-permute-start.16) | collective-permute-done | bytes 163872 | tf_op jit(solution)/shard_map/ppermute | solution.py:454
  70.2 1.6 %collective-permute-done.15.r1 = bf16[640,128]{1,0:T(8,128)(2,1)S(1)} collective-permute-done((bf16[640,128]{1,0:T(8,128)(2,1)S(1)}, bf16[640,128]{1,0:T(8,128)(2,1)S(1)}, u32[]{:S(2)}, u32[]{:S(2)}) %collective-permute-start.15) | collective-permute-done | bytes 163872 | tf_op jit(solution)/shard_map/ppermute | solution.py:454
  71.8 0.2 shard_map.92
  72.0 1.6 %collective-permute-start.18 = (bf16[640,128]{1,0:T(8,128)(2,1)S(1)}, bf16[640,128]{1,0:T(8,128)(2,1)S(1)}, u32[]{:S(2)}, u32[]{:S(2)}) collective-permute-start(bf16[640,128]{1,0:T(8,128)(2,1)S(1)} %get-tuple-element.56), channel_id=1, source_target_pairs={{0,16},{1,49},{2,18},{3,51},{4,20},{5,53},{6,22},{7,55},{8,24},{9,... | collective-permute-start | bytes 491528 | tf_op jit(solution)/shard_map/ppermute | solution.py:454
  73.6 0.8 collective-permute-start.19
  74.4 1.0 %collective-permute-start.20 = (bf16[640,128]{1,0:T(8,128)(2,1)S(1)}, bf16[640,128]{1,0:T(8,128)(2,1)S(1)}, u32[]{:S(2)}, u32[]{:S(2)}) collective-permute-start(bf16[640,128]{1,0:T(8,128)(2,1)S(1)} %get-tuple-element.58), channel_id=1, source_target_pairs={{0,48},{1,17},{2,50},{3,19},{4,52},{5,21},{6,54},{7,23},{8,56},{9,... | collective-permute-start | bytes 491528 | tf_op jit(solution)/shard_map/ppermute | solution.py:454
  75.3 2.1 %collective-permute-done.18.r1 = bf16[640,128]{1,0:T(8,128)(2,1)S(1)} collective-permute-done((bf16[640,128]{1,0:T(8,128)(2,1)S(1)}, bf16[640,128]{1,0:T(8,128)(2,1)S(1)}, u32[]{:S(2)}, u32[]{:S(2)}) %collective-permute-start.18) | collective-permute-done | bytes 163872 | tf_op jit(solution)/shard_map/ppermute | solution.py:454
  77.4 3.1 %collective-permute-done.19.r2 = bf16[640,128]{1,0:T(8,128)(2,1)S(1)} collective-permute-done((bf16[640,128]{1,0:T(8,128)(2,1)S(1)}, bf16[640,128]{1,0:T(8,128)(2,1)S(1)}, u32[]{:S(2)}, u32[]{:S(2)}) %collective-permute-start.19) | collective-permute-done | bytes 163872 | tf_op jit(solution)/shard_map/ppermute | solution.py:454
  80.6 1.7 %collective-permute-done.20.r3 = bf16[640,128]{1,0:T(8,128)(2,1)S(1)} collective-permute-done((bf16[640,128]{1,0:T(8,128)(2,1)S(1)}, bf16[640,128]{1,0:T(8,128)(2,1)S(1)}, u32[]{:S(2)}, u32[]{:S(2)}) %collective-permute-start.20) | collective-permute-done | bytes 163872 | tf_op jit(solution)/shard_map/ppermute | solution.py:454
  82.2 1.0 %shard_map.93 = bf16[1024,320]{1,0:T(8,128)(2,1)} custom-call(bf16[640,128]{1,0:T(8,128)(2,1)S(1)} %get-tuple-element.55.r0, bf16[640,128]{1,0:T(8,128)(2,1)S(1)} %collective-permute-done.18.r1, bf16[640,128]{1,0:T(8,128)(2,1)S(1)} %collective-permute-done.19.r2, bf16[640,128]{1,0:T(8,128)(2,1)S(1)} %collective-permute-done.20.r3), custom_call_target="tpu_custom_call" | custom-call | bytes 1310720 | tf_op jit(solution)/shard_map/pallas_call | solution.py:435
  (1 shorter events, 0.0 us)
Async XLA Ops:
  3.3 11.0 %collective-permute-start.1 = (bf16[800,128]{1,0:T(8,128)(2,1)S(1)}, bf16[800,128]{1,0:T(8,128)(2,1)S(1)}, u32[]{:S(2)}, u32[]{:S(2)}) collective-permute-start(bf16[800,128]{1,0:T(8,128)(2,1)S(1)} %get-tuple-element.36.normed), channel_id=1, source_target_pairs={{0,15},{1,0},{2,1},{3,2},{4,3},{5,4},{6,5},{7,6},{8,7},{9,8},{10,9... | collective-permute-start | bytes 614408 | tf_op jit(solution)/shard_map/ppermute | solution.py:454
  8.6 6.4 %collective-permute-start = (bf16[800,128]{1,0:T(8,128)(2,1)S(1)}, bf16[800,128]{1,0:T(8,128)(2,1)S(1)}, u32[]{:S(2)}, u32[]{:S(2)}) collective-permute-start(bf16[800,128]{1,0:T(8,128)(2,1)S(1)} %get-tuple-element.36.normed), channel_id=1, source_target_pairs={{0,1},{1,2},{2,3},{3,4},{4,5},{5,6},{6,7},{7,8},{8,9},{9,10},{10,1... | collective-permute-start | bytes 614408 | tf_op jit(solution)/shard_map/ppermute | solution.py:454
  8.6 8.0 %collective-permute-start.2 = (bf16[688,128]{1,0:T(8,128)(2,1)S(1)}, bf16[688,128]{1,0:T(8,128)(2,1)S(1)}, u32[]{:S(2)}, u32[]{:S(2)}) collective-permute-start(bf16[688,128]{1,0:T(8,128)(2,1)S(1)} %get-tuple-element.43), channel_id=1, source_target_pairs={{0,16},{1,49},{2,18},{3,51},{4,20},{5,53},{6,22},{7,55},{8,24},{9,... | collective-permute-start | bytes 528392 | tf_op jit(solution)/shard_map/ppermute | solution.py:454
  9.1 7.5 %collective-permute-start.3 = (bf16[688,128]{1,0:T(8,128)(2,1)S(1)}, bf16[688,128]{1,0:T(8,128)(2,1)S(1)}, u32[]{:S(2)}, u32[]{:S(2)}) collective-permute-start(bf16[688,128]{1,0:T(8,128)(2,1)S(1)} %get-tuple-element.44), channel_id=1, source_target_pairs={{0,32},{1,33},{2,34},{3,35},{4,36},{5,37},{6,38},{7,39},{8,40},{9,... | collective-permute-start | bytes 528392 | tf_op jit(solution)/shard_map/ppermute | solution.py:454
  11.5 6.7 %collective-permute-start.4 = (bf16[688,128]{1,0:T(8,128)(2,1)S(1)}, bf16[688,128]{1,0:T(8,128)(2,1)S(1)}, u32[]{:S(2)}, u32[]{:S(2)}) collective-permute-start(bf16[688,128]{1,0:T(8,128)(2,1)S(1)} %get-tuple-element.45), channel_id=1, source_target_pairs={{0,48},{1,17},{2,50},{3,19},{4,52},{5,21},{6,54},{7,23},{8,56},{9,... | collective-permute-start | bytes 528392 | tf_op jit(solution)/shard_map/ppermute | solution.py:454
  19.8 7.0 %collective-permute-start.7 = (bf16[640,128]{1,0:T(8,128)(2,1)S(1)}, bf16[640,128]{1,0:T(8,128)(2,1)S(1)}, u32[]{:S(2)}, u32[]{:S(2)}) collective-permute-start(bf16[640,128]{1,0:T(8,128)(2,1)S(1)} %get-tuple-element.48), channel_id=1, source_target_pairs={{0,192},{1,65},{2,194},{3,67},{4,196},{5,69},{6,198},{7,71},{8,200... | collective-permute-start | bytes 491528 | tf_op jit(solution)/shard_map/ppermute | solution.py:454
  22.8 6.9 %collective-permute-start.6 = (bf16[640,128]{1,0:T(8,128)(2,1)S(1)}, bf16[640,128]{1,0:T(8,128)(2,1)S(1)}, u32[]{:S(2)}, u32[]{:S(2)}) collective-permute-start(bf16[640,128]{1,0:T(8,128)(2,1)S(1)} %get-tuple-element.48), channel_id=1, source_target_pairs={{0,128},{1,129},{2,130},{3,131},{4,132},{5,133},{6,134},{7,135},{8... | collective-permute-start | bytes 491528 | tf_op jit(solution)/shard_map/ppermute | solution.py:454
  23.5 8.0 %collective-permute-start.5 = (bf16[640,128]{1,0:T(8,128)(2,1)S(1)}, bf16[640,128]{1,0:T(8,128)(2,1)S(1)}, u32[]{:S(2)}, u32[]{:S(2)}) collective-permute-start(bf16[640,128]{1,0:T(8,128)(2,1)S(1)} %get-tuple-element.48), channel_id=1, source_target_pairs={{0,64},{1,193},{2,66},{3,195},{4,68},{5,197},{6,70},{7,199},{8,72}... | collective-permute-start | bytes 491528 | tf_op jit(solution)/shard_map/ppermute | solution.py:454
  32.5 7.4 %collective-permute-start.8 = (bf16[464,128]{1,0:T(8,128)(2,1)S(1)}, bf16[464,128]{1,0:T(8,128)(2,1)S(1)}, u32[]{:S(2)}, u32[]{:S(2)}) collective-permute-start(bf16[464,128]{1,0:T(8,128)(2,1)S(1)} %get-tuple-element.50), channel_id=1, source_target_pairs={{0,16},{1,17},{2,18},{3,19},{4,20},{5,21},{6,22},{7,23},{8,24},{9,... | collective-permute-start | bytes 356360 | tf_op jit(solution)/shard_map/ppermute | solution.py:454
  34.3 6.2 %collective-permute-start.9 = (bf16[464,128]{1,0:T(8,128)(2,1)S(1)}, bf16[464,128]{1,0:T(8,128)(2,1)S(1)}, u32[]{:S(2)}, u32[]{:S(2)}) collective-permute-start(bf16[464,128]{1,0:T(8,128)(2,1)S(1)} %get-tuple-element.51), channel_id=1, source_target_pairs={{0,48},{1,49},{2,50},{3,51},{4,52},{5,53},{6,54},{7,55},{8,56},{9,... | collective-permute-start | bytes 356360 | tf_op jit(solution)/shard_map/ppermute | solution.py:454
  34.5 5.4 %collective-permute-start.10 = (bf16[72,128]{1,0:T(8,128)(2,1)S(1)}, bf16[72,128]{1,0:T(8,128)(2,1)S(1)}, u32[]{:S(2)}, u32[]{:S(2)}) collective-permute-start(bf16[72,128]{1,0:T(8,128)(2,1)S(1)} %get-tuple-element.52.mine), channel_id=1, source_target_pairs={{0,32},{1,33},{2,34},{3,35},{4,36},{5,37},{6,38},{7,39},{8,40},{9,... | collective-permute-start | bytes 55304 | tf_op jit(solution)/shard_map/ppermute | solution.py:454
  45.2 19.2 %collective-permute-start.12 = (bf16[4,640,128]{2,1,0:T(8,128)(2,1)S(1)}, bf16[4,640,128]{2,1,0:T(8,128)(2,1)S(1)}, u32[]{:S(2)}, u32[]{:S(2)}) collective-permute-start(bf16[4,640,128]{2,1,0:T(8,128)(2,1)S(1)} %get-tuple-element.53.own), channel_id=1, source_target_pairs={{0,15},{1,0},{2,1},{3,2},{4,3},{5,4},{6,5},{7,6},{8,7},{9,8},{10,9... | collective-permute-start | bytes 1966088 | tf_op jit(solution)/shard_map/ppermute | solution.py:454
  46.5 17.8 %collective-permute-start.11 = (bf16[4,640,128]{2,1,0:T(8,128)(2,1)S(1)}, bf16[4,640,128]{2,1,0:T(8,128)(2,1)S(1)}, u32[]{:S(2)}, u32[]{:S(2)}) collective-permute-start(bf16[4,640,128]{2,1,0:T(8,128)(2,1)S(1)} %get-tuple-element.53.own), channel_id=1, source_target_pairs={{0,1},{1,2},{2,3},{3,4},{4,5},{5,6},{6,7},{7,8},{8,9},{9,10},{10,1... | collective-permute-start | bytes 1966088 | tf_op jit(solution)/shard_map/ppermute | solution.py:454
  46.5 9.9 %collective-permute-start.14 = (bf16[640,128]{1,0:T(8,128)(2,1)S(1)}, bf16[640,128]{1,0:T(8,128)(2,1)S(1)}, u32[]{:S(2)}, u32[]{:S(2)}) collective-permute-start(bf16[640,128]{1,0:T(8,128)(2,1)S(1)} %get-tuple-element.54.own), channel_id=1, source_target_pairs={{0,15},{1,0},{2,1},{3,2},{4,3},{5,4},{6,5},{7,6},{8,7},{9,8},{10,9... | collective-permute-start | bytes 491528 | tf_op jit(solution)/shard_map/ppermute | solution.py:454
  49.4 10.0 %collective-permute-start.13 = (bf16[640,128]{1,0:T(8,128)(2,1)S(1)}, bf16[640,128]{1,0:T(8,128)(2,1)S(1)}, u32[]{:S(2)}, u32[]{:S(2)}) collective-permute-start(bf16[640,128]{1,0:T(8,128)(2,1)S(1)} %get-tuple-element.54.own), channel_id=1, source_target_pairs={{0,1},{1,2},{2,3},{3,4},{4,5},{5,6},{6,7},{7,8},{8,9},{9,10},{10,1... | collective-permute-start | bytes 491528 | tf_op jit(solution)/shard_map/ppermute | solution.py:454
  60.0 7.9 %collective-permute-start.17 = (bf16[640,128]{1,0:T(8,128)(2,1)S(1)}, bf16[640,128]{1,0:T(8,128)(2,1)S(1)}, u32[]{:S(2)}, u32[]{:S(2)}) collective-permute-start(bf16[640,128]{1,0:T(8,128)(2,1)S(1)} %shard_map.91), channel_id=1, source_target_pairs={{0,192},{1,65},{2,194},{3,67},{4,196},{5,69},{6,198},{7,71},{8,200... | collective-permute-start | bytes 491528 | tf_op jit(solution)/shard_map/ppermute | solution.py:454
  63.3 6.9 %collective-permute-start.16 = (bf16[640,128]{1,0:T(8,128)(2,1)S(1)}, bf16[640,128]{1,0:T(8,128)(2,1)S(1)}, u32[]{:S(2)}, u32[]{:S(2)}) collective-permute-start(bf16[640,128]{1,0:T(8,128)(2,1)S(1)} %shard_map.91), channel_id=1, source_target_pairs={{0,128},{1,129},{2,130},{3,131},{4,132},{5,133},{6,134},{7,135},{8... | collective-permute-start | bytes 491528 | tf_op jit(solution)/shard_map/ppermute | solution.py:454
  63.5 8.3 %collective-permute-start.15 = (bf16[640,128]{1,0:T(8,128)(2,1)S(1)}, bf16[640,128]{1,0:T(8,128)(2,1)S(1)}, u32[]{:S(2)}, u32[]{:S(2)}) collective-permute-start(bf16[640,128]{1,0:T(8,128)(2,1)S(1)} %shard_map.91), channel_id=1, source_target_pairs={{0,64},{1,193},{2,66},{3,195},{4,68},{5,197},{6,70},{7,199},{8,72}... | collective-permute-start | bytes 491528 | tf_op jit(solution)/shard_map/ppermute | solution.py:454
  72.0 5.4 %collective-permute-start.18 = (bf16[640,128]{1,0:T(8,128)(2,1)S(1)}, bf16[640,128]{1,0:T(8,128)(2,1)S(1)}, u32[]{:S(2)}, u32[]{:S(2)}) collective-permute-start(bf16[640,128]{1,0:T(8,128)(2,1)S(1)} %get-tuple-element.56), channel_id=1, source_target_pairs={{0,16},{1,49},{2,18},{3,51},{4,20},{5,53},{6,22},{7,55},{8,24},{9,... | collective-permute-start | bytes 491528 | tf_op jit(solution)/shard_map/ppermute | solution.py:454
  73.6 6.9 %collective-permute-start.19 = (bf16[640,128]{1,0:T(8,128)(2,1)S(1)}, bf16[640,128]{1,0:T(8,128)(2,1)S(1)}, u32[]{:S(2)}, u32[]{:S(2)}) collective-permute-start(bf16[640,128]{1,0:T(8,128)(2,1)S(1)} %get-tuple-element.57), channel_id=1, source_target_pairs={{0,32},{1,33},{2,34},{3,35},{4,36},{5,37},{6,38},{7,39},{8,40},{9,... | collective-permute-start | bytes 491528 | tf_op jit(solution)/shard_map/ppermute | solution.py:454
  74.4 7.8 %collective-permute-start.20 = (bf16[640,128]{1,0:T(8,128)(2,1)S(1)}, bf16[640,128]{1,0:T(8,128)(2,1)S(1)}, u32[]{:S(2)}, u32[]{:S(2)}) collective-permute-start(bf16[640,128]{1,0:T(8,128)(2,1)S(1)} %get-tuple-element.58), channel_id=1, source_target_pairs={{0,48},{1,17},{2,50},{3,19},{4,52},{5,21},{6,54},{7,23},{8,56},{9,... | collective-permute-start | bytes 491528 | tf_op jit(solution)/shard_map/ppermute | solution.py:454

commit v5 on v4

--- a/solution.py
+++ b/solution.py
@@ -93,7 +93,7 @@
     outs = {0: o0, 1: o1, 2: o2, 3: o3}
     copies = {}
     for slot in (2, 1, 3, 0):
-        at = pl.multiple_of(lax.rem(x + hop_of(slot), 4) * POS, POS)
+        at = pl.multiple_of((x ^ hop_of(slot)) * POS, POS)
         copies[slot] = pltpu.make_async_copy(noise_hbm.at[pl.ds(at, POS)], noise.at[slot], sems.at[slot])
         copies[slot].start()
     rest = [
@@ -156,12 +156,13 @@
 
 
 def first_own_kernel(sw, tw, tew_hbm, normed, pre, wp, wt, tp, tew, taps, sems):
-    frame = lax.axis_index("z") * 2 + lax.axis_index("core")
+    core = lax.axis_index("core")
+    frame = lax.axis_index("z") * 2 + core
     copies = []
     for row in range(4):
         out = tp if row == 3 else wp.at[row]
         for place in range(3):
-            one = tw.at[place] if row == 3 else sw.at[row, place]
+            one = tw.at[place + core * (2 - 2 * place)] if row == 3 else sw.at[row, place]
             for source, target in (
                 (one.at[0:256], out.at[place * 256 : place * 256 + 256]),
                 (one.at[256:320], out.at[768 + 64 * place : 832 + 64 * place]),
@@ -184,12 +185,11 @@
     conv_frame(normed, wp, wt, pre.at[0], taps, before_row)
     for copy in copies[18:]:
         copy.wait()
-    for place, missing in ((0, frame == 0), (2, frame == 15)):
-
-        @pl.when(missing)
-        def _():
-            tp[place * 256 : place * 256 + 256] = jnp.zeros((256, 320), BF16)
-            tp[768 + 64 * place : 832 + 64 * place] = jnp.zeros((64, 320), BF16)
+
+    @pl.when((frame == 0) | (frame == 15))
+    def _():
+        tp[0:256] = jnp.zeros((256, 320), BF16)
+        tp[768:832] = jnp.zeros((64, 320), BF16)
 
 
 def first_sides_kernel(before, after, wp, wt, pre, taps):
@@ -227,7 +227,7 @@
         bias = term if bias is None else bias + term
     bias = bias / (1.0 + jnp.exp(-bias))
     for slot, one in enumerate(arrived):
-        step = lax.rem(x + 4 - hop_of(slot), 4)
+        step = x ^ hop_of(slot)
         noise[step] = one[0:640]
         tb[step] = bias[slot * 16 : slot * 16 + 16]
     halves = [0.5 * bias[slot * 16 : slot * 16 + 1] for slot in range(4)]
@@ -271,9 +271,13 @@
     return jnp.concatenate([parts[:, 0:256], third], axis=1)
 
 
+def slot_1_is_ahead():
+    return ((lax.axis_index("x") + lax.axis_index("core")) & 1) == 0
+
+
 def offset_of(totals):
     y = lax.axis_index("y")
-    kept = [jnp.where(y >= hop_of(slot), one[...].astype(F32), 0.0) for slot, one in enumerate(totals, 1)]
+    kept = [jnp.where((y ^ hop_of(slot)) < y, one[...].astype(F32), 0.0) for slot, one in enumerate(totals, 1)]
     return kept[0] + kept[1] + kept[2]
 
 
@@ -283,7 +287,8 @@
     return jnp.concatenate(sums[:2] + [(third + swapped(third))[0:1]], axis=1)
 
 
-def states_kernel(sp, prefix, r1, r2, r3, states, up, down, far):
+def states_kernel(sp, prefix, r1, r2, r3, states, halo1, halo3, far):
+    ahead = slot_1_is_ahead()
     members = same_group(384)
     base = sp[...].astype(F32) + offset_of((r1, r2, r3))
     spans = ((0, 256), (256, 512), (512, 640))
@@ -293,8 +298,8 @@
         sums.append(position_sum([states[step, a:b].astype(F32) for a, b in spans]))
         for i, (first, last) in enumerate(((0, 224), (256, 480), (512, 608))):
             at = step * 96 + i * 32
-            up[at : at + 32] = states[step, last : last + 32]
-            down[at : at + 32] = states[step, first : first + 32]
+            for halo, row in ((halo1, jnp.where(ahead, last, first)), (halo3, jnp.where(ahead, first, last))):
+                halo[at : at + 32] = states[step, pl.ds(pl.multiple_of(row, 32), 32)]
     means = dup_third(group_sum(jnp.concatenate(sums + sums, axis=0), members) * (1.0 / 2560))
     spreads = []
     for step in range(4):
@@ -310,8 +315,8 @@
             at = (part * 3 + tile) * 8
             value = piece[:, tile * 128 : tile * 128 + 128]
             far[at : at + 8] = value
-            up[384 + at : 392 + at] = value
-            down[384 + at : 392 + at] = value
+            halo1[384 + at : 392 + at] = value
+            halo3[384 + at : 392 + at] = value
 
 
 def stats_of(ref, base):
@@ -329,10 +334,11 @@
     return jnp.concatenate([vector, vector[:, 256:320]], axis=1)
 
 
-def second_sweep_kernel(states, above, below, far, mine, gain_ref, bias_ref, wp, wt, tb, out, total, taps, scales):
+def second_sweep_kernel(states, halo1, halo3, far, mine, gain_ref, bias_ref, wp, wt, tb, out, total, taps, scales):
     gain, bias = wide(gain_ref), wide(bias_ref)
     x = lax.axis_index("x")
-    parts = [stats_of(mine, 0), stats_of(above, 384), stats_of(below, 384), stats_of(far, 0)]
+    ahead = slot_1_is_ahead()
+    parts = [stats_of(mine, 0), stats_of(halo1, 384), stats_of(halo3, 384), stats_of(far, 0)]
     mean = (parts[0][0] + parts[1][0] + parts[2][0] + parts[3][0]) * 0.25
     spread = parts[0][1] + parts[1][1] + parts[2][1] + parts[3][1]
     for one in parts:
@@ -354,8 +360,10 @@
         tiles = []
         low = low_lanes(32)
         for tile in range(3):
-            top = normed(above[pl.ds(edge + 32 * tile, 32)], tile)
-            bottom = normed(below[pl.ds(edge + 32 * tile, 32)], tile)
+            one = halo1[pl.ds(edge + 32 * tile, 32)].astype(F32)
+            three = halo3[pl.ds(edge + 32 * tile, 32)].astype(F32)
+            top = normed(jnp.where(ahead, three, one), tile)
+            bottom = normed(jnp.where(ahead, one, three), tile)
             if tile < 2:
                 middle = normed(states[step, 256 * tile : 256 * tile + 256], tile)
             else:
@@ -412,13 +420,13 @@
     x = lax.axis_index("x")
     base = sp[...].astype(F32) + offset_of((r1, r2, r3))
     for slot, out in enumerate(outs):
-        out[...] = (base + prefix[lax.rem(x + hop_of(slot), 4)]).astype(BF16)
+        out[...] = (base + prefix[x ^ hop_of(slot)]).astype(BF16)
 
 
 def unpack_kernel(r0, r1, r2, r3, out):
     x = lax.axis_index("x")
     for slot, one in enumerate((r0, r1, r2, r3)):
-        start = pl.multiple_of(lax.rem(x + 4 - hop_of(slot), 4) * POS, POS)
+        start = pl.multiple_of((x ^ hop_of(slot)) * POS, POS)
         out[pl.ds(start, POS), 0:128] = one[0:256]
         out[pl.ds(start, POS), 128:256] = one[256:512]
         tail = spread_tail(one[512:640].astype(F32))
@@ -461,23 +469,20 @@
 def swap_x(values):
     out = [values[0]]
     for slot in (1, 2, 3):
-        out.append(moved(values[slot], lambda y, x, frame: (y, (x + hop_on(slot, frame % 2)) % 4, frame)))
+        out.append(moved(values[slot], lambda y, x, frame: (y, x ^ hop_on(slot, frame % 2), frame)))
     return out
 
 
 def gather_y(value):
     out = []
     for slot in (1, 2, 3):
-        out.append(moved(value, lambda y, x, frame: ((y + hop_on(slot, frame % 2)) % 4, x, frame)))
+        out.append(moved(value, lambda y, x, frame: (y ^ hop_on(slot, frame % 2), x, frame)))
     return out
 
 
-def along_x(value, hop):
-    return moved(value, lambda y, x, frame: (y, (x + hop) % 4, frame))
-
-
-def along_frame(value, hop):
-    return moved(value, lambda y, x, frame: (y, x, (frame + hop) % 16))
+def beside(value):
+    there = moved(value, lambda y, x, frame: (y, x, (frame + (1 if frame % 2 else 15)) % 16))
+    return there, moved(value, lambda y, x, frame: (y, x, frame ^ 1))
 
 
 def embedding_of(step_index, half_dim):
@@ -504,7 +509,7 @@
     )
     arrived = swap_x(outgoing)
     nq, sp = call(norm_start_kernel, [((800, 128), BF16), (packed, BF16)], start, gain, bias)
-    before, after = along_frame(nq, 1), along_frame(nq, -1)
+    there, mate = beside(nq)
     taps = ((320, 1024), BF16)
     a3 = ((256, 1024), BF16)
     pre = (256, 320)
@@ -518,7 +523,7 @@
         sems=25,
     )
     sides = call(
-        first_sides_kernel, [((2,) + pre, F32)], before, after, wp, wt, scratch=(taps,), flops=1024 * 320 * 2880
+        first_sides_kernel, [((2,) + pre, F32)], there, mate, wp, wt, scratch=(taps,), flops=1024 * 320 * 2880
     )[0]
     rt, noises, tb = call(
         first_total_kernel,
@@ -531,21 +536,21 @@
     prefix = call(
         first_prefix_kernel, [(four, F32)], here, sides, tb, tp, noises, scratch=(a3,), flops=1536 * 320 * 960
     )[0]
-    states, up, down, far = call(
+    states, *halos = call(
         states_kernel,
         [(four, BF16), ((464, 128), BF16), ((464, 128), BF16), ((72, 128), BF16)],
         sp, prefix, *totals,
     )
-    edges = along_x(up, 1), along_x(down, -1), along_x(far, 2), far
+    _, halo1, far, halo3 = swap_x((None, halos[0], halos[2], halos[1]))
     own, total = call(
         second_sweep_kernel,
         [(four, BF16), (packed, BF16)],
-        states, *edges, gain, bias, wp, wt, tb,
+        states, halo1, halo3, far, halos[2], gain, bias, wp, wt, tb,
         scratch=(taps, ((4, 8, 384), F32)),
         flops=2048 * 320 * 2880,
     )
-    sums = total, along_frame(total, 1), along_frame(total, -1)
-    parts = own, along_frame(own, 1), along_frame(own, -1)
+    sums = total, *beside(total)
+    parts = own, *beside(own)
     rt = call(second_total_kernel, [(packed, BF16)], *sums, tp, noises, scratch=(a3,), flops=512 * 320 * 960)[0]
     totals = gather_y(rt)
     prefix = call(second_prefix_kernel, [(four, F32)], *parts, tp, noises, scratch=(a3,), flops=2048 * 320 * 960)[0]

time: 83.4 us -> 84.7 us (1.016)
  the two profiles are of different devices: /device:TPU:6 before, /device:TPU:1 now
where the time goes in v5:
time: 84.7 us; the launch traced here: 84.6 us
  waiting for transfers between devices  32.5 us (38%)
  starting transfers between devices  32.1 us (38%)
  Pallas kernels  19.1 us (23%)
    ppermute x21, waiting for transfers between devices, moved(): return lax.ppermute(value, AXES, pairs)  32.5 us
    ppermute x21, starting transfers between devices, moved(): return lax.ppermute(value, AXES, pairs)  32.1 us
    pallas_call x12, Pallas kernels, call(): pl.pallas_call(body, out_shape=shapes, in_specs=[pl.BlockSpec(memory_spac...  19.1 us
  transfers between devices with their start and end apart: 21, of which 12 were waited for; matrix products, arithmetic and copies ran while one was open for 0% of the time, Pallas kernels for 9%

profile of v5, /device:TPU:1, one launch (start us, length us, event | category | flops | bytes accessed | tf_op | source)
XLA Modules:
  0.0 84.6 jit_solution(4921089999078175652)
XLA Ops:
  0.7 0.1 sine_convert_fusion
  0.7 0.1 fusion.2
  0.8 1.6 %shard_map.82 = (bf16[688,128]{1,0:T(8,128)(2,1)S(1)}, bf16[688,128]{1,0:T(8,128)(2,1)S(1)}, bf16[688,128]{1,0:T(8,128)(2,1)S(1)}, bf16[688,128]{1,0:T(8,128)(2,...) custom-call(bf16[1024,320]{1,0:T(8,128)(2,1)} %bitcast.4, bf16[1024,320]{1,0:T(8,128)(2,1)} %bitcast.5, ...), custom_call_target="tpu_custom_call" | custom-call | bytes 2688000 | tf_op jit(solution)/shard_map/pallas_call | solution.py:443
  2.4 0.9 %shard_map.83 = (bf16[800,128]{1,0:T(8,128)(2,1)S(1)}, bf16[640,128]{1,0:T(8,128)(2,1)S(1)}) custom-call(bf16[1024,320]{1,0:T(8,128)(2,1)S(1)} %get-tuple-element.32.start, f32[320]{0:T(512)S(1)} %get-tuple-element.33.gain_ref, f32[320]{0:T(512)S(1)} %get-tuple-element.34.bias_ref), custom_call_target="tpu_custom_call" | custom-call | bytes 1026560 | tf_op jit(solution)/shard_map/pallas_call | solution.py:443
  3.3 3.3 %collective-permute-start.1 = (bf16[800,128]{1,0:T(8,128)(2,1)S(1)}, bf16[800,128]{1,0:T(8,128)(2,1)S(1)}, u32[]{:S(2)}, u32[]{:S(2)}) collective-permute-start(bf16[800,128]{1,0:T(8,128)(2,1)S(1)} %get-tuple-element.36.normed), channel_id=1, source_target_pairs={{0,1},{1,0},{2,3},{3,2},{4,5},{5,4},{6,7},{7,6},{8,9},{9,8},{10,11... | collective-permute-start | bytes 614408 | tf_op jit(solution)/shard_map/ppermute | solution.py:462
  6.6 0.0 collective-permute-start
  6.6 2.4 %collective-permute-start.2 = (bf16[688,128]{1,0:T(8,128)(2,1)S(1)}, bf16[688,128]{1,0:T(8,128)(2,1)S(1)}, u32[]{:S(2)}, u32[]{:S(2)}) collective-permute-start(bf16[688,128]{1,0:T(8,128)(2,1)S(1)} %get-tuple-element.43), channel_id=1, source_target_pairs={{0,16},{1,49},{2,18},{3,51},{4,20},{5,53},{6,22},{7,55},{8,24},{9,... | collective-permute-start | bytes 528392 | tf_op jit(solution)/shard_map/ppermute | solution.py:462
  9.0 0.5 collective-permute-start.3
  9.5 0.3 collective-permute-start.4
  9.9 2.8 %shard_map.84 = (f32[1,256,320]{2,1,0:T(8,128)S(1)}, bf16[3,1024,320]{2,1,0:T(8,128)(2,1)S(1)}, bf16[1024,192]{1,0:T(8,128)(2,1)S(1)}, bf16[1024,320]{1,0:T(8,128)(2,1)S(1)}, bf16[320,320]{1,0:T(8,128)(2,1)S(1)}) custom-call(bf16[3,3,320,320]{3,2,1,0:T(8,128)(2,1)} %sw.1, bf16[3,320,320]{2,1,0:T(8,128)(2,1)} %tw.1, bf16[320,320]{1,0:T(8,128)(2,1)} %tew_hbm.1, ...), custom_call_target="tpu_custom_call" | custom-call | flops 471859200 | bytes 6414336 | tf_op jit(solution)/shard_map/pallas_call | solution.py:443
  12.6 0.0 collective-permute-done.1.after
  12.6 0.0 collective-permute-done.before
  12.7 1.6 %shard_map.85.sides = f32[2,256,320]{2,1,0:T(8,128)S(1)} custom-call(bf16[800,128]{1,0:T(8,128)(2,1)S(1)} %collective-permute-done.before, bf16[800,128]{1,0:T(8,128)(2,1)S(1)} %collective-permute-done.1.after, bf16[3,1024,320]{2,1,0:T(8,128)(2,1)S(1)} %get-tuple-element.38.wp, bf16[1024,192]{1,0:T(8,128)(2,1)S(1)} %get-tuple-element.39.wt), custom_call_target="tpu_custom_call" | custom-call | flops 943718400 | bytes 3424256 | tf_op jit(solution)/shard_map/pallas_call | solution.py:443
  14.2 0.0 collective-permute-done.2.n1
  14.2 0.6 collective-permute-done.3.n2
  14.8 1.0 %collective-permute-done.4.n3 = bf16[688,128]{1,0:T(8,128)(2,1)S(1)} collective-permute-done((bf16[688,128]{1,0:T(8,128)(2,1)S(1)}, bf16[688,128]{1,0:T(8,128)(2,1)S(1)}, u32[]{:S(2)}, u32[]{:S(2)}) %collective-permute-start.4) | collective-permute-done | bytes 176160 | tf_op jit(solution)/shard_map/ppermute | solution.py:462
  15.8 1.6 %shard_map.86 = (bf16[640,128]{1,0:T(8,128)(2,1)S(1)}, bf16[4,640,128]{2,1,0:T(8,128)(2,1)S(1)}, f32[4,16,320]{2,1,0:T(8,128)S(1)}) custom-call(f32[1,256,320]{2,1,0:T(8,128)S(1)} %get-tuple-element.37.here, f32[2,256,320]{2,1,0:T(8,128)S(1)} %shard_map.85.sides, bf16[1024,320]{1,0:T(8,128)(2,1)S(1)} %get-tuple-element.40.tp, ...), custom_call_target="tpu_custom_call" | custom-call | flops 157286400 | bytes 3448832 | tf_op jit(solution)/shard_map/pallas_call | solution.py:443
  17.4 1.2 %collective-permute-start.7 = (bf16[640,128]{1,0:T(8,128)(2,1)S(1)}, bf16[640,128]{1,0:T(8,128)(2,1)S(1)}, u32[]{:S(2)}, u32[]{:S(2)}) collective-permute-start(bf16[640,128]{1,0:T(8,128)(2,1)S(1)} %get-tuple-element.48), channel_id=1, source_target_pairs={{0,192},{1,65},{2,194},{3,67},{4,196},{5,69},{6,198},{7,71},{8,200... | collective-permute-start | bytes 491528 | tf_op jit(solution)/shard_map/ppermute | solution.py:462
  18.6 2.6 %collective-permute-start.6 = (bf16[640,128]{1,0:T(8,128)(2,1)S(1)}, bf16[640,128]{1,0:T(8,128)(2,1)S(1)}, u32[]{:S(2)}, u32[]{:S(2)}) collective-permute-start(bf16[640,128]{1,0:T(8,128)(2,1)S(1)} %get-tuple-element.48), channel_id=1, source_target_pairs={{0,128},{1,129},{2,130},{3,131},{4,132},{5,133},{6,134},{7,135},{8... | collective-permute-start | bytes 491528 | tf_op jit(solution)/shard_map/ppermute | solution.py:462
  21.2 0.1 collective-permute-start.5
  21.3 1.5 %shard_map.87.prefix = f32[4,640,128]{2,1,0:T(8,128)S(1)} custom-call(f32[1,256,320]{2,1,0:T(8,128)S(1)} %get-tuple-element.37.here, f32[2,256,320]{2,1,0:T(8,128)S(1)} %shard_map.85.sides, f32[4,16,320]{2,1,0:T(8,128)S(1)} %get-tuple-element.46.tb, bf16[1024,320]{1,0:T(8,128)(2,1)S(1)} %get-tuple-element.40.tp, bf16[4,640,128]{2,1,0:T(8,128)(2,1)S(1)} %get-tuple-element.47.noise), custom_call_target="tpu_custom_call" | custom-call | flops 471859200 | bytes 3686400 | tf_op jit(solution)/shard_map/pallas_call | solution.py:443
  22.9 0.0 collective-permute-done.7.r3
  22.9 2.9 %collective-permute-done.6.r2 = bf16[640,128]{1,0:T(8,128)(2,1)S(1)} collective-permute-done((bf16[640,128]{1,0:T(8,128)(2,1)S(1)}, bf16[640,128]{1,0:T(8,128)(2,1)S(1)}, u32[]{:S(2)}, u32[]{:S(2)}) %collective-permute-start.6) | collective-permute-done | bytes 163872 | tf_op jit(solution)/shard_map/ppermute | solution.py:462
  25.8 1.7 %collective-permute-done.5.r1 = bf16[640,128]{1,0:T(8,128)(2,1)S(1)} collective-permute-done((bf16[640,128]{1,0:T(8,128)(2,1)S(1)}, bf16[640,128]{1,0:T(8,128)(2,1)S(1)}, u32[]{:S(2)}, u32[]{:S(2)}) %collective-permute-start.5) | collective-permute-done | bytes 163872 | tf_op jit(solution)/shard_map/ppermute | solution.py:462
  27.4 1.1 %shard_map.88 = (bf16[4,640,128]{2,1,0:T(8,128)(2,1)S(1)}, bf16[464,128]{1,0:T(8,128)(2,1)S(1)}, bf16[464,128]{1,0:T(8,128)(2,1)S(1)}, bf16[72,128]{1,0:T(8,128)(2,1)S(1)}) custom-call(bf16[640,128]{1,0:T(8,128)(2,1)S(1)} %get-tuple-element.35.sp, f32[4,640,128]{2,1,0:T(8,128)S(1)} %shard_map.87.prefix, bf16[640,128]{1,0:T(8,128)(2,1)S(1)} %collective-permute-done.5.r1, ...), custom_call_target="tpu_custom_call" | custom-call | bytes 2877440 | tf_op jit(solution)/shard_map/pallas_call | solution.py:443
  28.5 3.4 %collective-permute-start.8 = (bf16[464,128]{1,0:T(8,128)(2,1)S(1)}, bf16[464,128]{1,0:T(8,128)(2,1)S(1)}, u32[]{:S(2)}, u32[]{:S(2)}) collective-permute-start(bf16[464,128]{1,0:T(8,128)(2,1)S(1)} %get-tuple-element.50), channel_id=1, source_target_pairs={{0,16},{1,49},{2,18},{3,51},{4,20},{5,53},{6,22},{7,55},{8,24},{9,... | collective-permute-start | bytes 356360 | tf_op jit(solution)/shard_map/ppermute | solution.py:462
  31.9 0.6 collective-permute-start.9
  32.6 0.7 collective-permute-start.10
  33.3 3.4 %collective-permute-done.10.far = bf16[72,128]{1,0:T(8,128)(2,1)S(1)} collective-permute-done((bf16[72,128]{1,0:T(8,128)(2,1)S(1)}, bf16[72,128]{1,0:T(8,128)(2,1)S(1)}, u32[]{:S(2)}, u32[]{:S(2)}) %collective-permute-start.10) | collective-permute-done | bytes 18464 | tf_op jit(solution)/shard_map/ppermute | solution.py:462
  36.7 0.0 collective-permute-done.8.halo1
  36.7 0.0 collective-permute-done.9.halo3
  36.7 4.7 %shard_map.89 = (bf16[4,640,128]{2,1,0:T(8,128)(2,1)S(1)}, bf16[640,128]{1,0:T(8,128)(2,1)S(1)}) custom-call(bf16[4,640,128]{2,1,0:T(8,128)(2,1)S(1)} %get-tuple-element.49.states, bf16[464,128]{1,0:T(8,128)(2,1)S(1)} %collective-permute-done.8.halo1, bf16[464,128]{1,0:T(8,128)(2,1)S(1)} %collective-permute-done.9.halo3, ...), custom_call_target="tpu_custom_call" | custom-call | flops 1887436800 | bytes 4192768 | tf_op jit(solution)/shard_map/pallas_call | solution.py:443
  41.3 5.4 %collective-permute-start.12 = (bf16[4,640,128]{2,1,0:T(8,128)(2,1)S(1)}, bf16[4,640,128]{2,1,0:T(8,128)(2,1)S(1)}, u32[]{:S(2)}, u32[]{:S(2)}) collective-permute-start(bf16[4,640,128]{2,1,0:T(8,128)(2,1)S(1)} %get-tuple-element.53.own), channel_id=1, source_target_pairs={{0,1},{1,0},{2,3},{3,2},{4,5},{5,4},{6,7},{7,6},{8,9},{9,8},{10,11... | collective-permute-start | bytes 1966088 | tf_op jit(solution)/shard_map/ppermute | solution.py:462
  46.8 0.1 collective-permute-start.11
  46.9 4.1 %collective-permute-start.14 = (bf16[640,128]{1,0:T(8,128)(2,1)S(1)}, bf16[640,128]{1,0:T(8,128)(2,1)S(1)}, u32[]{:S(2)}, u32[]{:S(2)}) collective-permute-start(bf16[640,128]{1,0:T(8,128)(2,1)S(1)} %get-tuple-element.54.own), channel_id=1, source_target_pairs={{0,1},{1,0},{2,3},{3,2},{4,5},{5,4},{6,7},{7,6},{8,9},{9,8},{10,11... | collective-permute-start | bytes 491528 | tf_op jit(solution)/shard_map/ppermute | solution.py:462
  50.9 0.0 collective-permute-start.13
  50.9 1.0 %collective-permute-done.14.after = bf16[640,128]{1,0:T(8,128)(2,1)S(1)} collective-permute-done((bf16[640,128]{1,0:T(8,128)(2,1)S(1)}, bf16[640,128]{1,0:T(8,128)(2,1)S(1)}, u32[]{:S(2)}, u32[]{:S(2)}) %collective-permute-start.14) | collective-permute-done | bytes 163872 | tf_op jit(solution)/shard_map/ppermute | solution.py:462
  51.9 6.9 %collective-permute-done.13.before = bf16[640,128]{1,0:T(8,128)(2,1)S(1)} collective-permute-done((bf16[640,128]{1,0:T(8,128)(2,1)S(1)}, bf16[640,128]{1,0:T(8,128)(2,1)S(1)}, u32[]{:S(2)}, u32[]{:S(2)}) %collective-permute-start.13) | collective-permute-done | bytes 163872 | tf_op jit(solution)/shard_map/ppermute | solution.py:462
  58.8 0.5 shard_map.91
  59.4 0.7 collective-permute-start.17
  60.0 2.6 %collective-permute-start.16 = (bf16[640,128]{1,0:T(8,128)(2,1)S(1)}, bf16[640,128]{1,0:T(8,128)(2,1)S(1)}, u32[]{:S(2)}, u32[]{:S(2)}) collective-permute-start(bf16[640,128]{1,0:T(8,128)(2,1)S(1)} %shard_map.91), channel_id=1, source_target_pairs={{0,128},{1,129},{2,130},{3,131},{4,132},{5,133},{6,134},{7,135},{8... | collective-permute-start | bytes 491528 | tf_op jit(solution)/shard_map/ppermute | solution.py:462
  62.7 0.6 collective-permute-start.15
  63.3 0.0 collective-permute-done.12.after
  63.3 0.0 collective-permute-done.11.before
  63.3 1.6 %shard_map.90.prefix = f32[4,640,128]{2,1,0:T(8,128)S(1)} custom-call(bf16[4,640,128]{2,1,0:T(8,128)(2,1)S(1)} %get-tuple-element.53.own, bf16[4,640,128]{2,1,0:T(8,128)(2,1)S(1)} %collective-permute-done.11.before, bf16[4,640,128]{2,1,0:T(8,128)(2,1)S(1)} %collective-permute-done.12.after, bf16[1024,320]{1,0:T(8,128)(2,1)S(1)} %get-tuple-element.40.tp, ...), custom_call_target="tpu_custom_call" | custom-call | flops 629145600 | bytes 4587520 | tf_op jit(solution)/shard_map/pallas_call | solution.py:443
  64.9 0.0 collective-permute-done.17.r3
  64.9 2.3 %collective-permute-done.16.r2 = bf16[640,128]{1,0:T(8,128)(2,1)S(1)} collective-permute-done((bf16[640,128]{1,0:T(8,128)(2,1)S(1)}, bf16[640,128]{1,0:T(8,128)(2,1)S(1)}, u32[]{:S(2)}, u32[]{:S(2)}) %collective-permute-start.16) | collective-permute-done | bytes 163872 | tf_op jit(solution)/shard_map/ppermute | solution.py:462
  67.2 5.4 %collective-permute-done.15.r1 = bf16[640,128]{1,0:T(8,128)(2,1)S(1)} collective-permute-done((bf16[640,128]{1,0:T(8,128)(2,1)S(1)}, bf16[640,128]{1,0:T(8,128)(2,1)S(1)}, u32[]{:S(2)}, u32[]{:S(2)}) %collective-permute-start.15) | collective-permute-done | bytes 163872 | tf_op jit(solution)/shard_map/ppermute | solution.py:462
  72.6 0.2 shard_map.92
  72.8 2.1 %collective-permute-start.18 = (bf16[640,128]{1,0:T(8,128)(2,1)S(1)}, bf16[640,128]{1,0:T(8,128)(2,1)S(1)}, u32[]{:S(2)}, u32[]{:S(2)}) collective-permute-start(bf16[640,128]{1,0:T(8,128)(2,1)S(1)} %get-tuple-element.56), channel_id=1, source_target_pairs={{0,16},{1,49},{2,18},{3,51},{4,20},{5,53},{6,22},{7,55},{8,24},{9,... | collective-permute-start | bytes 491528 | tf_op jit(solution)/shard_map/ppermute | solution.py:462
  74.9 0.7 collective-permute-start.19
  75.6 0.5 collective-permute-start.20
  76.2 2.1 %collective-permute-done.18.r1 = bf16[640,128]{1,0:T(8,128)(2,1)S(1)} collective-permute-done((bf16[640,128]{1,0:T(8,128)(2,1)S(1)}, bf16[640,128]{1,0:T(8,128)(2,1)S(1)}, u32[]{:S(2)}, u32[]{:S(2)}) %collective-permute-start.18) | collective-permute-done | bytes 163872 | tf_op jit(solution)/shard_map/ppermute | solution.py:462
  78.3 4.3 %collective-permute-done.19.r2 = bf16[640,128]{1,0:T(8,128)(2,1)S(1)} collective-permute-done((bf16[640,128]{1,0:T(8,128)(2,1)S(1)}, bf16[640,128]{1,0:T(8,128)(2,1)S(1)}, u32[]{:S(2)}, u32[]{:S(2)}) %collective-permute-start.19) | collective-permute-done | bytes 163872 | tf_op jit(solution)/shard_map/ppermute | solution.py:462
  82.6 0.9 %collective-permute-done.20.r3 = bf16[640,128]{1,0:T(8,128)(2,1)S(1)} collective-permute-done((bf16[640,128]{1,0:T(8,128)(2,1)S(1)}, bf16[640,128]{1,0:T(8,128)(2,1)S(1)}, u32[]{:S(2)}, u32[]{:S(2)}) %collective-permute-start.20) | collective-permute-done | bytes 163872 | tf_op jit(solution)/shard_map/ppermute | solution.py:462
  83.5 1.1 %shard_map.93 = bf16[1024,320]{1,0:T(8,128)(2,1)} custom-call(bf16[640,128]{1,0:T(8,128)(2,1)S(1)} %get-tuple-element.55.r0, bf16[640,128]{1,0:T(8,128)(2,1)S(1)} %collective-permute-done.18.r1, bf16[640,128]{1,0:T(8,128)(2,1)S(1)} %collective-permute-done.19.r2, bf16[640,128]{1,0:T(8,128)(2,1)S(1)} %collective-permute-done.20.r3), custom_call_target="tpu_custom_call" | custom-call | bytes 1310720 | tf_op jit(solution)/shard_map/pallas_call | solution.py:443
  (1 shorter events, 0.0 us)
Async XLA Ops:
  3.3 9.3 %collective-permute-start.1 = (bf16[800,128]{1,0:T(8,128)(2,1)S(1)}, bf16[800,128]{1,0:T(8,128)(2,1)S(1)}, u32[]{:S(2)}, u32[]{:S(2)}) collective-permute-start(bf16[800,128]{1,0:T(8,128)(2,1)S(1)} %get-tuple-element.36.normed), channel_id=1, source_target_pairs={{0,1},{1,0},{2,3},{3,2},{4,5},{5,4},{6,7},{7,6},{8,9},{9,8},{10,11... | collective-permute-start | bytes 614408 | tf_op jit(solution)/shard_map/ppermute | solution.py:462
  6.6 6.0 %collective-permute-start = (bf16[800,128]{1,0:T(8,128)(2,1)S(1)}, bf16[800,128]{1,0:T(8,128)(2,1)S(1)}, u32[]{:S(2)}, u32[]{:S(2)}) collective-permute-start(bf16[800,128]{1,0:T(8,128)(2,1)S(1)} %get-tuple-element.36.normed), channel_id=1, source_target_pairs={{0,15},{1,2},{2,1},{3,4},{4,3},{5,6},{6,5},{7,8},{8,7},{9,10},{10,... | collective-permute-start | bytes 614408 | tf_op jit(solution)/shard_map/ppermute | solution.py:462
  6.6 7.6 %collective-permute-start.2 = (bf16[688,128]{1,0:T(8,128)(2,1)S(1)}, bf16[688,128]{1,0:T(8,128)(2,1)S(1)}, u32[]{:S(2)}, u32[]{:S(2)}) collective-permute-start(bf16[688,128]{1,0:T(8,128)(2,1)S(1)} %get-tuple-element.43), channel_id=1, source_target_pairs={{0,16},{1,49},{2,18},{3,51},{4,20},{5,53},{6,22},{7,55},{8,24},{9,... | collective-permute-start | bytes 528392 | tf_op jit(solution)/shard_map/ppermute | solution.py:462
  9.0 5.8 %collective-permute-start.3 = (bf16[688,128]{1,0:T(8,128)(2,1)S(1)}, bf16[688,128]{1,0:T(8,128)(2,1)S(1)}, u32[]{:S(2)}, u32[]{:S(2)}) collective-permute-start(bf16[688,128]{1,0:T(8,128)(2,1)S(1)} %get-tuple-element.44), channel_id=1, source_target_pairs={{0,32},{1,33},{2,34},{3,35},{4,36},{5,37},{6,38},{7,39},{8,40},{9,... | collective-permute-start | bytes 528392 | tf_op jit(solution)/shard_map/ppermute | solution.py:462
  9.5 6.3 %collective-permute-start.4 = (bf16[688,128]{1,0:T(8,128)(2,1)S(1)}, bf16[688,128]{1,0:T(8,128)(2,1)S(1)}, u32[]{:S(2)}, u32[]{:S(2)}) collective-permute-start(bf16[688,128]{1,0:T(8,128)(2,1)S(1)} %get-tuple-element.45), channel_id=1, source_target_pairs={{0,48},{1,17},{2,50},{3,19},{4,52},{5,21},{6,54},{7,23},{8,56},{9,... | collective-permute-start | bytes 528392 | tf_op jit(solution)/shard_map/ppermute | solution.py:462
  17.4 5.5 %collective-permute-start.7 = (bf16[640,128]{1,0:T(8,128)(2,1)S(1)}, bf16[640,128]{1,0:T(8,128)(2,1)S(1)}, u32[]{:S(2)}, u32[]{:S(2)}) collective-permute-start(bf16[640,128]{1,0:T(8,128)(2,1)S(1)} %get-tuple-element.48), channel_id=1, source_target_pairs={{0,192},{1,65},{2,194},{3,67},{4,196},{5,69},{6,198},{7,71},{8,200... | collective-permute-start | bytes 491528 | tf_op jit(solution)/shard_map/ppermute | solution.py:462
  18.6 7.2 %collective-permute-start.6 = (bf16[640,128]{1,0:T(8,128)(2,1)S(1)}, bf16[640,128]{1,0:T(8,128)(2,1)S(1)}, u32[]{:S(2)}, u32[]{:S(2)}) collective-permute-start(bf16[640,128]{1,0:T(8,128)(2,1)S(1)} %get-tuple-element.48), channel_id=1, source_target_pairs={{0,128},{1,129},{2,130},{3,131},{4,132},{5,133},{6,134},{7,135},{8... | collective-permute-start | bytes 491528 | tf_op jit(solution)/shard_map/ppermute | solution.py:462
  21.2 6.2 %collective-permute-start.5 = (bf16[640,128]{1,0:T(8,128)(2,1)S(1)}, bf16[640,128]{1,0:T(8,128)(2,1)S(1)}, u32[]{:S(2)}, u32[]{:S(2)}) collective-permute-start(bf16[640,128]{1,0:T(8,128)(2,1)S(1)} %get-tuple-element.48), channel_id=1, source_target_pairs={{0,64},{1,193},{2,66},{3,195},{4,68},{5,197},{6,70},{7,199},{8,72}... | collective-permute-start | bytes 491528 | tf_op jit(solution)/shard_map/ppermute | solution.py:462
  28.5 8.2 %collective-permute-start.8 = (bf16[464,128]{1,0:T(8,128)(2,1)S(1)}, bf16[464,128]{1,0:T(8,128)(2,1)S(1)}, u32[]{:S(2)}, u32[]{:S(2)}) collective-permute-start(bf16[464,128]{1,0:T(8,128)(2,1)S(1)} %get-tuple-element.50), channel_id=1, source_target_pairs={{0,16},{1,49},{2,18},{3,51},{4,20},{5,53},{6,22},{7,55},{8,24},{9,... | collective-permute-start | bytes 356360 | tf_op jit(solution)/shard_map/ppermute | solution.py:462
  31.9 4.8 %collective-permute-start.9 = (bf16[464,128]{1,0:T(8,128)(2,1)S(1)}, bf16[464,128]{1,0:T(8,128)(2,1)S(1)}, u32[]{:S(2)}, u32[]{:S(2)}) collective-permute-start(bf16[464,128]{1,0:T(8,128)(2,1)S(1)} %get-tuple-element.51), channel_id=1, source_target_pairs={{0,48},{1,17},{2,50},{3,19},{4,52},{5,21},{6,54},{7,23},{8,56},{9,... | collective-permute-start | bytes 356360 | tf_op jit(solution)/shard_map/ppermute | solution.py:462
  32.6 4.1 %collective-permute-start.10 = (bf16[72,128]{1,0:T(8,128)(2,1)S(1)}, bf16[72,128]{1,0:T(8,128)(2,1)S(1)}, u32[]{:S(2)}, u32[]{:S(2)}) collective-permute-start(bf16[72,128]{1,0:T(8,128)(2,1)S(1)} %get-tuple-element.52.mine), channel_id=1, source_target_pairs={{0,32},{1,33},{2,34},{3,35},{4,36},{5,37},{6,38},{7,39},{8,40},{9,... | collective-permute-start | bytes 55304 | tf_op jit(solution)/shard_map/ppermute | solution.py:462
  41.3 22.0 %collective-permute-start.12 = (bf16[4,640,128]{2,1,0:T(8,128)(2,1)S(1)}, bf16[4,640,128]{2,1,0:T(8,128)(2,1)S(1)}, u32[]{:S(2)}, u32[]{:S(2)}) collective-permute-start(bf16[4,640,128]{2,1,0:T(8,128)(2,1)S(1)} %get-tuple-element.53.own), channel_id=1, source_target_pairs={{0,1},{1,0},{2,3},{3,2},{4,5},{5,4},{6,7},{7,6},{8,9},{9,8},{10,11... | collective-permute-start | bytes 1966088 | tf_op jit(solution)/shard_map/ppermute | solution.py:462
  46.8 16.5 %collective-permute-start.11 = (bf16[4,640,128]{2,1,0:T(8,128)(2,1)S(1)}, bf16[4,640,128]{2,1,0:T(8,128)(2,1)S(1)}, u32[]{:S(2)}, u32[]{:S(2)}) collective-permute-start(bf16[4,640,128]{2,1,0:T(8,128)(2,1)S(1)} %get-tuple-element.53.own), channel_id=1, source_target_pairs={{0,15},{1,2},{2,1},{3,4},{4,3},{5,6},{6,5},{7,8},{8,7},{9,10},{10,... | collective-permute-start | bytes 1966088 | tf_op jit(solution)/shard_map/ppermute | solution.py:462
  46.9 5.1 %collective-permute-start.14 = (bf16[640,128]{1,0:T(8,128)(2,1)S(1)}, bf16[640,128]{1,0:T(8,128)(2,1)S(1)}, u32[]{:S(2)}, u32[]{:S(2)}) collective-permute-start(bf16[640,128]{1,0:T(8,128)(2,1)S(1)} %get-tuple-element.54.own), channel_id=1, source_target_pairs={{0,1},{1,0},{2,3},{3,2},{4,5},{5,4},{6,7},{7,6},{8,9},{9,8},{10,11... | collective-permute-start | bytes 491528 | tf_op jit(solution)/shard_map/ppermute | solution.py:462
  50.9 7.9 %collective-permute-start.13 = (bf16[640,128]{1,0:T(8,128)(2,1)S(1)}, bf16[640,128]{1,0:T(8,128)(2,1)S(1)}, u32[]{:S(2)}, u32[]{:S(2)}) collective-permute-start(bf16[640,128]{1,0:T(8,128)(2,1)S(1)} %get-tuple-element.54.own), channel_id=1, source_target_pairs={{0,15},{1,2},{2,1},{3,4},{4,3},{5,6},{6,5},{7,8},{8,7},{9,10},{10,... | collective-permute-start | bytes 491528 | tf_op jit(solution)/shard_map/ppermute | solution.py:462
  59.4 5.5 %collective-permute-start.17 = (bf16[640,128]{1,0:T(8,128)(2,1)S(1)}, bf16[640,128]{1,0:T(8,128)(2,1)S(1)}, u32[]{:S(2)}, u32[]{:S(2)}) collective-permute-start(bf16[640,128]{1,0:T(8,128)(2,1)S(1)} %shard_map.91), channel_id=1, source_target_pairs={{0,192},{1,65},{2,194},{3,67},{4,196},{5,69},{6,198},{7,71},{8,200... | collective-permute-start | bytes 491528 | tf_op jit(solution)/shard_map/ppermute | solution.py:462
  60.0 7.2 %collective-permute-start.16 = (bf16[640,128]{1,0:T(8,128)(2,1)S(1)}, bf16[640,128]{1,0:T(8,128)(2,1)S(1)}, u32[]{:S(2)}, u32[]{:S(2)}) collective-permute-start(bf16[640,128]{1,0:T(8,128)(2,1)S(1)} %shard_map.91), channel_id=1, source_target_pairs={{0,128},{1,129},{2,130},{3,131},{4,132},{5,133},{6,134},{7,135},{8... | collective-permute-start | bytes 491528 | tf_op jit(solution)/shard_map/ppermute | solution.py:462
  62.7 10.0 %collective-permute-start.15 = (bf16[640,128]{1,0:T(8,128)(2,1)S(1)}, bf16[640,128]{1,0:T(8,128)(2,1)S(1)}, u32[]{:S(2)}, u32[]{:S(2)}) collective-permute-start(bf16[640,128]{1,0:T(8,128)(2,1)S(1)} %shard_map.91), channel_id=1, source_target_pairs={{0,64},{1,193},{2,66},{3,195},{4,68},{5,197},{6,70},{7,199},{8,72}... | collective-permute-start | bytes 491528 | tf_op jit(solution)/shard_map/ppermute | solution.py:462
  72.8 5.5 %collective-permute-start.18 = (bf16[640,128]{1,0:T(8,128)(2,1)S(1)}, bf16[640,128]{1,0:T(8,128)(2,1)S(1)}, u32[]{:S(2)}, u32[]{:S(2)}) collective-permute-start(bf16[640,128]{1,0:T(8,128)(2,1)S(1)} %get-tuple-element.56), channel_id=1, source_target_pairs={{0,16},{1,49},{2,18},{3,51},{4,20},{5,53},{6,22},{7,55},{8,24},{9,... | collective-permute-start | bytes 491528 | tf_op jit(solution)/shard_map/ppermute | solution.py:462
  74.9 7.7 %collective-permute-start.19 = (bf16[640,128]{1,0:T(8,128)(2,1)S(1)}, bf16[640,128]{1,0:T(8,128)(2,1)S(1)}, u32[]{:S(2)}, u32[]{:S(2)}) collective-permute-start(bf16[640,128]{1,0:T(8,128)(2,1)S(1)} %get-tuple-element.57), channel_id=1, source_target_pairs={{0,32},{1,33},{2,34},{3,35},{4,36},{5,37},{6,38},{7,39},{8,40},{9,... | collective-permute-start | bytes 491528 | tf_op jit(solution)/shard_map/ppermute | solution.py:462
  75.6 7.9 %collective-permute-start.20 = (bf16[640,128]{1,0:T(8,128)(2,1)S(1)}, bf16[640,128]{1,0:T(8,128)(2,1)S(1)}, u32[]{:S(2)}, u32[]{:S(2)}) collective-permute-start(bf16[640,128]{1,0:T(8,128)(2,1)S(1)} %get-tuple-element.58), channel_id=1, source_target_pairs={{0,48},{1,17},{2,50},{3,19},{4,52},{5,21},{6,54},{7,23},{8,56},{9,... | collective-permute-start | bytes 491528 | tf_op jit(solution)/shard_map/ppermute | solution.py:462

commit v6 on v5

--- a/solution.py
+++ b/solution.py
@@ -81,7 +81,21 @@
 
 
 def conv_row(taps, wp, row):
-    return jnp.dot(taps[row * 32 : row * 32 + POS, :], wp[row, :, 0:256], preferred_element_type=F32)
+    return jnp.dot(taps[row * 32 : row * 32 + POS, :], wp[row][:, 0:256], preferred_element_type=F32)
+
+
+def weight_copies(places, out, sems, first):
+    copies = []
+    for place, one in enumerate(places):
+        for source, target in (
+            (one.at[0:256], out.at[place * 256 : place * 256 + 256]),
+            (one.at[256:320], out.at[768 + 64 * place : 832 + 64 * place]),
+        ):
+            copies.append(pltpu.make_async_copy(source, target, sems.at[first + len(copies)]))
+    for copy in copies:
+        copy.start()
+    out[960:1024] = jnp.zeros((64, 320), BF16)
+    return copies
 
 
 def hop_of(slot):
@@ -114,8 +128,9 @@
         copy.wait()
 
 
-def norm_start_kernel(start, gain_ref, bias_ref, nq, sp):
+def norm_start_kernel(sw, start, gain_ref, bias_ref, nq, sp, wp0, sems):
     x = lax.axis_index("x")
+    copies = weight_copies([sw.at[0, place] for place in range(3)], wp0, sems, 0)
     members = same_group(320)
     values = start[...].astype(F32)
     mean = group_sum(jnp.broadcast_to(jnp.sum(values, axis=0, keepdims=True), (8, 320)), members)[0:1] * (1.0 / 10240)
@@ -139,6 +154,8 @@
     sp[0:256] = start[pl.ds(first, POS), 0:128]
     sp[256:512] = start[pl.ds(first, POS), 128:256]
     sp[512:640] = pack_tail(start[pl.ds(first, POS), 256:320].astype(F32)).astype(BF16)
+    for copy in copies:
+        copy.wait()
 
 
 def conv_frame(normed, wp, wt, pre, taps, before_row=None):
@@ -155,46 +172,35 @@
     pre[:, 256:320] = 0.5 * conv_tail(taps, wt)
 
 
-def first_own_kernel(sw, tw, tew_hbm, normed, pre, wp, wt, tp, tew, taps, sems):
+def first_own_kernel(sw, normed, wp0, pre, wp1, wp2, wt, taps, sems):
+    wp = (wp0, wp1, wp2)
+    copies = [weight_copies([sw.at[row, place] for place in range(3)], wp[row], sems, 6 * row - 6) for row in (1, 2)]
+
+    def before_row(row):
+        if row < 3:
+            for copy in copies[row - 1] if row else ():
+                copy.wait()
+        else:
+            wt[...] = jnp.concatenate([one[:, 256:320].astype(F32) for one in wp], axis=1).astype(BF16)
+
+    conv_frame(normed, wp, wt, pre.at[0], taps, before_row)
+
+
+def first_sides_kernel(tw, tew_hbm, there, mate, wp0, wp1, wp2, wt, pre, tp, tew, taps, sems):
     core = lax.axis_index("core")
     frame = lax.axis_index("z") * 2 + core
-    copies = []
-    for row in range(4):
-        out = tp if row == 3 else wp.at[row]
-        for place in range(3):
-            one = tw.at[place + core * (2 - 2 * place)] if row == 3 else sw.at[row, place]
-            for source, target in (
-                (one.at[0:256], out.at[place * 256 : place * 256 + 256]),
-                (one.at[256:320], out.at[768 + 64 * place : 832 + 64 * place]),
-            ):
-                copies.append(pltpu.make_async_copy(source, target, sems.at[len(copies)]))
-    copies.append(pltpu.make_async_copy(tew_hbm, tew, sems.at[24]))
+    copies = weight_copies([tw.at[place + core * (2 - 2 * place)] for place in range(3)], tp, sems, 0)
+    copies.append(pltpu.make_async_copy(tew_hbm, tew, sems.at[6]))
+    copies[-1].start()
+    for place, normed in enumerate((there, mate)):
+        conv_frame(normed, (wp0, wp1, wp2), wt, pre.at[place], taps)
     for copy in copies:
-        copy.start()
-    for row in range(3):
-        wp[row, 960:1024] = jnp.zeros((64, 320), BF16)
-    tp[960:1024] = jnp.zeros((64, 320), BF16)
-
-    def before_row(row):
-        if row < 3:
-            for copy in copies[6 * row : 6 * row + 6]:
-                copy.wait()
-        else:
-            wt[...] = jnp.concatenate([wp[i, :, 256:320].astype(F32) for i in range(3)], axis=1).astype(BF16)
-
-    conv_frame(normed, wp, wt, pre.at[0], taps, before_row)
-    for copy in copies[18:]:
         copy.wait()
 
     @pl.when((frame == 0) | (frame == 15))
     def _():
         tp[0:256] = jnp.zeros((256, 320), BF16)
         tp[768:832] = jnp.zeros((64, 320), BF16)
-
-
-def first_sides_kernel(before, after, wp, wt, pre, taps):
-    for place, normed in enumerate((before, after)):
-        conv_frame(normed, wp, wt, pre.at[place], taps)
 
 
 def silu_half(half):
@@ -334,7 +340,8 @@
     return jnp.concatenate([vector, vector[:, 256:320]], axis=1)
 
 
-def second_sweep_kernel(states, halo1, halo3, far, mine, gain_ref, bias_ref, wp, wt, tb, out, total, taps, scales):
+def second_sweep_kernel(states, halo1, halo3, far, mine, gain_ref, bias_ref, wp0, wp1, wp2, wt, tb, out, total, taps, scales):
+    wp = (wp0, wp1, wp2)
     gain, bias = wide(gain_ref), wide(bias_ref)
     x = lax.axis_index("x")
     ahead = slot_1_is_ahead()
@@ -508,23 +515,37 @@
         sems=7,
     )
     arrived = swap_x(outgoing)
-    nq, sp = call(norm_start_kernel, [((800, 128), BF16), (packed, BF16)], start, gain, bias)
+    weight = ((1024, 320), BF16)
+    nq, sp, wp0 = call(
+        norm_start_kernel,
+        [((800, 128), BF16), (packed, BF16), weight],
+        spatial_weight, start, gain, bias,
+        hbm=1,
+        sems=6,
+    )
     there, mate = beside(nq)
     taps = ((320, 1024), BF16)
     a3 = ((256, 1024), BF16)
     pre = (256, 320)
-    here, wp, wt, tp, tew = call(
+    here, wp1, wp2, wt = call(
         first_own_kernel,
-        [((1,) + pre, F32), ((3, 1024, 320), BF16), ((1024, 192), BF16), ((1024, 320), BF16), ((320, 320), BF16)],
-        spatial_weight, temporal_weight, temb_weight, nq,
+        [((1,) + pre, F32), weight, weight, ((1024, 192), BF16)],
+        spatial_weight, nq, wp0,
         scratch=(taps,),
         flops=512 * 320 * 2880,
-        hbm=3,
-        sems=25,
-    )
-    sides = call(
-        first_sides_kernel, [((2,) + pre, F32)], there, mate, wp, wt, scratch=(taps,), flops=1024 * 320 * 2880
-    )[0]
+        hbm=1,
+        sems=12,
+    )
+    conv_weights = wp0, wp1, wp2, wt
+    sides, tp, tew = call(
+        first_sides_kernel,
+        [((2,) + pre, F32), weight, ((320, 320), BF16)],
+        temporal_weight, temb_weight, there, mate, *conv_weights,
+        scratch=(taps,),
+        flops=1024 * 320 * 2880,
+        hbm=2,
+        sems=7,
+    )
     rt, noises, tb = call(
         first_total_kernel,
         [(packed, BF16), (four, BF16), ((4, 16, 320), F32)],
@@ -545,7 +566,7 @@
     own, total = call(
         second_sweep_kernel,
         [(four, BF16), (packed, BF16)],
-        states, halo1, halo3, far, halos[2], gain, bias, wp, wt, tb,
+        states, halo1, halo3, far, halos[2], gain, bias, *conv_weights, tb,
         scratch=(taps, ((4, 8, 384), F32)),
         flops=2048 * 320 * 2880,
     )

time: 84.7 us -> 85.7 us (1.012)
  Pallas kernels: 19.1 us -> 20.7 us
    pallas_call x12, Pallas kernels: 19.1 us -> 20.7 us  [call(): pl.pallas_call(body, out_shape=shapes, in_specs=[pl.BlockSpec(memory_spac...]
  transfers between devices with their start and end apart: 21 -> 21, of which waited for: 12 -> 11; matrix products, arithmetic and copies ran while one was open for 0% -> 0% of each run, Pallas kernels for 9% -> 10%
where the time goes in v6:
time: 85.7 us; the launch traced here: 85.5 us
  starting transfers between devices  32.1 us (37%)
  waiting for transfers between devices  31.7 us (37%)
  Pallas kernels  20.7 us (24%)
    ppermute x21, starting transfers between devices, moved(): return lax.ppermute(value, AXES, pairs)  32.1 us
    ppermute x21, waiting for transfers between devices, moved(): return lax.ppermute(value, AXES, pairs)  31.7 us
    pallas_call x12, Pallas kernels, call(): pl.pallas_call(body, out_shape=shapes, in_specs=[pl.BlockSpec(memory_spac...  20.7 us
  transfers between devices with their start and end apart: 21, of which 11 were waited for; matrix products, arithmetic and copies ran while one was open for 0% of the time, Pallas kernels for 10%

profile of v6, /device:TPU:1, one launch (start us, length us, event | category | flops | bytes accessed | tf_op | source)
XLA Modules:
  0.0 85.5 jit_solution(15241208025923500809)
XLA Ops:
  0.7 0.1 sine_convert_fusion
  0.7 0.1 fusion.2
  0.8 1.6 %shard_map.82 = (bf16[688,128]{1,0:T(8,128)(2,1)S(1)}, bf16[688,128]{1,0:T(8,128)(2,1)S(1)}, bf16[688,128]{1,0:T(8,128)(2,1)S(1)}, bf16[688,128]{1,0:T(8,128)(2,...) custom-call(bf16[1024,320]{1,0:T(8,128)(2,1)} %bitcast.4, bf16[1024,320]{1,0:T(8,128)(2,1)} %bitcast.5, ...), custom_call_target="tpu_custom_call" | custom-call | bytes 2688000 | tf_op jit(solution)/shard_map/pallas_call | solution.py:450
  2.4 2.0 %shard_map.83 = (bf16[800,128]{1,0:T(8,128)(2,1)S(1)}, bf16[640,128]{1,0:T(8,128)(2,1)S(1)}, bf16[1024,320]{1,0:T(8,128)(2,1)S(1)}) custom-call(bf16[3,3,320,320]{3,2,1,0:T(8,128)(2,1)} %sw.3, bf16[1024,320]{1,0:T(8,128)(2,1)S(1)} %get-tuple-element.35.start, f32[320]{0:T(512)S(1)} %get-tuple-element.36.gain_ref, f32[320]{0:T(512)S(1)} %get-tuple-element.37.bias_ref), custom_call_target="tpu_custom_call" | custom-call | bytes 3525120 | tf_op jit(solution)/shard_map/pallas_call | solution.py:450
  4.4 3.3 %collective-permute-start.1 = (bf16[800,128]{1,0:T(8,128)(2,1)S(1)}, bf16[800,128]{1,0:T(8,128)(2,1)S(1)}, u32[]{:S(2)}, u32[]{:S(2)}) collective-permute-start(bf16[800,128]{1,0:T(8,128)(2,1)S(1)} %get-tuple-element.39.normed), channel_id=1, source_target_pairs={{0,1},{1,0},{2,3},{3,2},{4,5},{5,4},{6,7},{7,6},{8,9},{9,8},{10,11... | collective-permute-start | bytes 614408 | tf_op jit(solution)/shard_map/ppermute | solution.py:469
  7.6 0.0 collective-permute-start
  7.6 2.4 %collective-permute-start.2 = (bf16[688,128]{1,0:T(8,128)(2,1)S(1)}, bf16[688,128]{1,0:T(8,128)(2,1)S(1)}, u32[]{:S(2)}, u32[]{:S(2)}) collective-permute-start(bf16[688,128]{1,0:T(8,128)(2,1)S(1)} %get-tuple-element.49), channel_id=1, source_target_pairs={{0,16},{1,49},{2,18},{3,51},{4,20},{5,53},{6,22},{7,55},{8,24},{9,... | collective-permute-start | bytes 528392 | tf_op jit(solution)/shard_map/ppermute | solution.py:469
  10.0 0.5 collective-permute-start.3
  10.6 0.3 collective-permute-start.4
  10.9 2.3 %shard_map.84 = (f32[1,256,320]{2,1,0:T(8,128)S(1)}, bf16[1024,320]{1,0:T(8,128)(2,1)S(1)}, bf16[1024,320]{1,0:T(8,128)(2,1)S(1)}, bf16[1024,192]{1,0:T(8,128)(2,1)S(1)}) custom-call(bf16[3,3,320,320]{3,2,1,0:T(8,128)(2,1)} %sw.3, bf16[800,128]{1,0:T(8,128)(2,1)S(1)} %get-tuple-element.39.normed, bf16[1024,320]{1,0:T(8,128)(2,1)S(1)} %get-tuple-element.40.wp0), custom_call_target="tpu_custom_call" | custom-call | flops 471859200 | bytes 4734976 | tf_op jit(solution)/shard_map/pallas_call | solution.py:450
  13.2 0.0 collective-permute-done.1.mate
  13.2 0.0 collective-permute-done.there
  13.3 2.8 %shard_map.85 = (f32[2,256,320]{2,1,0:T(8,128)S(1)}, bf16[1024,320]{1,0:T(8,128)(2,1)S(1)}, bf16[320,320]{1,0:T(8,128)(2,1)S(1)}) custom-call(bf16[3,320,320]{2,1,0:T(8,128)(2,1)} %tw.1, bf16[320,320]{1,0:T(8,128)(2,1)} %tew_hbm.1, bf16[800,128]{1,0:T(8,128)(2,1)S(1)} %collective-permute-done.there, bf16[800,128]{1,0:T(8,128)(2,1)S(1)} %collective-permute-done.1.mate, ...), custom_call_target="tpu_custom_call" | custom-call | flops 943718400 | bytes 5103616 | tf_op jit(solution)/shard_map/pallas_call | solution.py:450
  16.1 0.0 collective-permute-done.2.n1
  16.1 0.0 collective-permute-done.3.n2
  16.1 0.7 collective-permute-done.4.n3
  16.8 1.5 %shard_map.86 = (bf16[640,128]{1,0:T(8,128)(2,1)S(1)}, bf16[4,640,128]{2,1,0:T(8,128)(2,1)S(1)}, f32[4,16,320]{2,1,0:T(8,128)S(1)}) custom-call(f32[1,256,320]{2,1,0:T(8,128)S(1)} %get-tuple-element.41.here, f32[2,256,320]{2,1,0:T(8,128)S(1)} %get-tuple-element.45.sides, bf16[1024,320]{1,0:T(8,128)(2,1)S(1)} %get-tuple-element.46.tp, ...), custom_call_target="tpu_custom_call" | custom-call | flops 157286400 | bytes 3448832 | tf_op jit(solution)/shard_map/pallas_call | solution.py:450
  18.4 1.2 %collective-permute-start.7 = (bf16[640,128]{1,0:T(8,128)(2,1)S(1)}, bf16[640,128]{1,0:T(8,128)(2,1)S(1)}, u32[]{:S(2)}, u32[]{:S(2)}) collective-permute-start(bf16[640,128]{1,0:T(8,128)(2,1)S(1)} %get-tuple-element.54), channel_id=1, source_target_pairs={{0,192},{1,65},{2,194},{3,67},{4,196},{5,69},{6,198},{7,71},{8,200... | collective-permute-start | bytes 491528 | tf_op jit(solution)/shard_map/ppermute | solution.py:469
  19.6 2.6 %collective-permute-start.6 = (bf16[640,128]{1,0:T(8,128)(2,1)S(1)}, bf16[640,128]{1,0:T(8,128)(2,1)S(1)}, u32[]{:S(2)}, u32[]{:S(2)}) collective-permute-start(bf16[640,128]{1,0:T(8,128)(2,1)S(1)} %get-tuple-element.54), channel_id=1, source_target_pairs={{0,128},{1,129},{2,130},{3,131},{4,132},{5,133},{6,134},{7,135},{8... | collective-permute-start | bytes 491528 | tf_op jit(solution)/shard_map/ppermute | solution.py:469
  22.2 0.1 collective-permute-start.5
  22.3 1.5 %shard_map.87.prefix = f32[4,640,128]{2,1,0:T(8,128)S(1)} custom-call(f32[1,256,320]{2,1,0:T(8,128)S(1)} %get-tuple-element.41.here, f32[2,256,320]{2,1,0:T(8,128)S(1)} %get-tuple-element.45.sides, f32[4,16,320]{2,1,0:T(8,128)S(1)} %get-tuple-element.52.tb, bf16[1024,320]{1,0:T(8,128)(2,1)S(1)} %get-tuple-element.46.tp, ...), custom_call_target="tpu_custom_call" | custom-call | flops 471859200 | bytes 3686400 | tf_op jit(solution)/shard_map/pallas_call | solution.py:450
  23.9 0.0 collective-permute-done.7.r3
  23.9 2.9 %collective-permute-done.6.r2 = bf16[640,128]{1,0:T(8,128)(2,1)S(1)} collective-permute-done((bf16[640,128]{1,0:T(8,128)(2,1)S(1)}, bf16[640,128]{1,0:T(8,128)(2,1)S(1)}, u32[]{:S(2)}, u32[]{:S(2)}) %collective-permute-start.6) | collective-permute-done | bytes 163872 | tf_op jit(solution)/shard_map/ppermute | solution.py:469
  26.8 1.7 %collective-permute-done.5.r1 = bf16[640,128]{1,0:T(8,128)(2,1)S(1)} collective-permute-done((bf16[640,128]{1,0:T(8,128)(2,1)S(1)}, bf16[640,128]{1,0:T(8,128)(2,1)S(1)}, u32[]{:S(2)}, u32[]{:S(2)}) %collective-permute-start.5) | collective-permute-done | bytes 163872 | tf_op jit(solution)/shard_map/ppermute | solution.py:469
  28.4 1.1 %shard_map.88 = (bf16[4,640,128]{2,1,0:T(8,128)(2,1)S(1)}, bf16[464,128]{1,0:T(8,128)(2,1)S(1)}, bf16[464,128]{1,0:T(8,128)(2,1)S(1)}, bf16[72,128]{1,0:T(8,128)(2,1)S(1)}) custom-call(bf16[640,128]{1,0:T(8,128)(2,1)S(1)} %get-tuple-element.38.sp, f32[4,640,128]{2,1,0:T(8,128)S(1)} %shard_map.87.prefix, bf16[640,128]{1,0:T(8,128)(2,1)S(1)} %collective-permute-done.5.r1, ...), custom_call_target="tpu_custom_call" | custom-call | bytes 2877440 | tf_op jit(solution)/shard_map/pallas_call | solution.py:450
  29.5 3.4 %collective-permute-start.8 = (bf16[464,128]{1,0:T(8,128)(2,1)S(1)}, bf16[464,128]{1,0:T(8,128)(2,1)S(1)}, u32[]{:S(2)}, u32[]{:S(2)}) collective-permute-start(bf16[464,128]{1,0:T(8,128)(2,1)S(1)} %get-tuple-element.56), channel_id=1, source_target_pairs={{0,16},{1,49},{2,18},{3,51},{4,20},{5,53},{6,22},{7,55},{8,24},{9,... | collective-permute-start | bytes 356360 | tf_op jit(solution)/shard_map/ppermute | solution.py:469
  33.0 0.6 collective-permute-start.9
  33.6 0.7 collective-permute-start.10
  34.3 3.4 %collective-permute-done.10.far = bf16[72,128]{1,0:T(8,128)(2,1)S(1)} collective-permute-done((bf16[72,128]{1,0:T(8,128)(2,1)S(1)}, bf16[72,128]{1,0:T(8,128)(2,1)S(1)}, u32[]{:S(2)}, u32[]{:S(2)}) %collective-permute-start.10) | collective-permute-done | bytes 18464 | tf_op jit(solution)/shard_map/ppermute | solution.py:469
  37.7 0.0 collective-permute-done.8.halo1
  37.7 0.0 collective-permute-done.9.halo3
  37.7 4.5 %shard_map.89 = (bf16[4,640,128]{2,1,0:T(8,128)(2,1)S(1)}, bf16[640,128]{1,0:T(8,128)(2,1)S(1)}) custom-call(bf16[4,640,128]{2,1,0:T(8,128)(2,1)S(1)} %get-tuple-element.55.states, bf16[464,128]{1,0:T(8,128)(2,1)S(1)} %collective-permute-done.8.halo1, bf16[464,128]{1,0:T(8,128)(2,1)S(1)} %collective-permute-done.9.halo3, ...), custom_call_target="tpu_custom_call" | custom-call | flops 1887436800 | bytes 4192768 | tf_op jit(solution)/shard_map/pallas_call | solution.py:450
  42.3 5.4 %collective-permute-start.12 = (bf16[4,640,128]{2,1,0:T(8,128)(2,1)S(1)}, bf16[4,640,128]{2,1,0:T(8,128)(2,1)S(1)}, u32[]{:S(2)}, u32[]{:S(2)}) collective-permute-start(bf16[4,640,128]{2,1,0:T(8,128)(2,1)S(1)} %get-tuple-element.59.own), channel_id=1, source_target_pairs={{0,1},{1,0},{2,3},{3,2},{4,5},{5,4},{6,7},{7,6},{8,9},{9,8},{10,11... | collective-permute-start | bytes 1966088 | tf_op jit(solution)/shard_map/ppermute | solution.py:469
  47.7 0.1 collective-permute-start.11
  47.8 4.1 %collective-permute-start.14 = (bf16[640,128]{1,0:T(8,128)(2,1)S(1)}, bf16[640,128]{1,0:T(8,128)(2,1)S(1)}, u32[]{:S(2)}, u32[]{:S(2)}) collective-permute-start(bf16[640,128]{1,0:T(8,128)(2,1)S(1)} %get-tuple-element.60.own), channel_id=1, source_target_pairs={{0,1},{1,0},{2,3},{3,2},{4,5},{5,4},{6,7},{7,6},{8,9},{9,8},{10,11... | collective-permute-start | bytes 491528 | tf_op jit(solution)/shard_map/ppermute | solution.py:469
  51.8 0.0 collective-permute-start.13
  51.8 1.0 %collective-permute-done.14.after = bf16[640,128]{1,0:T(8,128)(2,1)S(1)} collective-permute-done((bf16[640,128]{1,0:T(8,128)(2,1)S(1)}, bf16[640,128]{1,0:T(8,128)(2,1)S(1)}, u32[]{:S(2)}, u32[]{:S(2)}) %collective-permute-start.14) | collective-permute-done | bytes 163872 | tf_op jit(solution)/shard_map/ppermute | solution.py:469
  52.9 6.9 %collective-permute-done.13.before = bf16[640,128]{1,0:T(8,128)(2,1)S(1)} collective-permute-done((bf16[640,128]{1,0:T(8,128)(2,1)S(1)}, bf16[640,128]{1,0:T(8,128)(2,1)S(1)}, u32[]{:S(2)}, u32[]{:S(2)}) %collective-permute-start.13) | collective-permute-done | bytes 163872 | tf_op jit(solution)/shard_map/ppermute | solution.py:469
  59.7 0.5 shard_map.91
  60.3 0.7 collective-permute-start.17
  61.0 2.6 %collective-permute-start.16 = (bf16[640,128]{1,0:T(8,128)(2,1)S(1)}, bf16[640,128]{1,0:T(8,128)(2,1)S(1)}, u32[]{:S(2)}, u32[]{:S(2)}) collective-permute-start(bf16[640,128]{1,0:T(8,128)(2,1)S(1)} %shard_map.91), channel_id=1, source_target_pairs={{0,128},{1,129},{2,130},{3,131},{4,132},{5,133},{6,134},{7,135},{8... | collective-permute-start | bytes 491528 | tf_op jit(solution)/shard_map/ppermute | solution.py:469
  63.6 0.6 collective-permute-start.15
  64.2 0.0 collective-permute-done.12.after
  64.2 0.0 collective-permute-done.11.before
  64.2 1.5 %shard_map.90.prefix = f32[4,640,128]{2,1,0:T(8,128)S(1)} custom-call(bf16[4,640,128]{2,1,0:T(8,128)(2,1)S(1)} %get-tuple-element.59.own, bf16[4,640,128]{2,1,0:T(8,128)(2,1)S(1)} %collective-permute-done.11.before, bf16[4,640,128]{2,1,0:T(8,128)(2,1)S(1)} %collective-permute-done.12.after, bf16[1024,320]{1,0:T(8,128)(2,1)S(1)} %get-tuple-element.46.tp, ...), custom_call_target="tpu_custom_call" | custom-call | flops 629145600 | bytes 4587520 | tf_op jit(solution)/shard_map/pallas_call | solution.py:450
  65.8 0.0 collective-permute-done.17.r3
  65.8 2.4 %collective-permute-done.16.r2 = bf16[640,128]{1,0:T(8,128)(2,1)S(1)} collective-permute-done((bf16[640,128]{1,0:T(8,128)(2,1)S(1)}, bf16[640,128]{1,0:T(8,128)(2,1)S(1)}, u32[]{:S(2)}, u32[]{:S(2)}) %collective-permute-start.16) | collective-permute-done | bytes 163872 | tf_op jit(solution)/shard_map/ppermute | solution.py:469
  68.1 5.4 %collective-permute-done.15.r1 = bf16[640,128]{1,0:T(8,128)(2,1)S(1)} collective-permute-done((bf16[640,128]{1,0:T(8,128)(2,1)S(1)}, bf16[640,128]{1,0:T(8,128)(2,1)S(1)}, u32[]{:S(2)}, u32[]{:S(2)}) %collective-permute-start.15) | collective-permute-done | bytes 163872 | tf_op jit(solution)/shard_map/ppermute | solution.py:469
  73.5 0.2 shard_map.92
  73.7 2.1 %collective-permute-start.18 = (bf16[640,128]{1,0:T(8,128)(2,1)S(1)}, bf16[640,128]{1,0:T(8,128)(2,1)S(1)}, u32[]{:S(2)}, u32[]{:S(2)}) collective-permute-start(bf16[640,128]{1,0:T(8,128)(2,1)S(1)} %get-tuple-element.62), channel_id=1, source_target_pairs={{0,16},{1,49},{2,18},{3,51},{4,20},{5,53},{6,22},{7,55},{8,24},{9,... | collective-permute-start | bytes 491528 | tf_op jit(solution)/shard_map/ppermute | solution.py:469
  75.8 0.8 collective-permute-start.19
  76.6 0.5 collective-permute-start.20
  77.1 2.1 %collective-permute-done.18.r1 = bf16[640,128]{1,0:T(8,128)(2,1)S(1)} collective-permute-done((bf16[640,128]{1,0:T(8,128)(2,1)S(1)}, bf16[640,128]{1,0:T(8,128)(2,1)S(1)}, u32[]{:S(2)}, u32[]{:S(2)}) %collective-permute-start.18) | collective-permute-done | bytes 163872 | tf_op jit(solution)/shard_map/ppermute | solution.py:469
  79.2 4.3 %collective-permute-done.19.r2 = bf16[640,128]{1,0:T(8,128)(2,1)S(1)} collective-permute-done((bf16[640,128]{1,0:T(8,128)(2,1)S(1)}, bf16[640,128]{1,0:T(8,128)(2,1)S(1)}, u32[]{:S(2)}, u32[]{:S(2)}) %collective-permute-start.19) | collective-permute-done | bytes 163872 | tf_op jit(solution)/shard_map/ppermute | solution.py:469
  83.5 0.9 %collective-permute-done.20.r3 = bf16[640,128]{1,0:T(8,128)(2,1)S(1)} collective-permute-done((bf16[640,128]{1,0:T(8,128)(2,1)S(1)}, bf16[640,128]{1,0:T(8,128)(2,1)S(1)}, u32[]{:S(2)}, u32[]{:S(2)}) %collective-permute-start.20) | collective-permute-done | bytes 163872 | tf_op jit(solution)/shard_map/ppermute | solution.py:469
  84.4 1.1 %shard_map.93 = bf16[1024,320]{1,0:T(8,128)(2,1)} custom-call(bf16[640,128]{1,0:T(8,128)(2,1)S(1)} %get-tuple-element.61.r0, bf16[640,128]{1,0:T(8,128)(2,1)S(1)} %collective-permute-done.18.r1, bf16[640,128]{1,0:T(8,128)(2,1)S(1)} %collective-permute-done.19.r2, bf16[640,128]{1,0:T(8,128)(2,1)S(1)} %collective-permute-done.20.r3), custom_call_target="tpu_custom_call" | custom-call | bytes 1310720 | tf_op jit(solution)/shard_map/pallas_call | solution.py:450
  (1 shorter events, 0.0 us)
Async XLA Ops:
  4.4 8.9 %collective-permute-start.1 = (bf16[800,128]{1,0:T(8,128)(2,1)S(1)}, bf16[800,128]{1,0:T(8,128)(2,1)S(1)}, u32[]{:S(2)}, u32[]{:S(2)}) collective-permute-start(bf16[800,128]{1,0:T(8,128)(2,1)S(1)} %get-tuple-element.39.normed), channel_id=1, source_target_pairs={{0,1},{1,0},{2,3},{3,2},{4,5},{5,4},{6,7},{7,6},{8,9},{9,8},{10,11... | collective-permute-start | bytes 614408 | tf_op jit(solution)/shard_map/ppermute | solution.py:469
  7.6 5.6 %collective-permute-start = (bf16[800,128]{1,0:T(8,128)(2,1)S(1)}, bf16[800,128]{1,0:T(8,128)(2,1)S(1)}, u32[]{:S(2)}, u32[]{:S(2)}) collective-permute-start(bf16[800,128]{1,0:T(8,128)(2,1)S(1)} %get-tuple-element.39.normed), channel_id=1, source_target_pairs={{0,15},{1,2},{2,1},{3,4},{4,3},{5,6},{6,5},{7,8},{8,7},{9,10},{10,... | collective-permute-start | bytes 614408 | tf_op jit(solution)/shard_map/ppermute | solution.py:469
  7.6 8.5 %collective-permute-start.2 = (bf16[688,128]{1,0:T(8,128)(2,1)S(1)}, bf16[688,128]{1,0:T(8,128)(2,1)S(1)}, u32[]{:S(2)}, u32[]{:S(2)}) collective-permute-start(bf16[688,128]{1,0:T(8,128)(2,1)S(1)} %get-tuple-element.49), channel_id=1, source_target_pairs={{0,16},{1,49},{2,18},{3,51},{4,20},{5,53},{6,22},{7,55},{8,24},{9,... | collective-permute-start | bytes 528392 | tf_op jit(solution)/shard_map/ppermute | solution.py:469
  10.0 6.1 %collective-permute-start.3 = (bf16[688,128]{1,0:T(8,128)(2,1)S(1)}, bf16[688,128]{1,0:T(8,128)(2,1)S(1)}, u32[]{:S(2)}, u32[]{:S(2)}) collective-permute-start(bf16[688,128]{1,0:T(8,128)(2,1)S(1)} %get-tuple-element.50), channel_id=1, source_target_pairs={{0,32},{1,33},{2,34},{3,35},{4,36},{5,37},{6,38},{7,39},{8,40},{9,... | collective-permute-start | bytes 528392 | tf_op jit(solution)/shard_map/ppermute | solution.py:469
  10.6 6.3 %collective-permute-start.4 = (bf16[688,128]{1,0:T(8,128)(2,1)S(1)}, bf16[688,128]{1,0:T(8,128)(2,1)S(1)}, u32[]{:S(2)}, u32[]{:S(2)}) collective-permute-start(bf16[688,128]{1,0:T(8,128)(2,1)S(1)} %get-tuple-element.51), channel_id=1, source_target_pairs={{0,48},{1,17},{2,50},{3,19},{4,52},{5,21},{6,54},{7,23},{8,56},{9,... | collective-permute-start | bytes 528392 | tf_op jit(solution)/shard_map/ppermute | solution.py:469
  18.4 5.5 %collective-permute-start.7 = (bf16[640,128]{1,0:T(8,128)(2,1)S(1)}, bf16[640,128]{1,0:T(8,128)(2,1)S(1)}, u32[]{:S(2)}, u32[]{:S(2)}) collective-permute-start(bf16[640,128]{1,0:T(8,128)(2,1)S(1)} %get-tuple-element.54), channel_id=1, source_target_pairs={{0,192},{1,65},{2,194},{3,67},{4,196},{5,69},{6,198},{7,71},{8,200... | collective-permute-start | bytes 491528 | tf_op jit(solution)/shard_map/ppermute | solution.py:469
  19.6 7.2 %collective-permute-start.6 = (bf16[640,128]{1,0:T(8,128)(2,1)S(1)}, bf16[640,128]{1,0:T(8,128)(2,1)S(1)}, u32[]{:S(2)}, u32[]{:S(2)}) collective-permute-start(bf16[640,128]{1,0:T(8,128)(2,1)S(1)} %get-tuple-element.54), channel_id=1, source_target_pairs={{0,128},{1,129},{2,130},{3,131},{4,132},{5,133},{6,134},{7,135},{8... | collective-permute-start | bytes 491528 | tf_op jit(solution)/shard_map/ppermute | solution.py:469
  22.2 6.2 %collective-permute-start.5 = (bf16[640,128]{1,0:T(8,128)(2,1)S(1)}, bf16[640,128]{1,0:T(8,128)(2,1)S(1)}, u32[]{:S(2)}, u32[]{:S(2)}) collective-permute-start(bf16[640,128]{1,0:T(8,128)(2,1)S(1)} %get-tuple-element.54), channel_id=1, source_target_pairs={{0,64},{1,193},{2,66},{3,195},{4,68},{5,197},{6,70},{7,199},{8,72}... | collective-permute-start | bytes 491528 | tf_op jit(solution)/shard_map/ppermute | solution.py:469
  29.5 8.2 %collective-permute-start.8 = (bf16[464,128]{1,0:T(8,128)(2,1)S(1)}, bf16[464,128]{1,0:T(8,128)(2,1)S(1)}, u32[]{:S(2)}, u32[]{:S(2)}) collective-permute-start(bf16[464,128]{1,0:T(8,128)(2,1)S(1)} %get-tuple-element.56), channel_id=1, source_target_pairs={{0,16},{1,49},{2,18},{3,51},{4,20},{5,53},{6,22},{7,55},{8,24},{9,... | collective-permute-start | bytes 356360 | tf_op jit(solution)/shard_map/ppermute | solution.py:469
  33.0 4.7 %collective-permute-start.9 = (bf16[464,128]{1,0:T(8,128)(2,1)S(1)}, bf16[464,128]{1,0:T(8,128)(2,1)S(1)}, u32[]{:S(2)}, u32[]{:S(2)}) collective-permute-start(bf16[464,128]{1,0:T(8,128)(2,1)S(1)} %get-tuple-element.57), channel_id=1, source_target_pairs={{0,48},{1,17},{2,50},{3,19},{4,52},{5,21},{6,54},{7,23},{8,56},{9,... | collective-permute-start | bytes 356360 | tf_op jit(solution)/shard_map/ppermute | solution.py:469
  33.6 4.1 %collective-permute-start.10 = (bf16[72,128]{1,0:T(8,128)(2,1)S(1)}, bf16[72,128]{1,0:T(8,128)(2,1)S(1)}, u32[]{:S(2)}, u32[]{:S(2)}) collective-permute-start(bf16[72,128]{1,0:T(8,128)(2,1)S(1)} %get-tuple-element.58.mine), channel_id=1, source_target_pairs={{0,32},{1,33},{2,34},{3,35},{4,36},{5,37},{6,38},{7,39},{8,40},{9,... | collective-permute-start | bytes 55304 | tf_op jit(solution)/shard_map/ppermute | solution.py:469
  42.3 22.0 %collective-permute-start.12 = (bf16[4,640,128]{2,1,0:T(8,128)(2,1)S(1)}, bf16[4,640,128]{2,1,0:T(8,128)(2,1)S(1)}, u32[]{:S(2)}, u32[]{:S(2)}) collective-permute-start(bf16[4,640,128]{2,1,0:T(8,128)(2,1)S(1)} %get-tuple-element.59.own), channel_id=1, source_target_pairs={{0,1},{1,0},{2,3},{3,2},{4,5},{5,4},{6,7},{7,6},{8,9},{9,8},{10,11... | collective-permute-start | bytes 1966088 | tf_op jit(solution)/shard_map/ppermute | solution.py:469
  47.7 16.5 %collective-permute-start.11 = (bf16[4,640,128]{2,1,0:T(8,128)(2,1)S(1)}, bf16[4,640,128]{2,1,0:T(8,128)(2,1)S(1)}, u32[]{:S(2)}, u32[]{:S(2)}) collective-permute-start(bf16[4,640,128]{2,1,0:T(8,128)(2,1)S(1)} %get-tuple-element.59.own), channel_id=1, source_target_pairs={{0,15},{1,2},{2,1},{3,4},{4,3},{5,6},{6,5},{7,8},{8,7},{9,10},{10,... | collective-permute-start | bytes 1966088 | tf_op jit(solution)/shard_map/ppermute | solution.py:469
  47.8 5.1 %collective-permute-start.14 = (bf16[640,128]{1,0:T(8,128)(2,1)S(1)}, bf16[640,128]{1,0:T(8,128)(2,1)S(1)}, u32[]{:S(2)}, u32[]{:S(2)}) collective-permute-start(bf16[640,128]{1,0:T(8,128)(2,1)S(1)} %get-tuple-element.60.own), channel_id=1, source_target_pairs={{0,1},{1,0},{2,3},{3,2},{4,5},{5,4},{6,7},{7,6},{8,9},{9,8},{10,11... | collective-permute-start | bytes 491528 | tf_op jit(solution)/shard_map/ppermute | solution.py:469
  51.8 7.9 %collective-permute-start.13 = (bf16[640,128]{1,0:T(8,128)(2,1)S(1)}, bf16[640,128]{1,0:T(8,128)(2,1)S(1)}, u32[]{:S(2)}, u32[]{:S(2)}) collective-permute-start(bf16[640,128]{1,0:T(8,128)(2,1)S(1)} %get-tuple-element.60.own), channel_id=1, source_target_pairs={{0,15},{1,2},{2,1},{3,4},{4,3},{5,6},{6,5},{7,8},{8,7},{9,10},{10,... | collective-permute-start | bytes 491528 | tf_op jit(solution)/shard_map/ppermute | solution.py:469
  60.3 5.5 %collective-permute-start.17 = (bf16[640,128]{1,0:T(8,128)(2,1)S(1)}, bf16[640,128]{1,0:T(8,128)(2,1)S(1)}, u32[]{:S(2)}, u32[]{:S(2)}) collective-permute-start(bf16[640,128]{1,0:T(8,128)(2,1)S(1)} %shard_map.91), channel_id=1, source_target_pairs={{0,192},{1,65},{2,194},{3,67},{4,196},{5,69},{6,198},{7,71},{8,200... | collective-permute-start | bytes 491528 | tf_op jit(solution)/shard_map/ppermute | solution.py:469
  61.0 7.2 %collective-permute-start.16 = (bf16[640,128]{1,0:T(8,128)(2,1)S(1)}, bf16[640,128]{1,0:T(8,128)(2,1)S(1)}, u32[]{:S(2)}, u32[]{:S(2)}) collective-permute-start(bf16[640,128]{1,0:T(8,128)(2,1)S(1)} %shard_map.91), channel_id=1, source_target_pairs={{0,128},{1,129},{2,130},{3,131},{4,132},{5,133},{6,134},{7,135},{8... | collective-permute-start | bytes 491528 | tf_op jit(solution)/shard_map/ppermute | solution.py:469
  63.6 10.0 %collective-permute-start.15 = (bf16[640,128]{1,0:T(8,128)(2,1)S(1)}, bf16[640,128]{1,0:T(8,128)(2,1)S(1)}, u32[]{:S(2)}, u32[]{:S(2)}) collective-permute-start(bf16[640,128]{1,0:T(8,128)(2,1)S(1)} %shard_map.91), channel_id=1, source_target_pairs={{0,64},{1,193},{2,66},{3,195},{4,68},{5,197},{6,70},{7,199},{8,72}... | collective-permute-start | bytes 491528 | tf_op jit(solution)/shard_map/ppermute | solution.py:469
  73.7 5.5 %collective-permute-start.18 = (bf16[640,128]{1,0:T(8,128)(2,1)S(1)}, bf16[640,128]{1,0:T(8,128)(2,1)S(1)}, u32[]{:S(2)}, u32[]{:S(2)}) collective-permute-start(bf16[640,128]{1,0:T(8,128)(2,1)S(1)} %get-tuple-element.62), channel_id=1, source_target_pairs={{0,16},{1,49},{2,18},{3,51},{4,20},{5,53},{6,22},{7,55},{8,24},{9,... | collective-permute-start | bytes 491528 | tf_op jit(solution)/shard_map/ppermute | solution.py:469
  75.8 7.7 %collective-permute-start.19 = (bf16[640,128]{1,0:T(8,128)(2,1)S(1)}, bf16[640,128]{1,0:T(8,128)(2,1)S(1)}, u32[]{:S(2)}, u32[]{:S(2)}) collective-permute-start(bf16[640,128]{1,0:T(8,128)(2,1)S(1)} %get-tuple-element.63), channel_id=1, source_target_pairs={{0,32},{1,33},{2,34},{3,35},{4,36},{5,37},{6,38},{7,39},{8,40},{9,... | collective-permute-start | bytes 491528 | tf_op jit(solution)/shard_map/ppermute | solution.py:469
  76.6 7.9 %collective-permute-start.20 = (bf16[640,128]{1,0:T(8,128)(2,1)S(1)}, bf16[640,128]{1,0:T(8,128)(2,1)S(1)}, u32[]{:S(2)}, u32[]{:S(2)}) collective-permute-start(bf16[640,128]{1,0:T(8,128)(2,1)S(1)} %get-tuple-element.64), channel_id=1, source_target_pairs={{0,48},{1,17},{2,50},{3,19},{4,52},{5,21},{6,54},{7,23},{8,56},{9,... | collective-permute-start | bytes 491528 | tf_op jit(solution)/shard_map/ppermute | solution.py:469

commit v7 on v5

--- a/solution.py
+++ b/solution.py
@@ -141,8 +141,11 @@
     sp[512:640] = pack_tail(start[pl.ds(first, POS), 256:320].astype(F32)).astype(BF16)
 
 
-def conv_frame(normed, wp, wt, pre, taps, before_row=None):
+def frame_taps(normed, taps):
     store_taps(taps, [normed[0:320].astype(F32), normed[320:640].astype(F32), spread_tail(normed[640:800].astype(F32))])
+
+
+def conv_frame(wp, wt, pre, taps, before_row=None):
     main = None
     for row in range(3):
         if before_row is not None:
@@ -182,7 +185,8 @@
         else:
             wt[...] = jnp.concatenate([wp[i, :, 256:320].astype(F32) for i in range(3)], axis=1).astype(BF16)
 
-    conv_frame(normed, wp, wt, pre.at[0], taps, before_row)
+    frame_taps(normed, taps)
+    conv_frame(wp, wt, pre.at[0], taps, before_row)
     for copy in copies[18:]:
         copy.wait()
 
@@ -192,9 +196,11 @@
         tp[768:832] = jnp.zeros((64, 320), BF16)
 
 
-def first_sides_kernel(before, after, wp, wt, pre, taps):
-    for place, normed in enumerate((before, after)):
-        conv_frame(normed, wp, wt, pre.at[place], taps)
+def first_sides_kernel(there, mate, wp, wt, pre, taps):
+    frame_taps(there, taps.at[0])
+    frame_taps(mate, taps.at[1])
+    for place in range(2):
+        conv_frame(wp, wt, pre.at[place], taps.at[place])
 
 
 def silu_half(half):
@@ -348,7 +354,9 @@
         scales[step, 0:1] = mean[step : step + 1]
         scales[step, 1:2] = rstd[step : step + 1]
 
-    def one_step(step, carry):
+    low = low_lanes(32)
+
+    def build(step):
         here = scales[step]
 
         def normed(value, tile):
@@ -356,12 +364,10 @@
             value = (value.astype(F32) - here[0:1, lanes]) * here[1:2, lanes]
             return silu(value * gain[:, lanes] + bias[:, lanes])
 
-        edge = pl.multiple_of(step * 96, 32)
         tiles = []
-        low = low_lanes(32)
         for tile in range(3):
-            one = halo1[pl.ds(edge + 32 * tile, 32)].astype(F32)
-            three = halo3[pl.ds(edge + 32 * tile, 32)].astype(F32)
+            edge = slice(step * 96 + 32 * tile, step * 96 + 32 * tile + 32)
+            one, three = halo1[edge].astype(F32), halo3[edge].astype(F32)
             top = normed(jnp.where(ahead, three, one), tile)
             bottom = normed(jnp.where(ahead, one, three), tile)
             if tile < 2:
@@ -373,17 +379,23 @@
             top = jnp.where(x > 0, top, 0.0)
             bottom = jnp.where(x < 3, bottom, 0.0)
             tiles.append(jnp.concatenate([top, middle, bottom], axis=0))
-        store_taps(taps, tiles)
+        store_taps(taps.at[step % 2], tiles)
+
+    def finish(step):
+        here = taps.at[step % 2]
         bias_here = tb[step][0:1]
-        main = (conv_row(taps, wp, 0) + conv_row(taps, wp, 1)) + conv_row(taps, wp, 2)
+        main = (conv_row(here, wp, 0) + conv_row(here, wp, 1)) + conv_row(here, wp, 2)
         activated = silu(main + bias_here[:, 0:256])
-        tail = silu(conv_tail(taps, wt) + bias_here[:, 256:320])
+        tail = silu(conv_tail(here, wt) + bias_here[:, 256:320])
         out[step, 0:256] = activated[:, 0:128].astype(BF16)
         out[step, 256:512] = activated[:, 128:256].astype(BF16)
         out[step, 512:640] = pack_tail(tail).astype(BF16)
-        return carry
-
-    lax.fori_loop(0, 4, one_step, 0)
+
+    build(0)
+    for step in range(4):
+        if step < 3:
+            build(step + 1)
+        finish(step)
     ones = [out[step].astype(F32) for step in range(4)]
     total[...] = ((ones[0] + ones[1]) + (ones[2] + ones[3])).astype(BF16)
 
@@ -523,7 +535,7 @@
         sems=25,
     )
     sides = call(
-        first_sides_kernel, [((2,) + pre, F32)], there, mate, wp, wt, scratch=(taps,), flops=1024 * 320 * 2880
+        first_sides_kernel, [((2,) + pre, F32)], there, mate, wp, wt, scratch=(((2, 320, 1024), BF16),), flops=1024 * 320 * 2880
     )[0]
     rt, noises, tb = call(
         first_total_kernel,
@@ -546,7 +558,7 @@
         second_sweep_kernel,
         [(four, BF16), (packed, BF16)],
         states, halo1, halo3, far, halos[2], gain, bias, wp, wt, tb,
-        scratch=(taps, ((4, 8, 384), F32)),
+        scratch=(((2, 320, 1024), BF16), ((4, 8, 384), F32)),
         flops=2048 * 320 * 2880,
     )
     sums = total, *beside(total)

time: 84.7 us -> 83.7 us (0.988)
  Pallas kernels: 19.1 us -> 18 us
    pallas_call x12, Pallas kernels: 19.1 us -> 18 us  [call(): pl.pallas_call(body, out_shape=shapes, in_specs=[pl.BlockSpec(memory_spac...]
  transfers between devices with their start and end apart: 21 -> 21, of which waited for: 12 -> 12; matrix products, arithmetic and copies ran while one was open for 0% -> 0% of each run, Pallas kernels for 9% -> 10%
where the time goes in v7:
time: 83.7 us; the launch traced here: 83.6 us
  waiting for transfers between devices  32.5 us (39%)
  starting transfers between devices  32.1 us (38%)
  Pallas kernels  18 us (22%)
    ppermute x21, waiting for transfers between devices, moved(): return lax.ppermute(value, AXES, pairs)  32.5 us
    ppermute x21, starting transfers between devices, moved(): return lax.ppermute(value, AXES, pairs)  32.1 us
    pallas_call x12, Pallas kernels, call(): pl.pallas_call(body, out_shape=shapes, in_specs=[pl.BlockSpec(memory_spac...  18 us
  transfers between devices with their start and end apart: 21, of which 12 were waited for; matrix products, arithmetic and copies ran while one was open for 0% of the time, Pallas kernels for 10%

profile of v7, /device:TPU:1, one launch (start us, length us, event | category | flops | bytes accessed | tf_op | source)
XLA Modules:
  0.0 83.6 jit_solution(8722333194833563412)
XLA Ops:
  0.7 0.1 sine_convert_fusion
  0.7 0.1 fusion.2
  0.8 1.6 %shard_map.82 = (bf16[688,128]{1,0:T(8,128)(2,1)S(1)}, bf16[688,128]{1,0:T(8,128)(2,1)S(1)}, bf16[688,128]{1,0:T(8,128)(2,1)S(1)}, bf16[688,128]{1,0:T(8,128)(2,...) custom-call(bf16[1024,320]{1,0:T(8,128)(2,1)} %bitcast.4, bf16[1024,320]{1,0:T(8,128)(2,1)} %bitcast.5, ...), custom_call_target="tpu_custom_call" | custom-call | bytes 2688000 | tf_op jit(solution)/shard_map/pallas_call | solution.py:455
  2.4 0.9 %shard_map.83 = (bf16[800,128]{1,0:T(8,128)(2,1)S(1)}, bf16[640,128]{1,0:T(8,128)(2,1)S(1)}) custom-call(bf16[1024,320]{1,0:T(8,128)(2,1)S(1)} %get-tuple-element.32.start, f32[320]{0:T(512)S(1)} %get-tuple-element.33.gain_ref, f32[320]{0:T(512)S(1)} %get-tuple-element.34.bias_ref), custom_call_target="tpu_custom_call" | custom-call | bytes 1026560 | tf_op jit(solution)/shard_map/pallas_call | solution.py:455
  3.3 3.3 %collective-permute-start.1 = (bf16[800,128]{1,0:T(8,128)(2,1)S(1)}, bf16[800,128]{1,0:T(8,128)(2,1)S(1)}, u32[]{:S(2)}, u32[]{:S(2)}) collective-permute-start(bf16[800,128]{1,0:T(8,128)(2,1)S(1)} %get-tuple-element.36.normed), channel_id=1, source_target_pairs={{0,1},{1,0},{2,3},{3,2},{4,5},{5,4},{6,7},{7,6},{8,9},{9,8},{10,11... | collective-permute-start | bytes 614408 | tf_op jit(solution)/shard_map/ppermute | solution.py:474
  6.6 0.0 collective-permute-start
  6.6 2.4 %collective-permute-start.2 = (bf16[688,128]{1,0:T(8,128)(2,1)S(1)}, bf16[688,128]{1,0:T(8,128)(2,1)S(1)}, u32[]{:S(2)}, u32[]{:S(2)}) collective-permute-start(bf16[688,128]{1,0:T(8,128)(2,1)S(1)} %get-tuple-element.43), channel_id=1, source_target_pairs={{0,16},{1,49},{2,18},{3,51},{4,20},{5,53},{6,22},{7,55},{8,24},{9,... | collective-permute-start | bytes 528392 | tf_op jit(solution)/shard_map/ppermute | solution.py:474
  9.0 0.5 collective-permute-start.3
  9.5 0.3 collective-permute-start.4
  9.9 2.8 %shard_map.84 = (f32[1,256,320]{2,1,0:T(8,128)S(1)}, bf16[3,1024,320]{2,1,0:T(8,128)(2,1)S(1)}, bf16[1024,192]{1,0:T(8,128)(2,1)S(1)}, bf16[1024,320]{1,0:T(8,128)(2,1)S(1)}, bf16[320,320]{1,0:T(8,128)(2,1)S(1)}) custom-call(bf16[3,3,320,320]{3,2,1,0:T(8,128)(2,1)} %sw.1, bf16[3,320,320]{2,1,0:T(8,128)(2,1)} %tw.1, bf16[320,320]{1,0:T(8,128)(2,1)} %tew_hbm.1, ...), custom_call_target="tpu_custom_call" | custom-call | flops 471859200 | bytes 6414336 | tf_op jit(solution)/shard_map/pallas_call | solution.py:455
  12.6 0.0 collective-permute-done.1.mate
  12.6 0.0 collective-permute-done.there
  12.7 1.5 %shard_map.85.sides = f32[2,256,320]{2,1,0:T(8,128)S(1)} custom-call(bf16[800,128]{1,0:T(8,128)(2,1)S(1)} %collective-permute-done.there, bf16[800,128]{1,0:T(8,128)(2,1)S(1)} %collective-permute-done.1.mate, bf16[3,1024,320]{2,1,0:T(8,128)(2,1)S(1)} %get-tuple-element.38.wp, bf16[1024,192]{1,0:T(8,128)(2,1)S(1)} %get-tuple-element.39.wt), custom_call_target="tpu_custom_call" | custom-call | flops 943718400 | bytes 3424256 | tf_op jit(solution)/shard_map/pallas_call | solution.py:455
  14.2 0.0 collective-permute-done.2.n1
  14.2 0.6 collective-permute-done.3.n2
  14.8 1.0 %collective-permute-done.4.n3 = bf16[688,128]{1,0:T(8,128)(2,1)S(1)} collective-permute-done((bf16[688,128]{1,0:T(8,128)(2,1)S(1)}, bf16[688,128]{1,0:T(8,128)(2,1)S(1)}, u32[]{:S(2)}, u32[]{:S(2)}) %collective-permute-start.4) | collective-permute-done | bytes 176160 | tf_op jit(solution)/shard_map/ppermute | solution.py:474
  15.8 1.6 %shard_map.86 = (bf16[640,128]{1,0:T(8,128)(2,1)S(1)}, bf16[4,640,128]{2,1,0:T(8,128)(2,1)S(1)}, f32[4,16,320]{2,1,0:T(8,128)S(1)}) custom-call(f32[1,256,320]{2,1,0:T(8,128)S(1)} %get-tuple-element.37.here, f32[2,256,320]{2,1,0:T(8,128)S(1)} %shard_map.85.sides, bf16[1024,320]{1,0:T(8,128)(2,1)S(1)} %get-tuple-element.40.tp, ...), custom_call_target="tpu_custom_call" | custom-call | flops 157286400 | bytes 3448832 | tf_op jit(solution)/shard_map/pallas_call | solution.py:455
  17.4 1.2 %collective-permute-start.7 = (bf16[640,128]{1,0:T(8,128)(2,1)S(1)}, bf16[640,128]{1,0:T(8,128)(2,1)S(1)}, u32[]{:S(2)}, u32[]{:S(2)}) collective-permute-start(bf16[640,128]{1,0:T(8,128)(2,1)S(1)} %get-tuple-element.48), channel_id=1, source_target_pairs={{0,192},{1,65},{2,194},{3,67},{4,196},{5,69},{6,198},{7,71},{8,200... | collective-permute-start | bytes 491528 | tf_op jit(solution)/shard_map/ppermute | solution.py:474
  18.6 2.6 %collective-permute-start.6 = (bf16[640,128]{1,0:T(8,128)(2,1)S(1)}, bf16[640,128]{1,0:T(8,128)(2,1)S(1)}, u32[]{:S(2)}, u32[]{:S(2)}) collective-permute-start(bf16[640,128]{1,0:T(8,128)(2,1)S(1)} %get-tuple-element.48), channel_id=1, source_target_pairs={{0,128},{1,129},{2,130},{3,131},{4,132},{5,133},{6,134},{7,135},{8... | collective-permute-start | bytes 491528 | tf_op jit(solution)/shard_map/ppermute | solution.py:474
  21.2 0.1 collective-permute-start.5
  21.3 1.5 %shard_map.87.prefix = f32[4,640,128]{2,1,0:T(8,128)S(1)} custom-call(f32[1,256,320]{2,1,0:T(8,128)S(1)} %get-tuple-element.37.here, f32[2,256,320]{2,1,0:T(8,128)S(1)} %shard_map.85.sides, f32[4,16,320]{2,1,0:T(8,128)S(1)} %get-tuple-element.46.tb, bf16[1024,320]{1,0:T(8,128)(2,1)S(1)} %get-tuple-element.40.tp, bf16[4,640,128]{2,1,0:T(8,128)(2,1)S(1)} %get-tuple-element.47.noise), custom_call_target="tpu_custom_call" | custom-call | flops 471859200 | bytes 3686400 | tf_op jit(solution)/shard_map/pallas_call | solution.py:455
  22.9 0.0 collective-permute-done.7.r3
  22.9 2.9 %collective-permute-done.6.r2 = bf16[640,128]{1,0:T(8,128)(2,1)S(1)} collective-permute-done((bf16[640,128]{1,0:T(8,128)(2,1)S(1)}, bf16[640,128]{1,0:T(8,128)(2,1)S(1)}, u32[]{:S(2)}, u32[]{:S(2)}) %collective-permute-start.6) | collective-permute-done | bytes 163872 | tf_op jit(solution)/shard_map/ppermute | solution.py:474
  25.8 1.7 %collective-permute-done.5.r1 = bf16[640,128]{1,0:T(8,128)(2,1)S(1)} collective-permute-done((bf16[640,128]{1,0:T(8,128)(2,1)S(1)}, bf16[640,128]{1,0:T(8,128)(2,1)S(1)}, u32[]{:S(2)}, u32[]{:S(2)}) %collective-permute-start.5) | collective-permute-done | bytes 163872 | tf_op jit(solution)/shard_map/ppermute | solution.py:474
  27.4 1.1 %shard_map.88 = (bf16[4,640,128]{2,1,0:T(8,128)(2,1)S(1)}, bf16[464,128]{1,0:T(8,128)(2,1)S(1)}, bf16[464,128]{1,0:T(8,128)(2,1)S(1)}, bf16[72,128]{1,0:T(8,128)(2,1)S(1)}) custom-call(bf16[640,128]{1,0:T(8,128)(2,1)S(1)} %get-tuple-element.35.sp, f32[4,640,128]{2,1,0:T(8,128)S(1)} %shard_map.87.prefix, bf16[640,128]{1,0:T(8,128)(2,1)S(1)} %collective-permute-done.5.r1, ...), custom_call_target="tpu_custom_call" | custom-call | bytes 2877440 | tf_op jit(solution)/shard_map/pallas_call | solution.py:455
  28.5 3.4 %collective-permute-start.8 = (bf16[464,128]{1,0:T(8,128)(2,1)S(1)}, bf16[464,128]{1,0:T(8,128)(2,1)S(1)}, u32[]{:S(2)}, u32[]{:S(2)}) collective-permute-start(bf16[464,128]{1,0:T(8,128)(2,1)S(1)} %get-tuple-element.50), channel_id=1, source_target_pairs={{0,16},{1,49},{2,18},{3,51},{4,20},{5,53},{6,22},{7,55},{8,24},{9,... | collective-permute-start | bytes 356360 | tf_op jit(solution)/shard_map/ppermute | solution.py:474
  31.9 0.6 collective-permute-start.9
  32.6 0.7 collective-permute-start.10
  33.3 3.4 %collective-permute-done.10.far = bf16[72,128]{1,0:T(8,128)(2,1)S(1)} collective-permute-done((bf16[72,128]{1,0:T(8,128)(2,1)S(1)}, bf16[72,128]{1,0:T(8,128)(2,1)S(1)}, u32[]{:S(2)}, u32[]{:S(2)}) %collective-permute-start.10) | collective-permute-done | bytes 18464 | tf_op jit(solution)/shard_map/ppermute | solution.py:474
  36.7 0.0 collective-permute-done.8.halo1
  36.7 0.0 collective-permute-done.9.halo3
  36.7 3.7 %shard_map.89 = (bf16[4,640,128]{2,1,0:T(8,128)(2,1)S(1)}, bf16[640,128]{1,0:T(8,128)(2,1)S(1)}) custom-call(bf16[4,640,128]{2,1,0:T(8,128)(2,1)S(1)} %get-tuple-element.49.states, bf16[464,128]{1,0:T(8,128)(2,1)S(1)} %collective-permute-done.8.halo1, bf16[464,128]{1,0:T(8,128)(2,1)S(1)} %collective-permute-done.9.halo3, ...), custom_call_target="tpu_custom_call" | custom-call | flops 1887436800 | bytes 4192768 | tf_op jit(solution)/shard_map/pallas_call | solution.py:455
  40.4 5.4 %collective-permute-start.12 = (bf16[4,640,128]{2,1,0:T(8,128)(2,1)S(1)}, bf16[4,640,128]{2,1,0:T(8,128)(2,1)S(1)}, u32[]{:S(2)}, u32[]{:S(2)}) collective-permute-start(bf16[4,640,128]{2,1,0:T(8,128)(2,1)S(1)} %get-tuple-element.53.own), channel_id=1, source_target_pairs={{0,1},{1,0},{2,3},{3,2},{4,5},{5,4},{6,7},{7,6},{8,9},{9,8},{10,11... | collective-permute-start | bytes 1966088 | tf_op jit(solution)/shard_map/ppermute | solution.py:474
  45.8 0.1 collective-permute-start.11
  45.9 4.1 %collective-permute-start.14 = (bf16[640,128]{1,0:T(8,128)(2,1)S(1)}, bf16[640,128]{1,0:T(8,128)(2,1)S(1)}, u32[]{:S(2)}, u32[]{:S(2)}) collective-permute-start(bf16[640,128]{1,0:T(8,128)(2,1)S(1)} %get-tuple-element.54.own), channel_id=1, source_target_pairs={{0,1},{1,0},{2,3},{3,2},{4,5},{5,4},{6,7},{7,6},{8,9},{9,8},{10,11... | collective-permute-start | bytes 491528 | tf_op jit(solution)/shard_map/ppermute | solution.py:474
  49.9 0.0 collective-permute-start.13
  49.9 1.0 %collective-permute-done.14.after = bf16[640,128]{1,0:T(8,128)(2,1)S(1)} collective-permute-done((bf16[640,128]{1,0:T(8,128)(2,1)S(1)}, bf16[640,128]{1,0:T(8,128)(2,1)S(1)}, u32[]{:S(2)}, u32[]{:S(2)}) %collective-permute-start.14) | collective-permute-done | bytes 163872 | tf_op jit(solution)/shard_map/ppermute | solution.py:474
  51.0 6.9 %collective-permute-done.13.before = bf16[640,128]{1,0:T(8,128)(2,1)S(1)} collective-permute-done((bf16[640,128]{1,0:T(8,128)(2,1)S(1)}, bf16[640,128]{1,0:T(8,128)(2,1)S(1)}, u32[]{:S(2)}, u32[]{:S(2)}) %collective-permute-start.13) | collective-permute-done | bytes 163872 | tf_op jit(solution)/shard_map/ppermute | solution.py:474
  57.8 0.5 shard_map.91
  58.4 0.7 collective-permute-start.17
  59.1 2.6 %collective-permute-start.16 = (bf16[640,128]{1,0:T(8,128)(2,1)S(1)}, bf16[640,128]{1,0:T(8,128)(2,1)S(1)}, u32[]{:S(2)}, u32[]{:S(2)}) collective-permute-start(bf16[640,128]{1,0:T(8,128)(2,1)S(1)} %shard_map.91), channel_id=1, source_target_pairs={{0,128},{1,129},{2,130},{3,131},{4,132},{5,133},{6,134},{7,135},{8... | collective-permute-start | bytes 491528 | tf_op jit(solution)/shard_map/ppermute | solution.py:474
  61.7 0.6 collective-permute-start.15
  62.3 0.0 collective-permute-done.12.after
  62.3 0.0 collective-permute-done.11.before
  62.3 1.6 %shard_map.90.prefix = f32[4,640,128]{2,1,0:T(8,128)S(1)} custom-call(bf16[4,640,128]{2,1,0:T(8,128)(2,1)S(1)} %get-tuple-element.53.own, bf16[4,640,128]{2,1,0:T(8,128)(2,1)S(1)} %collective-permute-done.11.before, bf16[4,640,128]{2,1,0:T(8,128)(2,1)S(1)} %collective-permute-done.12.after, bf16[1024,320]{1,0:T(8,128)(2,1)S(1)} %get-tuple-element.40.tp, ...), custom_call_target="tpu_custom_call" | custom-call | flops 629145600 | bytes 4587520 | tf_op jit(solution)/shard_map/pallas_call | solution.py:455
  63.9 0.0 collective-permute-done.17.r3
  63.9 2.3 %collective-permute-done.16.r2 = bf16[640,128]{1,0:T(8,128)(2,1)S(1)} collective-permute-done((bf16[640,128]{1,0:T(8,128)(2,1)S(1)}, bf16[640,128]{1,0:T(8,128)(2,1)S(1)}, u32[]{:S(2)}, u32[]{:S(2)}) %collective-permute-start.16) | collective-permute-done | bytes 163872 | tf_op jit(solution)/shard_map/ppermute | solution.py:474
  66.2 5.4 %collective-permute-done.15.r1 = bf16[640,128]{1,0:T(8,128)(2,1)S(1)} collective-permute-done((bf16[640,128]{1,0:T(8,128)(2,1)S(1)}, bf16[640,128]{1,0:T(8,128)(2,1)S(1)}, u32[]{:S(2)}, u32[]{:S(2)}) %collective-permute-start.15) | collective-permute-done | bytes 163872 | tf_op jit(solution)/shard_map/ppermute | solution.py:474
  71.6 0.2 shard_map.92
  71.8 2.1 %collective-permute-start.18 = (bf16[640,128]{1,0:T(8,128)(2,1)S(1)}, bf16[640,128]{1,0:T(8,128)(2,1)S(1)}, u32[]{:S(2)}, u32[]{:S(2)}) collective-permute-start(bf16[640,128]{1,0:T(8,128)(2,1)S(1)} %get-tuple-element.56), channel_id=1, source_target_pairs={{0,16},{1,49},{2,18},{3,51},{4,20},{5,53},{6,22},{7,55},{8,24},{9,... | collective-permute-start | bytes 491528 | tf_op jit(solution)/shard_map/ppermute | solution.py:474
  73.9 0.7 collective-permute-start.19
  74.7 0.5 collective-permute-start.20
  75.2 2.1 %collective-permute-done.18.r1 = bf16[640,128]{1,0:T(8,128)(2,1)S(1)} collective-permute-done((bf16[640,128]{1,0:T(8,128)(2,1)S(1)}, bf16[640,128]{1,0:T(8,128)(2,1)S(1)}, u32[]{:S(2)}, u32[]{:S(2)}) %collective-permute-start.18) | collective-permute-done | bytes 163872 | tf_op jit(solution)/shard_map/ppermute | solution.py:474
  77.3 4.3 %collective-permute-done.19.r2 = bf16[640,128]{1,0:T(8,128)(2,1)S(1)} collective-permute-done((bf16[640,128]{1,0:T(8,128)(2,1)S(1)}, bf16[640,128]{1,0:T(8,128)(2,1)S(1)}, u32[]{:S(2)}, u32[]{:S(2)}) %collective-permute-start.19) | collective-permute-done | bytes 163872 | tf_op jit(solution)/shard_map/ppermute | solution.py:474
  81.6 0.9 %collective-permute-done.20.r3 = bf16[640,128]{1,0:T(8,128)(2,1)S(1)} collective-permute-done((bf16[640,128]{1,0:T(8,128)(2,1)S(1)}, bf16[640,128]{1,0:T(8,128)(2,1)S(1)}, u32[]{:S(2)}, u32[]{:S(2)}) %collective-permute-start.20) | collective-permute-done | bytes 163872 | tf_op jit(solution)/shard_map/ppermute | solution.py:474
  82.5 1.1 %shard_map.93 = bf16[1024,320]{1,0:T(8,128)(2,1)} custom-call(bf16[640,128]{1,0:T(8,128)(2,1)S(1)} %get-tuple-element.55.r0, bf16[640,128]{1,0:T(8,128)(2,1)S(1)} %collective-permute-done.18.r1, bf16[640,128]{1,0:T(8,128)(2,1)S(1)} %collective-permute-done.19.r2, bf16[640,128]{1,0:T(8,128)(2,1)S(1)} %collective-permute-done.20.r3), custom_call_target="tpu_custom_call" | custom-call | bytes 1310720 | tf_op jit(solution)/shard_map/pallas_call | solution.py:455
  (1 shorter events, 0.0 us)
Async XLA Ops:
  3.3 9.3 %collective-permute-start.1 = (bf16[800,128]{1,0:T(8,128)(2,1)S(1)}, bf16[800,128]{1,0:T(8,128)(2,1)S(1)}, u32[]{:S(2)}, u32[]{:S(2)}) collective-permute-start(bf16[800,128]{1,0:T(8,128)(2,1)S(1)} %get-tuple-element.36.normed), channel_id=1, source_target_pairs={{0,1},{1,0},{2,3},{3,2},{4,5},{5,4},{6,7},{7,6},{8,9},{9,8},{10,11... | collective-permute-start | bytes 614408 | tf_op jit(solution)/shard_map/ppermute | solution.py:474
  6.6 6.0 %collective-permute-start = (bf16[800,128]{1,0:T(8,128)(2,1)S(1)}, bf16[800,128]{1,0:T(8,128)(2,1)S(1)}, u32[]{:S(2)}, u32[]{:S(2)}) collective-permute-start(bf16[800,128]{1,0:T(8,128)(2,1)S(1)} %get-tuple-element.36.normed), channel_id=1, source_target_pairs={{0,15},{1,2},{2,1},{3,4},{4,3},{5,6},{6,5},{7,8},{8,7},{9,10},{10,... | collective-permute-start | bytes 614408 | tf_op jit(solution)/shard_map/ppermute | solution.py:474
  6.6 7.6 %collective-permute-start.2 = (bf16[688,128]{1,0:T(8,128)(2,1)S(1)}, bf16[688,128]{1,0:T(8,128)(2,1)S(1)}, u32[]{:S(2)}, u32[]{:S(2)}) collective-permute-start(bf16[688,128]{1,0:T(8,128)(2,1)S(1)} %get-tuple-element.43), channel_id=1, source_target_pairs={{0,16},{1,49},{2,18},{3,51},{4,20},{5,53},{6,22},{7,55},{8,24},{9,... | collective-permute-start | bytes 528392 | tf_op jit(solution)/shard_map/ppermute | solution.py:474
  9.0 5.8 %collective-permute-start.3 = (bf16[688,128]{1,0:T(8,128)(2,1)S(1)}, bf16[688,128]{1,0:T(8,128)(2,1)S(1)}, u32[]{:S(2)}, u32[]{:S(2)}) collective-permute-start(bf16[688,128]{1,0:T(8,128)(2,1)S(1)} %get-tuple-element.44), channel_id=1, source_target_pairs={{0,32},{1,33},{2,34},{3,35},{4,36},{5,37},{6,38},{7,39},{8,40},{9,... | collective-permute-start | bytes 528392 | tf_op jit(solution)/shard_map/ppermute | solution.py:474
  9.5 6.3 %collective-permute-start.4 = (bf16[688,128]{1,0:T(8,128)(2,1)S(1)}, bf16[688,128]{1,0:T(8,128)(2,1)S(1)}, u32[]{:S(2)}, u32[]{:S(2)}) collective-permute-start(bf16[688,128]{1,0:T(8,128)(2,1)S(1)} %get-tuple-element.45), channel_id=1, source_target_pairs={{0,48},{1,17},{2,50},{3,19},{4,52},{5,21},{6,54},{7,23},{8,56},{9,... | collective-permute-start | bytes 528392 | tf_op jit(solution)/shard_map/ppermute | solution.py:474
  17.4 5.5 %collective-permute-start.7 = (bf16[640,128]{1,0:T(8,128)(2,1)S(1)}, bf16[640,128]{1,0:T(8,128)(2,1)S(1)}, u32[]{:S(2)}, u32[]{:S(2)}) collective-permute-start(bf16[640,128]{1,0:T(8,128)(2,1)S(1)} %get-tuple-element.48), channel_id=1, source_target_pairs={{0,192},{1,65},{2,194},{3,67},{4,196},{5,69},{6,198},{7,71},{8,200... | collective-permute-start | bytes 491528 | tf_op jit(solution)/shard_map/ppermute | solution.py:474
  18.6 7.2 %collective-permute-start.6 = (bf16[640,128]{1,0:T(8,128)(2,1)S(1)}, bf16[640,128]{1,0:T(8,128)(2,1)S(1)}, u32[]{:S(2)}, u32[]{:S(2)}) collective-permute-start(bf16[640,128]{1,0:T(8,128)(2,1)S(1)} %get-tuple-element.48), channel_id=1, source_target_pairs={{0,128},{1,129},{2,130},{3,131},{4,132},{5,133},{6,134},{7,135},{8... | collective-permute-start | bytes 491528 | tf_op jit(solution)/shard_map/ppermute | solution.py:474
  21.2 6.2 %collective-permute-start.5 = (bf16[640,128]{1,0:T(8,128)(2,1)S(1)}, bf16[640,128]{1,0:T(8,128)(2,1)S(1)}, u32[]{:S(2)}, u32[]{:S(2)}) collective-permute-start(bf16[640,128]{1,0:T(8,128)(2,1)S(1)} %get-tuple-element.48), channel_id=1, source_target_pairs={{0,64},{1,193},{2,66},{3,195},{4,68},{5,197},{6,70},{7,199},{8,72}... | collective-permute-start | bytes 491528 | tf_op jit(solution)/shard_map/ppermute | solution.py:474
  28.5 8.2 %collective-permute-start.8 = (bf16[464,128]{1,0:T(8,128)(2,1)S(1)}, bf16[464,128]{1,0:T(8,128)(2,1)S(1)}, u32[]{:S(2)}, u32[]{:S(2)}) collective-permute-start(bf16[464,128]{1,0:T(8,128)(2,1)S(1)} %get-tuple-element.50), channel_id=1, source_target_pairs={{0,16},{1,49},{2,18},{3,51},{4,20},{5,53},{6,22},{7,55},{8,24},{9,... | collective-permute-start | bytes 356360 | tf_op jit(solution)/shard_map/ppermute | solution.py:474
  31.9 4.8 %collective-permute-start.9 = (bf16[464,128]{1,0:T(8,128)(2,1)S(1)}, bf16[464,128]{1,0:T(8,128)(2,1)S(1)}, u32[]{:S(2)}, u32[]{:S(2)}) collective-permute-start(bf16[464,128]{1,0:T(8,128)(2,1)S(1)} %get-tuple-element.51), channel_id=1, source_target_pairs={{0,48},{1,17},{2,50},{3,19},{4,52},{5,21},{6,54},{7,23},{8,56},{9,... | collective-permute-start | bytes 356360 | tf_op jit(solution)/shard_map/ppermute | solution.py:474
  32.6 4.1 %collective-permute-start.10 = (bf16[72,128]{1,0:T(8,128)(2,1)S(1)}, bf16[72,128]{1,0:T(8,128)(2,1)S(1)}, u32[]{:S(2)}, u32[]{:S(2)}) collective-permute-start(bf16[72,128]{1,0:T(8,128)(2,1)S(1)} %get-tuple-element.52.mine), channel_id=1, source_target_pairs={{0,32},{1,33},{2,34},{3,35},{4,36},{5,37},{6,38},{7,39},{8,40},{9,... | collective-permute-start | bytes 55304 | tf_op jit(solution)/shard_map/ppermute | solution.py:474
  40.4 22.0 %collective-permute-start.12 = (bf16[4,640,128]{2,1,0:T(8,128)(2,1)S(1)}, bf16[4,640,128]{2,1,0:T(8,128)(2,1)S(1)}, u32[]{:S(2)}, u32[]{:S(2)}) collective-permute-start(bf16[4,640,128]{2,1,0:T(8,128)(2,1)S(1)} %get-tuple-element.53.own), channel_id=1, source_target_pairs={{0,1},{1,0},{2,3},{3,2},{4,5},{5,4},{6,7},{7,6},{8,9},{9,8},{10,11... | collective-permute-start | bytes 1966088 | tf_op jit(solution)/shard_map/ppermute | solution.py:474
  45.8 16.5 %collective-permute-start.11 = (bf16[4,640,128]{2,1,0:T(8,128)(2,1)S(1)}, bf16[4,640,128]{2,1,0:T(8,128)(2,1)S(1)}, u32[]{:S(2)}, u32[]{:S(2)}) collective-permute-start(bf16[4,640,128]{2,1,0:T(8,128)(2,1)S(1)} %get-tuple-element.53.own), channel_id=1, source_target_pairs={{0,15},{1,2},{2,1},{3,4},{4,3},{5,6},{6,5},{7,8},{8,7},{9,10},{10,... | collective-permute-start | bytes 1966088 | tf_op jit(solution)/shard_map/ppermute | solution.py:474
  45.9 5.1 %collective-permute-start.14 = (bf16[640,128]{1,0:T(8,128)(2,1)S(1)}, bf16[640,128]{1,0:T(8,128)(2,1)S(1)}, u32[]{:S(2)}, u32[]{:S(2)}) collective-permute-start(bf16[640,128]{1,0:T(8,128)(2,1)S(1)} %get-tuple-element.54.own), channel_id=1, source_target_pairs={{0,1},{1,0},{2,3},{3,2},{4,5},{5,4},{6,7},{7,6},{8,9},{9,8},{10,11... | collective-permute-start | bytes 491528 | tf_op jit(solution)/shard_map/ppermute | solution.py:474
  49.9 7.9 %collective-permute-start.13 = (bf16[640,128]{1,0:T(8,128)(2,1)S(1)}, bf16[640,128]{1,0:T(8,128)(2,1)S(1)}, u32[]{:S(2)}, u32[]{:S(2)}) collective-permute-start(bf16[640,128]{1,0:T(8,128)(2,1)S(1)} %get-tuple-element.54.own), channel_id=1, source_target_pairs={{0,15},{1,2},{2,1},{3,4},{4,3},{5,6},{6,5},{7,8},{8,7},{9,10},{10,... | collective-permute-start | bytes 491528 | tf_op jit(solution)/shard_map/ppermute | solution.py:474
  58.4 5.5 %collective-permute-start.17 = (bf16[640,128]{1,0:T(8,128)(2,1)S(1)}, bf16[640,128]{1,0:T(8,128)(2,1)S(1)}, u32[]{:S(2)}, u32[]{:S(2)}) collective-permute-start(bf16[640,128]{1,0:T(8,128)(2,1)S(1)} %shard_map.91), channel_id=1, source_target_pairs={{0,192},{1,65},{2,194},{3,67},{4,196},{5,69},{6,198},{7,71},{8,200... | collective-permute-start | bytes 491528 | tf_op jit(solution)/shard_map/ppermute | solution.py:474
  59.1 7.2 %collective-permute-start.16 = (bf16[640,128]{1,0:T(8,128)(2,1)S(1)}, bf16[640,128]{1,0:T(8,128)(2,1)S(1)}, u32[]{:S(2)}, u32[]{:S(2)}) collective-permute-start(bf16[640,128]{1,0:T(8,128)(2,1)S(1)} %shard_map.91), channel_id=1, source_target_pairs={{0,128},{1,129},{2,130},{3,131},{4,132},{5,133},{6,134},{7,135},{8... | collective-permute-start | bytes 491528 | tf_op jit(solution)/shard_map/ppermute | solution.py:474
  61.7 10.0 %collective-permute-start.15 = (bf16[640,128]{1,0:T(8,128)(2,1)S(1)}, bf16[640,128]{1,0:T(8,128)(2,1)S(1)}, u32[]{:S(2)}, u32[]{:S(2)}) collective-permute-start(bf16[640,128]{1,0:T(8,128)(2,1)S(1)} %shard_map.91), channel_id=1, source_target_pairs={{0,64},{1,193},{2,66},{3,195},{4,68},{5,197},{6,70},{7,199},{8,72}... | collective-permute-start | bytes 491528 | tf_op jit(solution)/shard_map/ppermute | solution.py:474
  71.8 5.5 %collective-permute-start.18 = (bf16[640,128]{1,0:T(8,128)(2,1)S(1)}, bf16[640,128]{1,0:T(8,128)(2,1)S(1)}, u32[]{:S(2)}, u32[]{:S(2)}) collective-permute-start(bf16[640,128]{1,0:T(8,128)(2,1)S(1)} %get-tuple-element.56), channel_id=1, source_target_pairs={{0,16},{1,49},{2,18},{3,51},{4,20},{5,53},{6,22},{7,55},{8,24},{9,... | collective-permute-start | bytes 491528 | tf_op jit(solution)/shard_map/ppermute | solution.py:474
  73.9 7.7 %collective-permute-start.19 = (bf16[640,128]{1,0:T(8,128)(2,1)S(1)}, bf16[640,128]{1,0:T(8,128)(2,1)S(1)}, u32[]{:S(2)}, u32[]{:S(2)}) collective-permute-start(bf16[640,128]{1,0:T(8,128)(2,1)S(1)} %get-tuple-element.57), channel_id=1, source_target_pairs={{0,32},{1,33},{2,34},{3,35},{4,36},{5,37},{6,38},{7,39},{8,40},{9,... | collective-permute-start | bytes 491528 | tf_op jit(solution)/shard_map/ppermute | solution.py:474
  74.7 7.9 %collective-permute-start.20 = (bf16[640,128]{1,0:T(8,128)(2,1)S(1)}, bf16[640,128]{1,0:T(8,128)(2,1)S(1)}, u32[]{:S(2)}, u32[]{:S(2)}) collective-permute-start(bf16[640,128]{1,0:T(8,128)(2,1)S(1)} %get-tuple-element.58), channel_id=1, source_target_pairs={{0,48},{1,17},{2,50},{3,19},{4,52},{5,21},{6,54},{7,23},{8,56},{9,... | collective-permute-start | bytes 491528 | tf_op jit(solution)/shard_map/ppermute | solution.py:474
